TPU v7x, 128 devices: a whole 4x4x4 slice. The times are simulated.
128 devices in a mesh: ep: 32 (over z, y, core), dp: 4 (over x).
Axes of the slice: x: 4, y: 4, z: 4, core: 2. Of those that a mesh axis runs over, the one named last changes fastest.
Arguments:
- tokens: bfloat16 [2048, 7168], P(('ep', 'dp')), may hold values from -6 to 6
- routes: int32 [2048, 8], P(('ep', 'dp')), may hold values from 0 to 31, all different within a row; in each aligned block of 16 rows (0 to 15, 16 to 31, ...) at most 8 rows name the same one
- route_logits: float32 [2048, 8], P(('ep', 'dp')), may hold values from -6 to 6
- gate_weight: bfloat16 [32, 7168, 2048], P('ep', None, 'dp'), may hold values from -0.0625 to 0.0625
- up_weight: bfloat16 [32, 7168, 2048], P('ep', None, 'dp'), may hold values from -0.0625 to 0.0625
- down_weight: bfloat16 [32, 2048, 7168], P('ep', 'dp'), may hold values from -0.125 to 0.125
Outputs:
- moe_output: bfloat16 [2048, 7168], P(('ep', 'dp'))
- expert_load: float32 [32], P('ep')
Inputs may be any that keep to these rules, and one draw needn't show every extreme that they name: `routes`: each row names 8 different experts. Within the rows of one device (aligned blocks of 16 rows) no expert is named more than 8 times, and in every draw some expert is named exactly 8 times there; every expert is named somewhere.
All inputs are finite; a program needn't handle non-finite values.
Results may differ from a plain program's by a relative error of at most 0.012.
Values may be sent and summed in bfloat16 or wider, within the bound.
No kernel may reach another device: no remote copies, remote signals or barrier semaphores. Data moves between devices by JAX's collectives and lax.ppermute only.
A program may use at most 128 MiB of HBM per device.

v0:
```python
import jax
import jax.numpy as jnp
from jax import lax
from jax.experimental import pallas as pl
from jax.experimental.pallas import tpu as pltpu
from jax.sharding import Mesh
from jax.sharding import PartitionSpec as P

EP = ("z", "y", "c")
EP_DP = ("z", "y", "c", "x")
ROUTE_SCALE = 2.5
EXTRA = 128
SIDE = 4
GATHER = (("x", "y", "z"), ("y", "z", "x"), ("z", "x", "y"))
REDUCE = (("z", "y", "x"), ("x", "z", "y"), ("y", "x", "z"))


def pairwise(v, axis, turn):
    pairs = []
    for core in range(2):
        flip = 1 if core == turn else 3
        for i in range(SIDE):
            j = i ^ flip
            if axis == "x":
                pairs.append((core * SIDE + i, core * SIDE + j))
            else:
                pairs.append((i * 2 + core, j * 2 + core))
    return lax.ppermute(v, ("c", "x") if axis == "x" else (axis, "c"), pairs)


def swap(v):
    return lax.ppermute(v, "c", [(0, 1), (1, 0)])


def after(values, *others):
    return list(lax.optimization_barrier(tuple(values) + others)[: len(values)])


def route_columns(routes, route_logits, experts):
    affinity = jax.nn.sigmoid(route_logits)
    weights = ROUTE_SCALE * affinity / jnp.sum(affinity, axis=1, keepdims=True)
    hit = routes[:, :, None] == jnp.arange(experts, dtype=jnp.int32)[None, None, :]
    mask = jnp.sum(hit.astype(jnp.float32), axis=1)
    dense = jnp.sum(jnp.where(hit, weights[:, :, None], 0.0), axis=1)
    high = lax.reduce_precision(dense, 8, 7)
    rest = dense - high
    mid = lax.reduce_precision(rest, 8, 7)
    low = rest - mid
    return jnp.concatenate([mask, high, mid, low], axis=1).astype(jnp.bfloat16)


def combine_kernel(*refs):
    kinds = [refs[k * 12 : k * 12 + 12] for k in range(4)]
    route = refs[48:52]
    own_ref, peer_ref, count_ref = refs[52:55]
    buf, route_buf, sems = refs[55:]

    def copies(i, slot):
        out = []
        for k, parts in enumerate(kinds):
            first, second, third = parts[0:4], parts[4:8], parts[8:12]
            sem = sems.at[slot, k]
            out.append(pltpu.make_async_copy(first[i], buf.at[slot, k, 0], sem.at[0]))
            for r in range(SIDE):
                out.append(
                    pltpu.make_async_copy(second[r].at[i], buf.at[slot, k, 1, :, r], sem.at[1 + r])
                )
                out.append(
                    pltpu.make_async_copy(third[r].at[:, i], buf.at[slot, k, 2, r], sem.at[5 + r])
                )
        for r in range(SIDE):
            out.append(
                pltpu.make_async_copy(
                    route[r].at[:, i], route_buf.at[slot, r], sems.at[slot, 4, r]
                )
            )
        return out

    for copy in copies(0, 0):
        copy.start()
    width = buf.shape[-1]
    count_ref[...] = jnp.zeros_like(count_ref)
    for i in range(SIDE):
        slot = i % 2
        if i + 1 < SIDE:
            for copy in copies(i + 1, 1 - slot):
                copy.start()
        for copy in copies(i, slot):
            copy.wait()

        def block(n, carry, i=i, slot=slot):
            y, x = n // SIDE, n % SIDE
            sums = [buf[slot, k, 0, y, x] + buf[slot, k, 1, y, x] + buf[slot, k, 2, y, x] for k in range(4)]
            extra = route_buf[slot, y, x]
            for e, out in enumerate((own_ref, peer_ref)):
                gate, up = sums[2 * e], sums[2 * e + 1]
                weight = jnp.concatenate([extra[:, e * 128 : e * 128 + 128]] * (width // 128), axis=1)
                act = gate / (1.0 + jnp.exp(-gate)) * up * weight
                out[i, y, x] = act.astype(jnp.bfloat16)
            count_ref[...] += jnp.sum(extra[:, 256:], axis=0, keepdims=True)
            return carry

        lax.fori_loop(0, SIDE * SIDE, block, 0)


def combine(kinds, route, tok, width):
    rows = jax.ShapeDtypeStruct((SIDE, SIDE, SIDE, tok, width), jnp.bfloat16)
    return pl.pallas_call(
        combine_kernel,
        out_shape=(rows, rows, jax.ShapeDtypeStruct((1, 256), jnp.float32)),
        in_specs=[pl.BlockSpec(memory_space=pl.ANY)] * 52,
        out_specs=(pl.BlockSpec(memory_space=pltpu.VMEM),) * 3,
        scratch_shapes=[
            pltpu.VMEM((2, 4, 3, SIDE, SIDE, tok, width), jnp.float32),
            pltpu.VMEM((2, SIDE, SIDE, tok, 512), jnp.float32),
            pltpu.SemaphoreType.DMA((2, 5, 9)),
        ],
        compiler_params=pltpu.CompilerParams(vmem_limit_bytes=32 * 1024 * 1024),
        name="combine",
    )(*kinds[0], *kinds[1], *kinds[2], *kinds[3], *route)


def cut(total, parts):
    tiles = total // 128
    sizes = [(tiles // parts + (1 if i < tiles % parts else 0)) * 128 for i in range(parts)]
    starts = [sum(sizes[:i]) for i in range(parts)]
    return list(zip(starts, sizes))


def product(rows, weight):
    flat = rows.reshape(-1, rows.shape[-1])
    out = jnp.dot(flat, weight, preferred_element_type=jnp.float32)
    return out.reshape(*rows.shape[:-1], weight.shape[1])


def on_device(tokens, routes, route_logits, gate_weight, up_weight, down_weight):
    tok, model = tokens.shape
    top_k = routes.shape[1]
    experts = lax.axis_size(EP)
    width = gate_weight.shape[2]
    expert = lax.axis_index(EP)
    gate_w, up_w, down_w = gate_weight[0], up_weight[0], down_weight[0]

    gate_p = swap(gate_w)
    up_p = swap(after([up_w], gate_p)[0])
    down_p = swap(after([down_w], up_p)[0])

    whole = jnp.concatenate([tokens, route_columns(routes, route_logits, experts)], axis=1)
    thirds = cut(model + EXTRA, 3)
    current = [whole[:, s : s + n] for s, n in thirds]
    for stage in range(2):
        got = [pairwise(c, GATHER[t][stage], 0) for t, c in enumerate(current)]
        current = after([jnp.stack([c, g]) for c, g in zip(current, got)])
        got = [pairwise(c, GATHER[t][stage], 1) for t, c in enumerate(current)]
        current = after([jnp.concatenate([c, g]) for c, g in zip(current, got)])

    lanes = jnp.arange(EXTRA, dtype=jnp.int32)
    own, peer = lanes % experts == expert, lanes % experts == expert + 1 - 2 * lax.axis_index("c")
    columns = [own & (lanes >= experts), peer & (lanes >= experts)]
    columns += [own & (lanes < experts), peer & (lanes < experts)]
    pick = jnp.concatenate(
        [jnp.broadcast_to(c[:, None], (EXTRA, 128)) for c in columns], axis=1
    ).astype(jnp.bfloat16)

    def products(blocks):
        out, extra = [], None
        for (s, n), b in zip(thirds, blocks):
            real = min(n, model - s)
            out += [product(b[..., :real], w[s : s + real]) for w in (gate_w, up_w, gate_p, up_p)]
            if real < n:
                extra = product(b[..., real:], pick)
        return out + [extra]

    first = current
    results = []
    blocks = [first]
    got = [pairwise(c, GATHER[t][2], 0) for t, c in enumerate(first)]
    done = products(first)
    moved = after(got + first + done)
    got, first, done = moved[:3], moved[3:6], moved[6:]
    results.append(done)
    second = got
    got = [pairwise(c, GATHER[t][2], 1) for t, c in enumerate(first)]
    done = products(second)
    moved = after(got + second + done)
    got, second, done = moved[:3], moved[3:6], moved[6:]
    results.append(done)
    fetched = [pairwise(c, GATHER[t][2], 1) for t, c in enumerate(second)]
    done = products(got)
    moved = after(fetched + done)
    fetched, done = moved[:3], moved[3:]
    results.append(done)
    results.append(products(fetched))

    kinds = [[results[r][t * 4 + k] for t in range(3) for r in range(SIDE)] for k in range(4)]
    own_rows, peer_rows, count = combine(kinds, [results[r][12] for r in range(SIDE)], tok, width)

    sums = []
    for (s, n), order in zip(cut(model, 3), REDUCE):
        names = ["z", "y", "x"]
        total = None
        for axis in order:
            d = names.index(axis)
            names.remove(axis)
            if total is None:

                def piece(lo, d=d, s=s, n=n):
                    return product(
                        lax.slice_in_dim(own_rows, lo, lo + 2, axis=d), down_w[:, s : s + n]
                    ) + product(
                        lax.slice_in_dim(peer_rows, lo, lo + 2, axis=d), down_p[:, s : s + n]
                    )
            else:

                def piece(lo, d=d, total=total):
                    return lax.slice_in_dim(total, lo, lo + 2, axis=d)

            got = pairwise(piece(2).astype(jnp.bfloat16), axis, 1)
            total = piece(0) + got.astype(jnp.float32)
            got = pairwise(lax.index_in_dim(total, 1, d, False).astype(jnp.bfloat16), axis, 0)
            total = lax.index_in_dim(total, 0, d, False) + got.astype(jnp.float32)
        sums.append(total.astype(jnp.bfloat16))
    moe_output = jnp.concatenate(sums, axis=-1)
    counted = count[:, :128] + swap(count[:, 128:])
    mean_count = float(tok * lax.axis_size("x") * top_k)
    expert_load = counted[0, :1] / mean_count
    return moe_output, expert_load


def solution(mesh):
    finer = Mesh(mesh.devices.reshape(SIDE, SIDE, 2, SIDE), EP_DP)
    in_specs = (
        P(EP_DP, None),
        P(EP_DP, None),
        P(EP_DP, None),
        P(EP, None, "x"),
        P(EP, None, "x"),
        P(EP, "x", None),
    )
    out_specs = (P(EP_DP, None), P(EP))
    return jax.shard_map(
        on_device, mesh=finer, in_specs=in_specs, out_specs=out_specs, check_vma=False
    )
```

profile of v0, /device:TPU:0, one launch (start us, length us, event | category | flops | bytes accessed | tf_op | source)
XLA Modules:
  0.0 301.6 jit_solution(14865787283975565701)
XLA Ops:
  13.3 2.6 collective-permute-start.5
  15.9 2.2 collective-permute-start.4
  18.1 2.8 collective-permute-start.3
  22.3 2.1 collective-permute-done.3
  26.6 4.9 %collective-permute-done.8 = bf16[4,16,2432]{2,1,0:T(8,128)(2,1)S(1)} collective-permute-done((bf16[4,16,2432]{2,1,0:T(8,128)(2,1)S(1)}, bf16[4,16,2432]{2,1,0:T(8,128)(2,1)S(1)}, u32[]{:S(2)}, u32[]{:S(2)}) %collective-permute-start.8) | collective-permute-done | bytes 311328 | tf_op jit(solution)/shard_map/ppermute | solution.py:28
  32.9 2.6 collective-permute-start.11
  37.4 7.0 %collective-permute-done.11 = bf16[2,4,16,2432]{3,2,1,0:T(8,128)(2,1)S(1)} collective-permute-done((bf16[2,4,16,2432]{3,2,1,0:T(8,128)(2,1)S(1)}, bf16[2,4,16,2432]{3,2,1,0:T(8,128)(2,1)S(1)}, u32[]{:S(2)}, u32[]{:S(2)}) %collective-permute-start.11) | collective-permute-done | bytes 622624 | tf_op jit(solution)/shard_map/ppermute | solution.py:28
  44.5 3.3 %collective-permute-done.10 = bf16[2,4,16,2432]{3,2,1,0:T(8,128)(2,1)S(1)} collective-permute-done((bf16[2,4,16,2432]{3,2,1,0:T(8,128)(2,1)S(1)}, bf16[2,4,16,2432]{3,2,1,0:T(8,128)(2,1)S(1)}, u32[]{:S(2)}, u32[]{:S(2)}) %collective-permute-start.10) | collective-permute-done | bytes 622624 | tf_op jit(solution)/shard_map/ppermute | solution.py:28
  51.4 2.7 fusion.12.refs_16_
  54.1 2.6 fusion.20.refs_4_
  60.0 2.5 fusion.115.refs_24_
  62.5 2.4 fusion.108.refs_32_
  65.0 2.5 fusion.123.refs_28_
  67.6 2.5 fusion.119.refs_36_
  70.1 2.5 fusion.127.refs_40_
  72.7 3.3 %fusion.106.refs_44_ = f32[4,4,16,512]{3,2,1,0:T(8,128)} fusion(bf16[4,4,16,2432]{3,2,1,0:T(8,128)(2,1)S(1)} %pad_maximum_fusion.2, bf16[7168,512]{1,0:T(8,128)(2,1)} %collective-permute-done.16), kind=kOutput, calls=%fused_computation.141 | convolution fusion | flops 603979776 | bytes 4063232 | tf_op jit(solution)/shard_map/dot_general | solution.py:132
  78.1 2.1 fusion.18.refs_5_
  80.2 2.1 fusion.26.refs_13_
  84.5 3.0 collective-permute-start.17
  91.0 2.9 fusion.126.refs_41_
  93.9 2.9 fusion.122.refs_29_
  96.8 2.9 fusion.118.refs_37_
  99.8 2.9 fusion.114.refs_25_
  104.5 3.3 %fusion.100.refs_45_ = f32[4,4,16,512]{3,2,1,0:T(8,128)} fusion(bf16[4,4,16,2432]{3,2,1,0:T(8,128)(2,1)S(1)} %collective-permute-done.14, bf16[7168,512]{1,0:T(8,128)(2,1)} %collective-permute-done.16), kind=kOutput, calls=%fused_computation.135 | convolution fusion | flops 603979776 | bytes 4063232 | tf_op jit(solution)/shard_map/dot_general | solution.py:132
  107.7 2.4 fusion.102.refs_33_
  115.7 2.8 collective-permute-start.21
  120.1 2.5 fusion.125.refs_42_
  122.7 2.9 fusion.121.refs_30_
  125.6 2.5 fusion.117.refs_38_
  128.2 2.5 fusion.113.refs_26_
  130.7 3.3 %fusion.94.refs_46_ = f32[4,4,16,512]{3,2,1,0:T(8,128)} fusion(bf16[4,4,16,2432]{3,2,1,0:T(8,128)(2,1)S(1)} %collective-permute-done.19, bf16[7168,512]{1,0:T(8,128)(2,1)} %collective-permute-done.16), kind=kOutput, calls=%fused_computation.129 | convolution fusion | flops 603979776 | bytes 4063232 | tf_op jit(solution)/shard_map/dot_general | solution.py:132
  135.0 2.4 fusion.96.refs_34_
  140.2 2.6 fusion.14.refs_7_
  143.6 3.4 %fusion.124.refs_43_ = f32[4,4,16,512]{3,2,1,0:T(8,128)} fusion(bf16[4,4,16,2432]{3,2,1,0:T(8,128)(2,1)S(1)} %collective-permute-done.21, bf16[7168,512]{1,0:T(8,128)(2,1)} %collective-permute-done.16), kind=kOutput, calls=%fused_computation.159 | convolution fusion | flops 637534208 | bytes 4259840 | tf_op jit(solution)/shard_map/dot_general | solution.py:132
  147.0 2.5 fusion.116.refs_39_
  149.5 2.5 fusion.120.refs_31_
  152.1 2.5 fusion.112.refs_27_
  155.4 2.4 fusion.47.refs_11_
  157.9 3.2 %fusion.88.refs_47_ = f32[4,4,16,512]{3,2,1,0:T(8,128)} fusion(bf16[4,4,16,2432]{3,2,1,0:T(8,128)(2,1)S(1)} %collective-permute-done.22, bf16[7168,512]{1,0:T(8,128)(2,1)} %collective-permute-done.16), kind=kOutput, calls=%fused_computation.123 | convolution fusion | flops 603979776 | bytes 4063232 | tf_op jit(solution)/shard_map/dot_general | solution.py:132
  161.1 2.4 fusion.90.refs_35_
  163.6 11.9 %combine.1 = (bf16[4,4,4,16,512]{4,3,2,1,0:T(8,128)(2,1)}, bf16[4,4,4,16,512]{4,3,2,1,0:T(8,128)(2,1)}, f32[1,256]{1,0:T(1,128)S(1)}) custom-call(f32[4,4,16,512]{3,2,1,0:T(8,128)S(1)} %fusion.36.refs_0_, f32[4,4,16,512]{3,2,1,0:T(8,128)S(1)} %fusion.34.refs_1_, f32[4,4,16,512]{3,2,1,0:T(8,128)S(1)} %fusion.32.refs_2_, ...), custom_call_target="tpu_custom_call" | custom-call | tf_op jit(solution)/shard_map/combine/pallas_call | solution.py:108
  177.5 3.1 %fusion.59 = f32[4,2,4,16,2304]{4,3,0,2,1:T(8,128)S(1)} fusion(bf16[512,7168]{1,0:T(8,128)(2,1)} %bitcast.65, bf16[4,2,4,16,512]{4,3,2,1,0:T(8,128)(2,1)S(1)} %get-tuple-element.152), kind=kOutput, calls=%fused_computation.85 | convolution fusion | flops 1207959552 | bytes 7602176 | tf_op jit(solution)/shard_map/dot_general | solution.py:132
  180.5 3.2 %fusion.55 = f32[2,4,4,16,2432]{4,3,2,1,0:T(8,128)S(1)} fusion(bf16[4,4,4,16,512]{4,3,2,1,0:T(8,128)(2,1)S(1)} %copy-done.1, bf16[512,7168]{1,0:T(8,128)(2,1)} %bitcast.65), kind=kOutput, calls=%fused_computation.81 | convolution fusion | flops 1275068416 | bytes 8519680 | tf_op jit(solution)/shard_map/dot_general | solution.py:132
  183.8 3.2 %fusion.56 = f32[2,4,4,16,2432]{4,3,2,1,0:T(8,128)S(1)} fusion(bf16[4,4,4,16,512]{4,3,2,1,0:T(8,128)(2,1)S(1)} %copy-done.1, bf16[512,7168]{1,0:T(8,128)(2,1)} %bitcast.65), kind=kOutput, calls=%fused_computation.82 | convolution fusion | flops 1275068416 | bytes 8519680 | tf_op jit(solution)/shard_map/dot_general | solution.py:132
  187.0 3.2 %fusion.57 = f32[4,4,2,16,2432]{4,3,1,0,2:T(8,128)S(1)} fusion(bf16[512,7168]{1,0:T(8,128)(2,1)} %bitcast.65, bf16[4,4,2,16,512]{4,3,2,1,0:T(8,128)(2,1)S(1)} %get-tuple-element.149), kind=kOutput, calls=%fused_computation.83 | convolution fusion | flops 1275068416 | bytes 7995392 | tf_op jit(solution)/shard_map/dot_general | solution.py:132
  190.2 2.9 fusion.3
  194.9 3.1 %fusion.60 = f32[4,2,4,16,2304]{4,3,0,2,1:T(8,128)S(1)} fusion(bf16[512,7168]{1,0:T(8,128)(2,1)} %bitcast.65, bf16[4,2,4,16,512]{4,3,2,1,0:T(8,128)(2,1)S(1)} %get-tuple-element.153), kind=kOutput, calls=%fused_computation.86 | convolution fusion | flops 1207959552 | bytes 7602176 | tf_op jit(solution)/shard_map/dot_general | solution.py:132
  198.2 3.2 %fusion.58 = f32[4,4,2,16,2432]{4,3,1,0,2:T(8,128)S(1)} fusion(bf16[512,7168]{1,0:T(8,128)(2,1)} %bitcast.65, bf16[4,4,2,16,512]{4,3,2,1,0:T(8,128)(2,1)S(1)} %get-tuple-element.148), kind=kOutput, calls=%fused_computation.84 | convolution fusion | flops 1275068416 | bytes 7995392 | tf_op jit(solution)/shard_map/dot_general | solution.py:132
  203.0 3.5 %collective-permute-start.24 = (bf16[2,4,4,16,2432]{4,3,2,1,0:T(8,128)(2,1)S(1)}, bf16[2,4,4,16,2432]{4,3,2,1,0:T(8,128)(2,1)S(1)}, u32[]{:S(2)}, u32[]{:S(2)}) collective-permute-start(bf16[2,4,4,16,2432]{4,3,2,1,0:T(8,128)(2,1)S(1)} %fusion.2), channel_id=1, source_target_pairs={{0,96},{32,64},{64,32},{96,0},{4,36},{36,4},{68,100},{100,68},{1,9... | collective-permute-start | bytes 7471112 | tf_op jit(solution)/shard_map/ppermute | solution.py:28
  208.3 15.2 %collective-permute-done.36 = bf16[4,2,4,16,2304]{4,3,0,2,1:T(8,128)(2,1)} collective-permute-done((bf16[4,2,4,16,2304]{4,3,0,2,1:T(8,128)(2,1)}, bf16[4,2,4,16,2304]{4,3,0,2,1:T(8,128)(2,1)}, u32[]{:S(2)}, u32[]{:S(2)}) %collective-permute-start.36) | collective-permute-done | bytes 2359328 | tf_op jit(solution)/shard_map/ppermute | solution.py:28
  223.5 3.1 %fusion = f32[4,2,4,16,2304]{4,3,0,2,1:T(8,128)S(1)} fusion(f32[4,2,4,16,2304]{4,3,0,2,1:T(8,128)S(1)} %fusion.60, bf16[4,2,4,16,2304]{4,3,0,2,1:T(8,128)(2,1)} %collective-permute-done.36, bf16[512,7168]{1,0:T(8,128)(2,1)S(1)} %collective-permute-done.23, bf16[4,2,4,16,512]{4,3,2,1,0:T(8,128)(2,1)S(1)} %get-tuple-element.150), kind=kOutput, calls=%fused_computation.8 | convolution fusion | flops 1211498496 | bytes 14680064 | tf_op jit(solution)/shard_map/dot_general | solution.py:132
  227.7 7.1 %collective-permute-done.24 = bf16[2,4,4,16,2432]{4,3,2,1,0:T(8,128)(2,1)S(1)} collective-permute-done((bf16[2,4,4,16,2432]{4,3,2,1,0:T(8,128)(2,1)S(1)}, bf16[2,4,4,16,2432]{4,3,2,1,0:T(8,128)(2,1)S(1)}, u32[]{:S(2)}, u32[]{:S(2)}) %collective-permute-start.24) | collective-permute-done | bytes 2490400 | tf_op jit(solution)/shard_map/ppermute | solution.py:28
  236.8 3.0 collective-permute-done.30
  239.8 3.2 %convert_add_fusion = f32[4,4,2,16,2432]{4,3,1,0,2:T(8,128)S(1)} fusion(bf16[4,4,2,16,2432]{4,3,1,0,2:T(8,128)(2,1)} %collective-permute-done.30, f32[4,4,2,16,2432]{4,3,1,0,2:T(8,128)S(1)} %fusion.58, bf16[512,7168]{1,0:T(8,128)(2,1)S(1)} %collective-permute-done.23, bf16[4,4,2,16,512]{4,3,2,1,0:T(8,128)(2,1)S(1)} %get-tuple-element.146), kind=kOutput, calls=%fused_computation.6 | convolution fusion | flops 1278803968 | bytes 15466496 | tf_op jit(solution)/shard_map/dot_general | solution.py:132
  246.6 7.0 %collective-permute-done.25 = bf16[4,4,16,2432]{3,2,1,0:T(8,128)(2,1)S(1)} collective-permute-done((bf16[4,4,16,2432]{3,2,1,0:T(8,128)(2,1)S(1)}, bf16[4,4,16,2432]{3,2,1,0:T(8,128)(2,1)S(1)}, u32[]{:S(2)}, u32[]{:S(2)}) %collective-permute-start.25) | collective-permute-done | bytes 1245216 | tf_op jit(solution)/shard_map/ppermute | solution.py:28
  255.5 10.1 %collective-permute-done.31 = bf16[4,4,16,2432]{3,2,1,0:T(8,128)(2,1)S(1)} collective-permute-done((bf16[4,4,16,2432]{3,2,1,0:T(8,128)(2,1)S(1)}, bf16[4,4,16,2432]{3,2,1,0:T(8,128)(2,1)S(1)}, u32[]{:S(2)}, u32[]{:S(2)}) %collective-permute-start.31) | collective-permute-done | bytes 1245216 | tf_op jit(solution)/shard_map/ppermute | solution.py:28
  267.8 5.8 %collective-permute-done.39 = bf16[4,16,2304]{2,1,0:T(8,128)(2,1)S(1)} collective-permute-done((bf16[4,16,2304]{2,1,0:T(8,128)(2,1)S(1)}, bf16[4,16,2304]{2,1,0:T(8,128)(2,1)S(1)}, u32[]{:S(2)}, u32[]{:S(2)}) %collective-permute-start.39) | collective-permute-done | bytes 294944 | tf_op jit(solution)/shard_map/ppermute | solution.py:28
  273.6 2.8 collective-permute-start.40
  277.6 2.4 collective-permute-done.40
  282.3 2.2 collective-permute-done.41
  285.6 2.2 collective-permute-done.33
  289.4 2.4 collective-permute-done.28
  292.0 2.8 collective-permute-done.34
  296.4 2.9 collective-permute-done.35
  (167 shorter events, 74.5 us)
Async XLA Ops:
  0.6 20.2 %collective-permute-start.15 = (bf16[7168,512]{1,0:T(8,128)(2,1)}, bf16[7168,512]{1,0:T(8,128)(2,1)}, u32[]{:S(2)}, u32[]{:S(2)}) collective-permute-start(bf16[7168,512]{1,0:T(8,128)(2,1)} %bitcast.298), channel_id=1, source_target_pairs={{0,4},{4,0},{1,5},{5,1},{2,6},{6,2},{3,7},{7,3},{8,12},{12,8},{9,1... | collective-permute-start | bytes 22020104 | tf_op jit(solution)/shard_map/ppermute | solution.py:32
  4.2 6.2 %collective-permute-start.2 = (bf16[16,2432]{1,0:T(8,128)(2,1)S(1)}, bf16[16,2432]{1,0:T(8,128)(2,1)S(1)}, u32[]{:S(2)}, u32[]{:S(2)}) collective-permute-start(bf16[16,2432]{1,0:T(8,128)(2,1)S(1)} %get-tuple-element.155), channel_id=1, source_target_pairs={{0,32},{32,0},{64,96},{96,64},{4,100},{36,68},{68,36},{100,4},{1,3... | collective-permute-start | bytes 233480 | tf_op jit(solution)/shard_map/ppermute | solution.py:28
  7.2 4.5 %collective-permute-start.1 = (bf16[16,2432]{1,0:T(8,128)(2,1)S(1)}, bf16[16,2432]{1,0:T(8,128)(2,1)S(1)}, u32[]{:S(2)}, u32[]{:S(2)}) collective-permute-start(bf16[16,2432]{1,0:T(8,128)(2,1)S(1)} %get-tuple-element.159), channel_id=1, source_target_pairs={{0,8},{8,0},{16,24},{24,16},{4,28},{12,20},{20,12},{28,4},{1,9},{9... | collective-permute-start | bytes 233480 | tf_op jit(solution)/shard_map/ppermute | solution.py:28
  8.8 4.4 %collective-permute-start = (bf16[16,2432]{1,0:T(8,128)(2,1)S(1)}, bf16[16,2432]{1,0:T(8,128)(2,1)S(1)}, u32[]{:S(2)}, u32[]{:S(2)}) collective-permute-start(bf16[16,2432]{1,0:T(8,128)(2,1)S(1)} %get-tuple-element.158), channel_id=1, source_target_pairs={{0,1},{1,0},{2,3},{3,2},{4,7},{5,6},{6,5},{7,4},{8,9},{9,8},{10,11... | collective-permute-start | bytes 233480 | tf_op jit(solution)/shard_map/ppermute | solution.py:28
  13.3 7.6 %collective-permute-start.5 = (bf16[2,16,2432]{2,1,0:T(8,128)(2,1)S(1)}, bf16[2,16,2432]{2,1,0:T(8,128)(2,1)S(1)}, u32[]{:S(2)}, u32[]{:S(2)}) collective-permute-start(bf16[2,16,2432]{2,1,0:T(8,128)(2,1)S(1)} %pad_maximum_fusion.12), channel_id=1, source_target_pairs={{0,96},{32,64},{64,32},{96,0},{4,36},{36,4},{68,100},{100,68},{1,9... | collective-permute-start | bytes 466952 | tf_op jit(solution)/shard_map/ppermute | solution.py:28
  15.9 6.4 %collective-permute-start.4 = (bf16[2,16,2432]{2,1,0:T(8,128)(2,1)S(1)}, bf16[2,16,2432]{2,1,0:T(8,128)(2,1)S(1)}, u32[]{:S(2)}, u32[]{:S(2)}) collective-permute-start(bf16[2,16,2432]{2,1,0:T(8,128)(2,1)S(1)} %pad_maximum_fusion.11), channel_id=1, source_target_pairs={{0,24},{8,16},{16,8},{24,0},{4,12},{12,4},{20,28},{28,20},{1,25},{... | collective-permute-start | bytes 466952 | tf_op jit(solution)/shard_map/ppermute | solution.py:28
  18.1 6.4 %collective-permute-start.3 = (bf16[2,16,2432]{2,1,0:T(8,128)(2,1)S(1)}, bf16[2,16,2432]{2,1,0:T(8,128)(2,1)S(1)}, u32[]{:S(2)}, u32[]{:S(2)}) collective-permute-start(bf16[2,16,2432]{2,1,0:T(8,128)(2,1)S(1)} %pad_maximum_fusion.10), channel_id=1, source_target_pairs={{0,3},{1,2},{2,1},{3,0},{4,5},{5,4},{6,7},{7,6},{8,11},{9,10},{10,... | collective-permute-start | bytes 466952 | tf_op jit(solution)/shard_map/ppermute | solution.py:28
  20.8 46.7 %collective-permute-start.16 = (bf16[7168,512]{1,0:T(8,128)(2,1)}, bf16[7168,512]{1,0:T(8,128)(2,1)}, u32[]{:S(2)}, u32[]{:S(2)}) collective-permute-start(bf16[7168,512]{1,0:T(8,128)(2,1)} %bitcast.295), channel_id=1, source_target_pairs={{0,4},{4,0},{1,5},{5,1},{2,6},{6,2},{3,7},{7,3},{8,12},{12,8},{9,1... | collective-permute-start | bytes 22020104 | tf_op jit(solution)/shard_map/ppermute | solution.py:32
  24.5 7.0 %collective-permute-start.8 = (bf16[4,16,2432]{2,1,0:T(8,128)(2,1)S(1)}, bf16[4,16,2432]{2,1,0:T(8,128)(2,1)S(1)}, u32[]{:S(2)}, u32[]{:S(2)}) collective-permute-start(bf16[4,16,2432]{2,1,0:T(8,128)(2,1)S(1)} %pad_maximum_fusion.8), channel_id=1, source_target_pairs={{0,1},{1,0},{2,3},{3,2},{4,7},{5,6},{6,5},{7,4},{8,9},{9,8},{10,11... | collective-permute-start | bytes 933896 | tf_op jit(solution)/shard_map/ppermute | solution.py:28
  24.9 6.9 %collective-permute-start.7 = (bf16[4,16,2432]{2,1,0:T(8,128)(2,1)S(1)}, bf16[4,16,2432]{2,1,0:T(8,128)(2,1)S(1)}, u32[]{:S(2)}, u32[]{:S(2)}) collective-permute-start(bf16[4,16,2432]{2,1,0:T(8,128)(2,1)S(1)} %pad_maximum_fusion.7), channel_id=1, source_target_pairs={{0,32},{32,0},{64,96},{96,64},{4,100},{36,68},{68,36},{100,4},{1,3... | collective-permute-start | bytes 933896 | tf_op jit(solution)/shard_map/ppermute | solution.py:28
  25.9 6.9 %collective-permute-start.6 = (bf16[4,16,2432]{2,1,0:T(8,128)(2,1)S(1)}, bf16[4,16,2432]{2,1,0:T(8,128)(2,1)S(1)}, u32[]{:S(2)}, u32[]{:S(2)}) collective-permute-start(bf16[4,16,2432]{2,1,0:T(8,128)(2,1)S(1)} %pad_maximum_fusion.6), channel_id=1, source_target_pairs={{0,8},{8,0},{16,24},{24,16},{4,28},{12,20},{20,12},{28,4},{1,9},{9... | collective-permute-start | bytes 933896 | tf_op jit(solution)/shard_map/ppermute | solution.py:28
  32.9 11.5 %collective-permute-start.11 = (bf16[2,4,16,2432]{3,2,1,0:T(8,128)(2,1)S(1)}, bf16[2,4,16,2432]{3,2,1,0:T(8,128)(2,1)S(1)}, u32[]{:S(2)}, u32[]{:S(2)}) collective-permute-start(bf16[2,4,16,2432]{3,2,1,0:T(8,128)(2,1)S(1)} %pad_maximum_fusion.5), channel_id=1, source_target_pairs={{0,3},{1,2},{2,1},{3,0},{4,5},{5,4},{6,7},{7,6},{8,11},{9,10},{10,... | collective-permute-start | bytes 1867784 | tf_op jit(solution)/shard_map/ppermute | solution.py:28
  35.5 12.3 %collective-permute-start.10 = (bf16[2,4,16,2432]{3,2,1,0:T(8,128)(2,1)S(1)}, bf16[2,4,16,2432]{3,2,1,0:T(8,128)(2,1)S(1)}, u32[]{:S(2)}, u32[]{:S(2)}) collective-permute-start(bf16[2,4,16,2432]{3,2,1,0:T(8,128)(2,1)S(1)} %pad_maximum_fusion.4), channel_id=1, source_target_pairs={{0,96},{32,64},{64,32},{96,0},{4,36},{36,4},{68,100},{100,68},{1,9... | collective-permute-start | bytes 1867784 | tf_op jit(solution)/shard_map/ppermute | solution.py:28
  36.2 11.7 %collective-permute-start.9 = (bf16[2,4,16,2432]{3,2,1,0:T(8,128)(2,1)S(1)}, bf16[2,4,16,2432]{3,2,1,0:T(8,128)(2,1)S(1)}, u32[]{:S(2)}, u32[]{:S(2)}) collective-permute-start(bf16[2,4,16,2432]{3,2,1,0:T(8,128)(2,1)S(1)} %pad_maximum_fusion.3), channel_id=1, source_target_pairs={{0,24},{8,16},{16,8},{24,0},{4,12},{12,4},{20,28},{28,20},{1,25},{... | collective-permute-start | bytes 1867784 | tf_op jit(solution)/shard_map/ppermute | solution.py:28
  47.8 9.8 %slice-start.2 = ((s8[7340032]{0:T(1024)(128)(4,1)}), s8[4194304]{0:T(1024)(128)(4,1)S(1)}, s32[]{:S(2)}) async-start(s8[7340032]{0:T(1024)(128)(4,1)} %bitcast.299), calls=%async_computation.2 | async-start | bytes 8388608
  47.9 8.8 %slice-start = ((s8[7340032]{0:T(1024)(128)(4,1)}), s8[4194304]{0:T(1024)(128)(4,1)S(1)}, s32[]{:S(2)}) async-start(s8[7340032]{0:T(1024)(128)(4,1)} %bitcast.296), calls=%async_computation | async-start | bytes 8388608
  48.1 27.9 %collective-permute-start.12 = (bf16[4,4,16,2432]{3,2,1,0:T(8,128)(2,1)S(1)}, bf16[4,4,16,2432]{3,2,1,0:T(8,128)(2,1)}, u32[]{:S(2)}, u32[]{:S(2)}) collective-permute-start(bf16[4,4,16,2432]{3,2,1,0:T(8,128)(2,1)S(1)} %pad_maximum_fusion), channel_id=1, source_target_pairs={{0,32},{32,0},{64,96},{96,64},{4,100},{36,68},{68,36},{100,4},{1,3... | collective-permute-start | bytes 3735560 | tf_op jit(solution)/shard_map/ppermute | solution.py:28
  48.4 27.5 %collective-permute-start.13 = (bf16[4,4,16,2432]{3,2,1,0:T(8,128)(2,1)S(1)}, bf16[4,4,16,2432]{3,2,1,0:T(8,128)(2,1)}, u32[]{:S(2)}, u32[]{:S(2)}) collective-permute-start(bf16[4,4,16,2432]{3,2,1,0:T(8,128)(2,1)S(1)} %pad_maximum_fusion.1), channel_id=1, source_target_pairs={{0,1},{1,0},{2,3},{3,2},{4,7},{5,6},{6,5},{7,4},{8,9},{9,8},{10,11... | collective-permute-start | bytes 3735560 | tf_op jit(solution)/shard_map/ppermute | solution.py:28
  49.7 26.2 %collective-permute-start.14 = (bf16[4,4,16,2432]{3,2,1,0:T(8,128)(2,1)S(1)}, bf16[4,4,16,2432]{3,2,1,0:T(8,128)(2,1)S(1)}, u32[]{:S(2)}, u32[]{:S(2)}) collective-permute-start(bf16[4,4,16,2432]{3,2,1,0:T(8,128)(2,1)S(1)} %pad_maximum_fusion.2), channel_id=1, source_target_pairs={{0,8},{8,0},{16,24},{24,16},{4,28},{12,20},{20,12},{28,4},{1,9},{9... | collective-permute-start | bytes 3735560 | tf_op jit(solution)/shard_map/ppermute | solution.py:28
  51.4 5.3 %slice-start.1 = ((s8[7340032]{0:T(1024)(128)(4,1)}), s8[3145728]{0:T(1024)(128)(4,1)S(1)}, s32[]{:S(2)}) async-start(s8[7340032]{0:T(1024)(128)(4,1)} %bitcast.296), calls=%async_computation.1 | async-start | bytes 6291456
  51.4 6.1 %slice-start.3 = ((s8[7340032]{0:T(1024)(128)(4,1)}), s8[3145728]{0:T(1024)(128)(4,1)S(1)}, s32[]{:S(2)}) async-start(s8[7340032]{0:T(1024)(128)(4,1)} %bitcast.299), calls=%async_computation.3 | async-start | bytes 6291456
  84.5 25.7 %collective-permute-start.17 = (bf16[4,4,16,2432]{3,2,1,0:T(8,128)(2,1)S(1)}, bf16[4,4,16,2432]{3,2,1,0:T(8,128)(2,1)S(1)}, u32[]{:S(2)}, u32[]{:S(2)}) collective-permute-start(bf16[4,4,16,2432]{3,2,1,0:T(8,128)(2,1)S(1)} %pad_maximum_fusion), channel_id=1, source_target_pairs={{0,96},{32,64},{64,32},{96,0},{4,36},{36,4},{68,100},{100,68},{1,9... | collective-permute-start | bytes 3735560 | tf_op jit(solution)/shard_map/ppermute | solution.py:28
  87.5 22.7 %collective-permute-start.18 = (bf16[4,4,16,2432]{3,2,1,0:T(8,128)(2,1)S(1)}, bf16[4,4,16,2432]{3,2,1,0:T(8,128)(2,1)S(1)}, u32[]{:S(2)}, u32[]{:S(2)}) collective-permute-start(bf16[4,4,16,2432]{3,2,1,0:T(8,128)(2,1)S(1)} %pad_maximum_fusion.1), channel_id=1, source_target_pairs={{0,3},{1,2},{2,1},{3,0},{4,5},{5,4},{6,7},{7,6},{8,11},{9,10},{10,... | collective-permute-start | bytes 3735560 | tf_op jit(solution)/shard_map/ppermute | solution.py:28
  87.8 22.4 %collective-permute-start.19 = (bf16[4,4,16,2432]{3,2,1,0:T(8,128)(2,1)S(1)}, bf16[4,4,16,2432]{3,2,1,0:T(8,128)(2,1)S(1)}, u32[]{:S(2)}, u32[]{:S(2)}) collective-permute-start(bf16[4,4,16,2432]{3,2,1,0:T(8,128)(2,1)S(1)} %pad_maximum_fusion.2), channel_id=1, source_target_pairs={{0,24},{8,16},{16,8},{24,0},{4,12},{12,4},{20,28},{28,20},{1,25},{... | collective-permute-start | bytes 3735560 | tf_op jit(solution)/shard_map/ppermute | solution.py:28
  90.4 99.9 %collective-permute-start.23 = (bf16[512,7168]{1,0:T(8,128)(2,1)}, bf16[512,7168]{1,0:T(8,128)(2,1)S(1)}, u32[]{:S(2)}, u32[]{:S(2)}) collective-permute-start(bf16[512,7168]{1,0:T(8,128)(2,1)} %bitcast.65), channel_id=1, source_target_pairs={{0,4},{4,0},{1,5},{5,1},{2,6},{6,2},{3,7},{7,3},{8,12},{12,8},{9,1... | collective-permute-start | bytes 22020104 | tf_op jit(solution)/shard_map/ppermute | solution.py:32
  110.2 9.9 %copy-start.2 = (bf16[4,4,16,2432]{3,2,1,0:T(8,128)(2,1)}, bf16[4,4,16,2432]{3,2,1,0:T(8,128)(2,1)S(1)}, u32[]{:S(2)}) copy-start(bf16[4,4,16,2432]{3,2,1,0:T(8,128)(2,1)S(1)} %collective-permute-done.18) | copy-start | bytes 3735556
  115.1 22.3 %collective-permute-start.20 = (bf16[4,4,16,2432]{3,2,1,0:T(8,128)(2,1)}, bf16[4,4,16,2432]{3,2,1,0:T(8,128)(2,1)S(1)}, u32[]{:S(2)}, u32[]{:S(2)}) collective-permute-start(bf16[4,4,16,2432]{3,2,1,0:T(8,128)(2,1)} %collective-permute-done.12), channel_id=1, source_target_pairs={{0,96},{32,64},{64,32},{96,0},{4,36},{36,4},{68,100},{100,68},{1,9... | collective-permute-start | bytes 3735560 | tf_op jit(solution)/shard_map/ppermute | solution.py:28
  115.7 21.8 %collective-permute-start.21 = (bf16[4,4,16,2432]{3,2,1,0:T(8,128)(2,1)}, bf16[4,4,16,2432]{3,2,1,0:T(8,128)(2,1)S(1)}, u32[]{:S(2)}, u32[]{:S(2)}) collective-permute-start(bf16[4,4,16,2432]{3,2,1,0:T(8,128)(2,1)} %collective-permute-done.13), channel_id=1, source_target_pairs={{0,3},{1,2},{2,1},{3,0},{4,5},{5,4},{6,7},{7,6},{8,11},{9,10},{10,... | collective-permute-start | bytes 3735560 | tf_op jit(solution)/shard_map/ppermute | solution.py:28
  118.6 19.0 %collective-permute-start.22 = (bf16[4,4,16,2432]{3,2,1,0:T(8,128)(2,1)S(1)}, bf16[4,4,16,2432]{3,2,1,0:T(8,128)(2,1)S(1)}, u32[]{:S(2)}, u32[]{:S(2)}) collective-permute-start(bf16[4,4,16,2432]{3,2,1,0:T(8,128)(2,1)S(1)} %collective-permute-done.14), channel_id=1, source_target_pairs={{0,24},{8,16},{16,8},{24,0},{4,12},{12,4},{20,28},{28,20},{1,25},{... | collective-permute-start | bytes 3735560 | tf_op jit(solution)/shard_map/ppermute | solution.py:28
  175.5 1.5 copy-start.1
  175.5 1.9 copy-start
  193.1 30.4 %collective-permute-start.36 = (bf16[4,2,4,16,2304]{4,3,0,2,1:T(8,128)(2,1)}, bf16[4,2,4,16,2304]{4,3,0,2,1:T(8,128)(2,1)}, u32[]{:S(2)}, u32[]{:S(2)}) collective-permute-start(bf16[4,2,4,16,2304]{4,3,0,2,1:T(8,128)(2,1)} %fusion.3), channel_id=1, source_target_pairs={{0,24},{8,16},{16,8},{24,0},{4,12},{12,4},{20,28},{28,20},{1,25},{... | collective-permute-start | bytes 7077896 | tf_op jit(solution)/shard_map/ppermute | solution.py:28
  198.0 8.5 %collective-permute-start.42 = (f32[1,128]{1,0:T(1,128)S(1)}, f32[1,128]{1,0:T(1,128)S(1)}, u32[]{:S(2)}, u32[]{:S(2)}) collective-permute-start(f32[1,128]{1,0:T(1,128)S(1)} %slice.387), channel_id=1, source_target_pairs={{0,4},{4,0},{1,5},{5,1},{2,6},{6,2},{3,7},{7,3},{8,12},{12,8},{9,1... | collective-permute-start | bytes 1544 | tf_op jit(solution)/shard_map/ppermute | solution.py:32
  203.0 31.8 %collective-permute-start.24 = (bf16[2,4,4,16,2432]{4,3,2,1,0:T(8,128)(2,1)S(1)}, bf16[2,4,4,16,2432]{4,3,2,1,0:T(8,128)(2,1)S(1)}, u32[]{:S(2)}, u32[]{:S(2)}) collective-permute-start(bf16[2,4,4,16,2432]{4,3,2,1,0:T(8,128)(2,1)S(1)} %fusion.2), channel_id=1, source_target_pairs={{0,96},{32,64},{64,32},{96,0},{4,36},{36,4},{68,100},{100,68},{1,9... | collective-permute-start | bytes 7471112 | tf_op jit(solution)/shard_map/ppermute | solution.py:28
  208.2 31.6 %collective-permute-start.30 = (bf16[4,4,2,16,2432]{4,3,1,0,2:T(8,128)(2,1)S(1)}, bf16[4,4,2,16,2432]{4,3,1,0,2:T(8,128)(2,1)}, u32[]{:S(2)}, u32[]{:S(2)}) collective-permute-start(bf16[4,4,2,16,2432]{4,3,1,0,2:T(8,128)(2,1)S(1)} %fusion.1), channel_id=1, source_target_pairs={{0,3},{1,2},{2,1},{3,0},{4,5},{5,4},{6,7},{7,6},{8,11},{9,10},{10,... | collective-permute-start | bytes 7471112 | tf_op jit(solution)/shard_map/ppermute | solution.py:28
  227.7 16.5 %collective-permute-start.37 = (bf16[4,4,16,2304]{3,2,0,1:T(8,128)(2,1)}, bf16[4,4,16,2304]{3,2,0,1:T(8,128)(2,1)}, u32[]{:S(2)}, u32[]{:S(2)}) collective-permute-start(bf16[4,4,16,2304]{3,2,0,1:T(8,128)(2,1)} %fusion.87), channel_id=1, source_target_pairs={{0,8},{8,0},{16,24},{24,16},{4,28},{12,20},{20,12},{28,4},{1,9},{9... | collective-permute-start | bytes 3538952 | tf_op jit(solution)/shard_map/ppermute | solution.py:28
  236.7 17.0 %collective-permute-start.25 = (bf16[4,4,16,2432]{3,2,1,0:T(8,128)(2,1)S(1)}, bf16[4,4,16,2432]{3,2,1,0:T(8,128)(2,1)S(1)}, u32[]{:S(2)}, u32[]{:S(2)}) collective-permute-start(bf16[4,4,16,2432]{3,2,1,0:T(8,128)(2,1)S(1)} %fusion.85), channel_id=1, source_target_pairs={{0,32},{32,0},{64,96},{96,64},{4,100},{36,68},{68,36},{100,4},{1,3... | collective-permute-start | bytes 3735560 | tf_op jit(solution)/shard_map/ppermute | solution.py:28
  243.2 22.4 %collective-permute-start.31 = (bf16[4,4,16,2432]{3,2,1,0:T(8,128)(2,1)S(1)}, bf16[4,4,16,2432]{3,2,1,0:T(8,128)(2,1)S(1)}, u32[]{:S(2)}, u32[]{:S(2)}) collective-permute-start(bf16[4,4,16,2432]{3,2,1,0:T(8,128)(2,1)S(1)} %fusion.86), channel_id=1, source_target_pairs={{0,1},{1,0},{2,3},{3,2},{4,7},{5,6},{6,5},{7,4},{8,9},{9,8},{10,11... | collective-permute-start | bytes 3735560 | tf_op jit(solution)/shard_map/ppermute | solution.py:28
  245.8 20.7 %collective-permute-start.38 = (bf16[4,2,16,2304]{3,2,0,1:T(8,128)(2,1)S(1)}, bf16[4,2,16,2304]{3,2,0,1:T(8,128)(2,1)S(1)}, u32[]{:S(2)}, u32[]{:S(2)}) collective-permute-start(bf16[4,2,16,2304]{3,2,0,1:T(8,128)(2,1)S(1)} %slice.694), channel_id=1, source_target_pairs={{0,3},{1,2},{2,1},{3,0},{4,5},{5,4},{6,7},{7,6},{8,11},{9,10},{10,... | collective-permute-start | bytes 1769480 | tf_op jit(solution)/shard_map/ppermute | solution.py:28
  254.0 13.3 %collective-permute-start.26 = (bf16[2,4,16,2432]{3,2,1,0:T(8,128)(2,1)S(1)}, bf16[2,4,16,2432]{3,2,1,0:T(8,128)(2,1)S(1)}, u32[]{:S(2)}, u32[]{:S(2)}) collective-permute-start(bf16[2,4,16,2432]{3,2,1,0:T(8,128)(2,1)S(1)} %slice.693), channel_id=1, source_target_pairs={{0,24},{8,16},{16,8},{24,0},{4,12},{12,4},{20,28},{28,20},{1,25},{... | collective-permute-start | bytes 1867784 | tf_op jit(solution)/shard_map/ppermute | solution.py:28
  265.9 11.5 %collective-permute-start.32 = (bf16[2,4,16,2432]{3,2,1,0:T(8,128)(2,1)S(1)}, bf16[2,4,16,2432]{3,2,1,0:T(8,128)(2,1)S(1)}, u32[]{:S(2)}, u32[]{:S(2)}) collective-permute-start(bf16[2,4,16,2432]{3,2,1,0:T(8,128)(2,1)S(1)} %slice.692), channel_id=1, source_target_pairs={{0,96},{32,64},{64,32},{96,0},{4,36},{36,4},{68,100},{100,68},{1,9... | collective-permute-start | bytes 1867784 | tf_op jit(solution)/shard_map/ppermute | solution.py:28
  266.7 6.8 %collective-permute-start.39 = (bf16[4,16,2304]{2,1,0:T(8,128)(2,1)S(1)}, bf16[4,16,2304]{2,1,0:T(8,128)(2,1)S(1)}, u32[]{:S(2)}, u32[]{:S(2)}) collective-permute-start(bf16[4,16,2304]{2,1,0:T(8,128)(2,1)S(1)} %fusion.141), channel_id=1, source_target_pairs={{0,1},{1,0},{2,3},{3,2},{4,7},{5,6},{6,5},{7,4},{8,9},{9,8},{10,11... | collective-permute-start | bytes 884744 | tf_op jit(solution)/shard_map/ppermute | solution.py:28
  267.5 17.1 %collective-permute-start.27 = (bf16[4,16,2432]{2,1,0:T(8,128)(2,1)S(1)}, bf16[4,16,2432]{2,1,0:T(8,128)(2,1)S(1)}, u32[]{:S(2)}, u32[]{:S(2)}) collective-permute-start(bf16[4,16,2432]{2,1,0:T(8,128)(2,1)S(1)} %fusion.139), channel_id=1, source_target_pairs={{0,8},{8,0},{16,24},{24,16},{4,28},{12,20},{20,12},{28,4},{1,9},{9... | collective-permute-start | bytes 933896 | tf_op jit(solution)/shard_map/ppermute | solution.py:28
  273.6 6.4 %collective-permute-start.40 = (bf16[2,16,2304]{2,1,0:T(8,128)(2,1)S(1)}, bf16[2,16,2304]{2,1,0:T(8,128)(2,1)S(1)}, u32[]{:S(2)}, u32[]{:S(2)}) collective-permute-start(bf16[2,16,2304]{2,1,0:T(8,128)(2,1)S(1)} %slice.697), channel_id=1, source_target_pairs={{0,96},{32,64},{64,32},{96,0},{4,36},{36,4},{68,100},{100,68},{1,9... | collective-permute-start | bytes 442376 | tf_op jit(solution)/shard_map/ppermute | solution.py:28
  280.1 4.4 %collective-permute-start.41 = (bf16[16,2304]{1,0:T(8,128)(2,1)S(1)}, bf16[16,2304]{1,0:T(8,128)(2,1)S(1)}, u32[]{:S(2)}, u32[]{:S(2)}) collective-permute-start(bf16[16,2304]{1,0:T(8,128)(2,1)S(1)} %fusion.150), channel_id=1, source_target_pairs={{0,32},{32,0},{64,96},{96,64},{4,100},{36,68},{68,36},{100,4},{1,3... | collective-permute-start | bytes 221192 | tf_op jit(solution)/shard_map/ppermute | solution.py:28
  280.2 7.6 %collective-permute-start.33 = (bf16[4,16,2432]{2,1,0:T(8,128)(2,1)S(1)}, bf16[4,16,2432]{2,1,0:T(8,128)(2,1)S(1)}, u32[]{:S(2)}, u32[]{:S(2)}) collective-permute-start(bf16[4,16,2432]{2,1,0:T(8,128)(2,1)S(1)} %fusion.140), channel_id=1, source_target_pairs={{0,32},{32,0},{64,96},{96,64},{4,100},{36,68},{68,36},{100,4},{1,3... | collective-permute-start | bytes 933896 | tf_op jit(solution)/shard_map/ppermute | solution.py:28
  284.6 7.2 %collective-permute-start.28 = (bf16[2,16,2432]{2,1,0:T(8,128)(2,1)S(1)}, bf16[2,16,2432]{2,1,0:T(8,128)(2,1)S(1)}, u32[]{:S(2)}, u32[]{:S(2)}) collective-permute-start(bf16[2,16,2432]{2,1,0:T(8,128)(2,1)S(1)} %slice.696), channel_id=1, source_target_pairs={{0,3},{1,2},{2,1},{3,0},{4,5},{5,4},{6,7},{7,6},{8,11},{9,10},{10,... | collective-permute-start | bytes 466952 | tf_op jit(solution)/shard_map/ppermute | solution.py:28
  288.0 6.9 %collective-permute-start.34 = (bf16[2,16,2432]{2,1,0:T(8,128)(2,1)S(1)}, bf16[2,16,2432]{2,1,0:T(8,128)(2,1)S(1)}, u32[]{:S(2)}, u32[]{:S(2)}) collective-permute-start(bf16[2,16,2432]{2,1,0:T(8,128)(2,1)S(1)} %slice.695), channel_id=1, source_target_pairs={{0,24},{8,16},{16,8},{24,0},{4,12},{12,4},{20,28},{28,20},{1,25},{... | collective-permute-start | bytes 466952 | tf_op jit(solution)/shard_map/ppermute | solution.py:28
  291.9 4.5 %collective-permute-start.29 = (bf16[16,2432]{1,0:T(8,128)(2,1)S(1)}, bf16[16,2432]{1,0:T(8,128)(2,1)S(1)}, u32[]{:S(2)}, u32[]{:S(2)}) collective-permute-start(bf16[16,2432]{1,0:T(8,128)(2,1)S(1)} %fusion.148), channel_id=1, source_target_pairs={{0,1},{1,0},{2,3},{3,2},{4,7},{5,6},{6,5},{7,4},{8,9},{9,8},{10,11... | collective-permute-start | bytes 233480 | tf_op jit(solution)/shard_map/ppermute | solution.py:28
  294.9 4.5 %collective-permute-start.35 = (bf16[16,2432]{1,0:T(8,128)(2,1)S(1)}, bf16[16,2432]{1,0:T(8,128)(2,1)S(1)}, u32[]{:S(2)}, u32[]{:S(2)}) collective-permute-start(bf16[16,2432]{1,0:T(8,128)(2,1)S(1)} %fusion.149), channel_id=1, source_target_pairs={{0,8},{8,0},{16,24},{24,16},{4,28},{12,20},{20,12},{28,4},{1,9},{9... | collective-permute-start | bytes 233480 | tf_op jit(solution)/shard_map/ppermute | solution.py:28
where the time goes:
time: 308 us; the launch traced here: 302 us
  matrix products  135 us (44%)
  waiting for transfers between devices  89.6 us (29%)
  starting transfers between devices  49 us (16%)
  Pallas kernels  11.9 us (4%)
  local copies, waits for them, and re-layouts  6.96 us (2%)
  other arithmetic  5.76 us (2%)
  between operations  3.22 us (1%)
    dot_general x64, matrix products, product(): out = jnp.dot(flat, weight, preferred_element_type=jnp.float32)  135 us
    ppermute x39, waiting for transfers between devices, pairwise(): return lax.ppermute(v, ('c', 'x') if axis == 'x' else (axis, 'c'), pairs)  89.6 us
    ppermute x39, starting transfers between devices, pairwise(): return lax.ppermute(v, ('c', 'x') if axis == 'x' else (axis, 'c'), pairs)  48.2 us
    pallas_call x1, Pallas kernels, combine(): pl.pallas_call(combine_kernel, out_shape=(rows, rows, jax.ShapeDtypeStruc...  11.9 us
  transfers between devices with their start and end apart: 43, of which 24 were waited for; matrix products, arithmetic and copies ran while one was open for 45% of the time, Pallas kernels for 4%

commit v1 on v0

v1 whole, which is shorter than its diff:
```python
import jax
import jax.numpy as jnp
from jax import lax
from jax.experimental import pallas as pl
from jax.experimental.pallas import tpu as pltpu
from jax.sharding import Mesh
from jax.sharding import PartitionSpec as P

EP = ("z", "y", "c")
EP_DP = ("z", "y", "c", "x")
ROUTE_SCALE = 2.5
EXTRA = 128
SIDE = 4
GATHER = (("x", "y", "z"), ("y", "z", "x"), ("z", "x", "y"))
REDUCE = (("z", "y", "x"), ("x", "z", "y"), ("y", "x", "z"))


def pairwise(v, axis, turn):
    pairs = []
    for core in range(2):
        flip = 1 if core == turn else 3
        for i in range(SIDE):
            j = i ^ flip
            if axis == "x":
                pairs.append((core * SIDE + i, core * SIDE + j))
            else:
                pairs.append((i * 2 + core, j * 2 + core))
    return lax.ppermute(v, ("c", "x") if axis == "x" else (axis, "c"), pairs)


def swap(v):
    return lax.ppermute(v, "c", [(0, 1), (1, 0)])


def after(values, *others):
    return list(lax.optimization_barrier(tuple(values) + others)[: len(values)])


def split(values):
    return values[:3], values[3:6], values[6]


def route_columns(routes, route_logits, experts):
    affinity = jax.nn.sigmoid(route_logits)
    weights = ROUTE_SCALE * affinity / jnp.sum(affinity, axis=1, keepdims=True)
    hit = routes[:, :, None] == jnp.arange(experts, dtype=jnp.int32)[None, None, :]
    mask = jnp.sum(hit.astype(jnp.float32), axis=1)
    dense = jnp.sum(jnp.where(hit, weights[:, :, None], 0.0), axis=1)
    high = lax.reduce_precision(dense, 8, 7)
    rest = dense - high
    mid = lax.reduce_precision(rest, 8, 7)
    low = rest - mid
    return jnp.concatenate([mask, high, mid, low], axis=1).astype(jnp.bfloat16)


def in_kernel(limits, t0, t1, t2, w0, w1, w2, w3, out, acc):
    j = pl.program_id(0)

    @pl.when((j == 0) | (j == limits[0]) | (j == limits[1]))
    def _():
        acc[...] = jnp.zeros_like(acc)

    flat = [t[...].reshape(acc.shape[1], t.shape[-1]) for t in (t0, t1, t2)]
    rows = jnp.where(j < limits[0], flat[0], jnp.where(j < limits[1], flat[1], flat[2]))
    for k, w in enumerate((w0, w1, w2, w3)):
        acc[k] += jnp.dot(rows, w[...], preferred_element_type=jnp.float32)

    @pl.when((j == limits[0] - 1) | (j == limits[1] - 1) | (j == limits[2] - 1))
    def _():
        out[0] = acc[...].astype(jnp.bfloat16).reshape(out.shape[1:])


def products(blocks, weights, starts, model, chunk):
    tok, width = blocks[0].shape[2], weights[0].shape[1]
    limits = (starts[1] // chunk, starts[2] // chunk, model // chunk)
    firsts = (0,) + limits[:2]
    tokens = [
        pl.BlockSpec(
            (SIDE, SIDE, tok, chunk),
            lambda j, lo=lo, hi=hi: (0, 0, 0, jnp.clip(j, lo, hi - 1) - lo),
        )
        for lo, hi in zip(firsts, limits)
    ]

    def third(j):
        return ((j >= limits[0]).astype(jnp.int32) + (j >= limits[1]).astype(jnp.int32), 0, 0, 0, 0, 0)

    return pl.pallas_call(
        lambda *refs: in_kernel(limits, *refs),
        out_shape=jax.ShapeDtypeStruct((3, 4, SIDE, SIDE, tok, width), jnp.bfloat16),
        grid=(model // chunk,),
        in_specs=tokens + [pl.BlockSpec((chunk, width), lambda j: (j, 0))] * 4,
        out_specs=pl.BlockSpec((1, 4, SIDE, SIDE, tok, width), third),
        scratch_shapes=[pltpu.VMEM((4, SIDE * SIDE * tok, width), jnp.float32)],
        name="products",
    )(*blocks, *weights)


def combine_kernel(start, *refs):
    parts, extras = refs[:4], refs[4:8]
    pick_ref = refs[8]
    own_ref, peer_ref, count_ref = refs[9:12]
    buf, extra_buf, route_buf, sems = refs[12:]

    def copies(i, slot):
        sem = sems.at[slot]
        out = [pltpu.make_async_copy(parts[i].at[0], buf.at[slot, :, 0], sem.at[0])]
        for r in range(SIDE):
            out.append(
                pltpu.make_async_copy(parts[r].at[1, :, i], buf.at[slot, :, 1, :, r], sem.at[1 + r])
            )
            out.append(
                pltpu.make_async_copy(parts[r].at[2, :, :, i], buf.at[slot, :, 2, r], sem.at[5 + r])
            )
            out.append(
                pltpu.make_async_copy(
                    extras[r].at[:, i, :, start : start + EXTRA], extra_buf.at[slot, r], sem.at[9 + r]
                )
            )
        return out

    for copy in copies(0, 0):
        copy.start()
    tok, width = buf.shape[-2:]
    count_ref[...] = jnp.zeros_like(count_ref)
    for i in range(SIDE):
        slot = i % 2
        if i + 1 < SIDE:
            for copy in copies(i + 1, 1 - slot):
                copy.start()
        for copy in copies(i, slot):
            copy.wait()
        extra = extra_buf[slot].reshape(SIDE * SIDE * tok, EXTRA)
        route = jnp.dot(extra, pick_ref[...], preferred_element_type=jnp.float32)
        count_ref[...] += jnp.sum(route[:, 256:], axis=0, keepdims=True)
        route_buf[...] = route[:, :256].reshape(route_buf.shape)

        def block(n, carry, i=i, slot=slot):
            y, x = n // SIDE, n % SIDE
            sums = []
            for k in range(4):
                three = [buf[slot, k, t, y, x].astype(jnp.float32) for t in range(3)]
                sums.append(three[0] + three[1] + three[2])
            weights = route_buf[y, x]
            for e, out in enumerate((own_ref, peer_ref)):
                gate, up = sums[2 * e], sums[2 * e + 1]
                weight = weights[:, e * 128 : e * 128 + 128]
                weight = jnp.concatenate([weight] * (width // 128), axis=1)
                act = gate / (1.0 + jnp.exp(-gate)) * up * weight
                out[i, y, x] = act.astype(jnp.bfloat16)
            return carry

        lax.fori_loop(0, SIDE * SIDE, block, 0)


def combine(parts, extras, pick, start):
    tok, width = parts[0].shape[-2:]
    rows = jax.ShapeDtypeStruct((SIDE, SIDE, SIDE, tok, width), jnp.bfloat16)
    return pl.pallas_call(
        lambda *refs: combine_kernel(start, *refs),
        out_shape=(rows, rows, jax.ShapeDtypeStruct((1, 256), jnp.float32)),
        in_specs=[pl.BlockSpec(memory_space=pl.ANY)] * 8 + [pl.BlockSpec(memory_space=pltpu.VMEM)],
        out_specs=(pl.BlockSpec(memory_space=pltpu.VMEM),) * 3,
        scratch_shapes=[
            pltpu.VMEM((2, 4, 3, SIDE, SIDE, tok, width), jnp.bfloat16),
            pltpu.VMEM((2, SIDE, SIDE, tok, EXTRA), jnp.bfloat16),
            pltpu.VMEM((SIDE, SIDE, tok, 256), jnp.float32),
            pltpu.SemaphoreType.DMA((2, 13)),
        ],
        name="combine",
    )(*parts, *extras, pick)


def down_kernel(d, lo, added, own_ref, peer_ref, own_w, peer_w, *refs):
    for p in range(2):
        index = (slice(None),) * d + (lo + p,)
        flat = own_ref[index].reshape(-1, own_ref.shape[-1])
        total = jnp.dot(flat, own_w[...], preferred_element_type=jnp.float32)
        flat = peer_ref[index].reshape(-1, peer_ref.shape[-1])
        total = total + jnp.dot(flat, peer_w[...], preferred_element_type=jnp.float32)
        if added:
            got, outs = refs[0], refs[1:]
            total = total + got[p].astype(jnp.float32)
            outs[p][...] = total.astype(outs[p].dtype)
        else:
            refs[0][p] = total.astype(jnp.bfloat16)


def down(own_rows, peer_rows, own_w, peer_w, d, lo, start, size, chunk, got=None):
    tok, width = own_rows.shape[-2:]
    count = SIDE * SIDE * tok
    whole = pl.BlockSpec(own_rows.shape, lambda j: (0,) * 5)
    weight = pl.BlockSpec((width, chunk), lambda j: (0, start // chunk + j))
    pair = pl.BlockSpec((2, count, chunk), lambda j: (0, 0, j))
    one = pl.BlockSpec((count, chunk), lambda j: (0, j))
    operands, specs = [own_rows, peer_rows, own_w, peer_w], [whole, whole, weight, weight]
    if got is None:
        out_shape, out_specs = jax.ShapeDtypeStruct((2, count, size), jnp.bfloat16), pair
    else:
        operands, specs = operands + [got], specs + [pair]
        out_shape = (
            jax.ShapeDtypeStruct((count, size), jnp.float32),
            jax.ShapeDtypeStruct((count, size), jnp.bfloat16),
        )
        out_specs = (one, one)
    return pl.pallas_call(
        lambda *refs: down_kernel(d, lo, got is not None, *refs),
        out_shape=out_shape,
        grid=(size // chunk,),
        in_specs=specs,
        out_specs=out_specs,
        compiler_params=pltpu.CompilerParams(vmem_limit_bytes=32 * 1024 * 1024),
        name="down",
    )(*operands)


def cut(total, chunk):
    tiles = total // chunk
    sizes = [(tiles // 3 + (1 if i < tiles % 3 else 0)) * chunk for i in range(3)]
    return [sum(sizes[:i]) for i in range(3)], sizes


def on_device(tokens, routes, route_logits, gate_weight, up_weight, down_weight):
    tok, model = tokens.shape
    top_k = routes.shape[1]
    experts = lax.axis_size(EP)
    width = gate_weight.shape[2]
    expert = lax.axis_index(EP)
    gate_w, up_w, down_w = gate_weight[0], up_weight[0], down_weight[0]

    gate_p = swap(gate_w)
    up_p = swap(after([up_w], gate_p)[0])
    down_p = swap(after([down_w], up_p)[0])

    chunk = min(512, model // 3 // 128 * 128)
    starts, sizes = cut(model, chunk)
    whole = jnp.concatenate([tokens, route_columns(routes, route_logits, experts)], axis=1)
    stops = starts[1:] + [model + EXTRA]
    current = [whole[:, lo:hi] for lo, hi in zip(starts, stops)]
    for stage in range(2):
        got = [pairwise(c, GATHER[t][stage], 0) for t, c in enumerate(current)]
        current = after([jnp.stack([c, g]) for c, g in zip(current, got)])
        got = [pairwise(c, GATHER[t][stage], 1) for t, c in enumerate(current)]
        current = after([jnp.concatenate([c, g]) for c, g in zip(current, got)])

    lanes = jnp.arange(EXTRA, dtype=jnp.int32)
    own, peer = lanes % experts == expert, lanes % experts == expert + 1 - 2 * lax.axis_index("c")
    columns = [own & (lanes >= experts), peer & (lanes >= experts)]
    columns += [own & (lanes < experts), peer & (lanes < experts)]
    pick = jnp.concatenate(
        [jnp.broadcast_to(c[:, None], (EXTRA, 128)) for c in columns], axis=1
    ).astype(jnp.bfloat16)

    def part(blocks):
        return products(blocks, (gate_w, up_w, gate_p, up_p), starts, model, chunk)

    def moved(blocks, turn):
        return [pairwise(b, GATHER[t][2], turn) for t, b in enumerate(blocks)]

    me = current
    first, p0 = moved(me, 0), part(me)
    first, me, p0 = split(after(first + me + [p0]))
    second, p1 = moved(me, 1), part(first)
    second, first, p1 = split(after(second + first + [p1]))
    both, p2 = moved(first, 1), part(second)
    both, second, p2 = split(after(both + second + [p2]))
    parts = [p0, p1, p2, part(both)]
    extras = [me[2], first[2], second[2], both[2]]
    own_rows, peer_rows, count = combine(parts, extras, pick, model - starts[2])

    weights = (own_rows, peer_rows, down_w, down_p)
    names = [["z", "y", "x"] for _ in REDUCE]

    def traded(values, level, turn):
        got = [pairwise(v, order[level], turn) for v, order in zip(values, REDUCE)]
        return [after([g], *values)[0] for g in got]

    sides = [n.index(order[0]) for n, order in zip(names, REDUCE)]
    spans = list(zip(sides, starts, sizes))
    sent = [down(*weights, d, 2, start, size, chunk) for d, start, size in spans]
    got = traded(sent, 0, 1)
    both = [down(*weights, d, 0, start, size, chunk, g) for (d, start, size), g in zip(spans, got)]
    got = traded([last for _, last in both], 0, 0)
    totals = []
    for (total, _), g, n, order, size in zip(both, got, names, REDUCE, sizes):
        n.remove(order[0])
        totals.append((total + g.astype(jnp.float32)).reshape(SIDE, SIDE, tok, size))
    for level in (1, 2):
        sides = [n.index(order[level]) for n, order in zip(names, REDUCE)]
        sent = [lax.slice_in_dim(v, 2, 4, axis=d).astype(jnp.bfloat16) for v, d in zip(totals, sides)]
        got = traded(sent, level, 1)
        totals = [
            lax.slice_in_dim(v, 0, 2, axis=d) + g.astype(jnp.float32)
            for v, g, d in zip(totals, got, sides)
        ]
        sent = [lax.index_in_dim(v, 1, d, False).astype(jnp.bfloat16) for v, d in zip(totals, sides)]
        got = traded(sent, level, 0)
        totals = [
            lax.index_in_dim(v, 0, d, False) + g.astype(jnp.float32)
            for v, g, d in zip(totals, got, sides)
        ]
        for n, order in zip(names, REDUCE):
            n.remove(order[level])
    moe_output = jnp.concatenate([v.astype(jnp.bfloat16) for v in totals], axis=-1)
    counted = count[:, :128] + swap(count[:, 128:])
    mean_count = float(tok * lax.axis_size("x") * top_k)
    expert_load = counted[0, :1] / mean_count
    return moe_output, expert_load


def solution(mesh):
    finer = Mesh(mesh.devices.reshape(SIDE, SIDE, 2, SIDE), EP_DP)
    in_specs = (
        P(EP_DP, None),
        P(EP_DP, None),
        P(EP_DP, None),
        P(EP, None, "x"),
        P(EP, None, "x"),
        P(EP, "x", None),
    )
    out_specs = (P(EP_DP, None), P(EP))
    return jax.shard_map(
        on_device, mesh=finer, in_specs=in_specs, out_specs=out_specs, check_vma=False
    )
```

time: 308 us -> 298 us (0.968); the launches traced: 302 us -> 295 us
  matrix products: 135 us -> 0 us
  Pallas kernels: 11.9 us -> 123 us
  local copies, waits for them, and re-layouts: 6.96 us -> 14.1 us
  waiting for transfers between devices: 89.6 us -> 95.6 us
  starting transfers between devices: 49 us -> 52.9 us
    dot_general x64 -> x0, matrix products: 135 us -> none  [product(): out = jnp.dot(flat, weight, preferred_element_type=jnp.float32)]
    pallas_call x1 -> x11, Pallas kernels: 11.9 us -> 123 us  [the longest x4 80.3 us: products(): pl.pallas_call(lambda *refs: in_kernel(limits, *refs), out_shape=jax.Shap...]
    ppermute x4, waiting for transfers between devices: 0.01 us -> 13.1 us  [swap(): return lax.ppermute(v, 'c', [(0, 1), (1, 0)])]
    unnamed x15 -> x30, local copies, waits for them, and re-layouts: 1.08 us -> 10.1 us
    ppermute x39, waiting for transfers between devices: 89.6 us -> 82.5 us  [pairwise(): return lax.ppermute(v, ('c', 'x') if axis == 'x' else (axis, 'c'), pairs)]
    ppermute x39, starting transfers between devices: 48.2 us -> 52.5 us  [pairwise(): return lax.ppermute(v, ('c', 'x') if axis == 'x' else (axis, 'c'), pairs)]
  transfers between devices with their start and end apart: 43 -> 43, of which waited for: 24 -> 23; matrix products, arithmetic and copies ran while one was open for 45% -> 4% of each run, Pallas kernels for 4% -> 40%
where the time goes in v1:
time: 298 us; the launch traced here: 295 us
  Pallas kernels  123 us (41%)
  waiting for transfers between devices  95.6 us (32%)
  starting transfers between devices  52.9 us (18%)
  local copies, waits for them, and re-layouts  14.1 us (5%)
  other arithmetic  7.61 us (3%)
    ppermute x39, waiting for transfers between devices, pairwise(): return lax.ppermute(v, ('c', 'x') if axis == 'x' else (axis, 'c'), pairs)  82.5 us
    pallas_call x4, Pallas kernels, products(): pl.pallas_call(lambda *refs: in_kernel(limits, *refs), out_shape=jax.Shap...  80.3 us
    ppermute x39, starting transfers between devices, pairwise(): return lax.ppermute(v, ('c', 'x') if axis == 'x' else (axis, 'c'), pairs)  52.5 us
    pallas_call x6, Pallas kernels, down(): pl.pallas_call(lambda *refs: down_kernel(d, lo, got is not None, *refs),...  32.4 us
    ppermute x4, waiting for transfers between devices, swap(): return lax.ppermute(v, 'c', [(0, 1), (1, 0)])  13.1 us
    unnamed x30, local copies, waits for them, and re-layouts  10.1 us
    pallas_call x1, Pallas kernels, combine(): pl.pallas_call(lambda *refs: combine_kernel(start, *refs), out_shape=(row...  9.82 us
  transfers between devices with their start and end apart: 43, of which 23 were waited for; matrix products, arithmetic and copies ran while one was open for 4% of the time, Pallas kernels for 40%

profile of v1, /device:TPU:0, one launch (start us, length us, event | category | flops | bytes accessed | tf_op | source)
XLA Modules:
  0.0 295.1 jit_solution(6837450753386945397)
XLA Ops:
  0.7 12.0 %collective-permute-done.15.refs_5_ = bf16[7168,512]{1,0:T(8,128)(2,1)} collective-permute-done((bf16[7168,512]{1,0:T(8,128)(2,1)}, bf16[7168,512]{1,0:T(8,128)(2,1)}, u32[]{:S(2)}, u32[]{:S(2)}) %collective-permute-start.15) | collective-permute-done | bytes 7340064 | tf_op jit(solution)/shard_map/ppermute | solution.py:32
  15.2 1.0 concatenate.30
  16.3 2.1 collective-permute-start.2
  19.3 1.6 collective-permute-start
  20.9 1.6 collective-permute-start.1
  22.5 1.3 collective-permute-done
  23.9 1.5 collective-permute-done.1
  25.3 2.6 collective-permute-start.5
  27.9 2.1 collective-permute-start.3
  30.0 3.0 %collective-permute-start.4 = (bf16[2,16,2560]{2,1,0:T(8,128)(2,1)S(1)}, bf16[2,16,2560]{2,1,0:T(8,128)(2,1)S(1)}, u32[]{:S(2)}, u32[]{:S(2)}) collective-permute-start(bf16[2,16,2560]{2,1,0:T(8,128)(2,1)S(1)} %pad_maximum_fusion.11), channel_id=1, source_target_pairs={{0,24},{8,16},{16,8},{24,0},{4,12},{12,4},{20,28},{28,20},{1,25},{... | collective-permute-start | bytes 491528 | tf_op jit(solution)/shard_map/ppermute | solution.py:28
  33.2 1.3 collective-permute-done.3
  34.5 2.1 collective-permute-done.4
  37.6 1.0 collective-permute-start.7
  38.7 4.6 %collective-permute-done.8 = bf16[4,16,2176]{2,1,0:T(8,128)(2,1)S(1)} collective-permute-done((bf16[4,16,2176]{2,1,0:T(8,128)(2,1)S(1)}, bf16[4,16,2176]{2,1,0:T(8,128)(2,1)S(1)}, u32[]{:S(2)}, u32[]{:S(2)}) %collective-permute-start.8) | collective-permute-done | bytes 278560 | tf_op jit(solution)/shard_map/ppermute | solution.py:28
  43.3 1.1 collective-permute-done.6
  45.6 2.6 collective-permute-start.9
  49.0 6.6 %collective-permute-done.11 = bf16[2,4,16,2176]{3,2,1,0:T(8,128)(2,1)S(1)} collective-permute-done((bf16[2,4,16,2176]{3,2,1,0:T(8,128)(2,1)S(1)}, bf16[2,4,16,2176]{3,2,1,0:T(8,128)(2,1)S(1)}, u32[]{:S(2)}, u32[]{:S(2)}) %collective-permute-start.11) | collective-permute-done | bytes 557088 | tf_op jit(solution)/shard_map/ppermute | solution.py:28
  55.7 1.7 collective-permute-done.9
  57.6 2.8 collective-permute-done.10
  60.3 1.3 pad_maximum_fusion.1.refs_1_
  61.6 1.4 collective-permute-start.13
  63.0 1.2 collective-permute-start.14
  64.2 20.2 %products.4.refs_0_ = bf16[3,4,4,4,16,512]{5,4,3,2,1,0:T(8,128)(2,1)} custom-call(bf16[4,4,16,2560]{3,2,1,0:T(8,128)(2,1)} %copy-done.8, bf16[4,4,16,2560]{3,2,1,0:T(8,128)(2,1)} %pad_maximum_fusion.1.refs_1_, bf16[4,4,16,2176]{3,2,1,0:T(8,128)(2,1)} %copy-done.5, bf16[7168,512]{1,0:T(8,128)(2,1)} %bitcast.75, bf16[7168,512]{1,0:T(8,128)(2,1)} %bitcast.80, ...), custom_call_target="tpu_custom_call" | custom-call | tf_op jit(solution)/shard_map/products/pallas_call | solution.py:88
  85.0 2.1 collective-permute-start.18
  87.7 20.1 %products.5.refs_1_ = bf16[3,4,4,4,16,512]{5,4,3,2,1,0:T(8,128)(2,1)} custom-call(bf16[4,4,16,2560]{3,2,1,0:T(8,128)(2,1)} %collective-permute-done.12.refs_0_, bf16[4,4,16,2560]{3,2,1,0:T(8,128)(2,1)} %collective-permute-done.13.refs_1_, bf16[4,4,16,2176]{3,2,1,0:T(8,128)(2,1)} %copy-done.9, bf16[7168,512]{1,0:T(8,128)(2,1)} %bitcast.76, ...), custom_call_target="tpu_custom_call" | custom-call | tf_op jit(solution)/shard_map/products/pallas_call | solution.py:88
  107.8 2.6 collective-permute-start.20
  110.4 1.1 collective-permute-start.21
  111.6 2.8 collective-permute-start.22
  115.5 20.1 %products.6.refs_2_ = bf16[3,4,4,4,16,512]{5,4,3,2,1,0:T(8,128)(2,1)} custom-call(bf16[4,4,16,2560]{3,2,1,0:T(8,128)(2,1)} %copy-done.12, bf16[4,4,16,2560]{3,2,1,0:T(8,128)(2,1)} %collective-permute-done.18.refs_1_, bf16[4,4,16,2176]{3,2,1,0:T(8,128)(2,1)} %copy-done.10, bf16[7168,512]{1,0:T(8,128)(2,1)} %bitcast.77, bf16[7168,512]{1,0:T(8,128)(2,1)} %bitcast.82, ...), custom_call_target="tpu_custom_call" | custom-call | tf_op jit(solution)/shard_map/products/pallas_call | solution.py:88
  135.6 1.0 copy-done.11
  136.5 20.0 %products.7.refs_3_ = bf16[3,4,4,4,16,512]{5,4,3,2,1,0:T(8,128)(2,1)} custom-call(bf16[4,4,16,2560]{3,2,1,0:T(8,128)(2,1)} %collective-permute-done.20.refs_0_, bf16[4,4,16,2560]{3,2,1,0:T(8,128)(2,1)} %collective-permute-done.21.refs_1_, bf16[4,4,16,2176]{3,2,1,0:T(8,128)(2,1)} %copy-done.11, bf16[7168,512]{1,0:T(8,128)(2,1)} %bitcast.78, ...), custom_call_target="tpu_custom_call" | custom-call | tf_op jit(solution)/shard_map/products/pallas_call | solution.py:88
  156.6 9.8 %combine.1 = (bf16[4,4,4,16,512]{4,3,2,1,0:T(8,128)(2,1)}, bf16[4,4,4,16,512]{4,3,2,1,0:T(8,128)(2,1)}, f32[1,256]{1,0:T(1,128)}) custom-call(bf16[3,4,4,4,16,512]{5,4,3,2,1,0:T(8,128)(2,1)} %products.4.refs_0_, bf16[3,4,4,4,16,512]{5,4,3,2,1,0:T(8,128)(2,1)} %products.5.refs_1_, bf16[3,4,4,4,16,512]{5,4,3,2,1,0:T(8,128)(2,1)} %products.6.refs_2_, ...), custom_call_target="tpu_custom_call" | custom-call | tf_op jit(solution)/shard_map/combine/pallas_call | solution.py:159
  166.4 3.1 %copy-done = bf16[1,512,7168]{2,1,0:T(8,128)(2,1)S(1)} copy-done((bf16[1,512,7168]{2,1,0:T(8,128)(2,1)S(1)}, bf16[1,512,7168]{2,1,0:T(8,128)(2,1)}, u32[]{:S(2)}) %copy-start) | copy-done | bytes 7340056
  169.5 1.2 copy-done.1
  170.7 1.2 copy-done.2
  172.0 5.5 %down.6 = bf16[2,256,2560]{2,1,0:T(8,128)(2,1)S(1)} custom-call(bf16[4,4,4,16,512]{4,3,2,1,0:T(8,128)(2,1)S(1)} %copy-done.1, bf16[4,4,4,16,512]{4,3,2,1,0:T(8,128)(2,1)S(1)} %copy-done.2, bf16[512,7168]{1,0:T(8,128)(2,1)S(1)} %bitcast.68, bf16[512,7168]{1,0:T(8,128)(2,1)} %collective-permute-done.23.refs_3_), custom_call_target="tpu_custom_call" | custom-call | tf_op jit(solution)/shard_map/down/pallas_call | solution.py:206
  177.4 1.1 collective-permute-start.24
  178.5 4.5 %down.8 = bf16[2,256,2048]{2,1,0:T(8,128)(2,1)S(1)} custom-call(bf16[4,4,4,16,512]{4,3,2,1,0:T(8,128)(2,1)S(1)} %copy-done.1, bf16[4,4,4,16,512]{4,3,2,1,0:T(8,128)(2,1)S(1)} %copy-done.2, bf16[512,7168]{1,0:T(8,128)(2,1)S(1)} %bitcast.69, bf16[512,7168]{1,0:T(8,128)(2,1)} %collective-permute-done.23.refs_3_), custom_call_target="tpu_custom_call" | custom-call | tf_op jit(solution)/shard_map/down/pallas_call | solution.py:206
  183.5 5.5 %down.7 = bf16[2,256,2560]{2,1,0:T(8,128)(2,1)S(1)} custom-call(bf16[4,4,4,16,512]{4,3,2,1,0:T(8,128)(2,1)S(1)} %copy-done.1, bf16[4,4,4,16,512]{4,3,2,1,0:T(8,128)(2,1)S(1)} %copy-done.2, bf16[512,7168]{1,0:T(8,128)(2,1)S(1)} %bitcast.70, bf16[512,7168]{1,0:T(8,128)(2,1)} %collective-permute-done.23.refs_3_), custom_call_target="tpu_custom_call" | custom-call | tf_op jit(solution)/shard_map/down/pallas_call | solution.py:206
  188.9 2.2 collective-permute-start.26
  191.1 22.2 %collective-permute-done.27.refs_4_ = bf16[2,256,2048]{2,1,0:T(8,128)(2,1)S(1)} collective-permute-done((bf16[2,256,2048]{2,1,0:T(8,128)(2,1)S(1)}, bf16[2,256,2048]{2,1,0:T(8,128)(2,1)S(1)}, u32[]{:S(2)}, u32[]{:S(2)}) %collective-permute-start.27) | collective-permute-done | bytes 2097184 | tf_op jit(solution)/shard_map/ppermute | solution.py:28
  213.3 5.3 %down.11 = (f32[256,2048]{1,0:T(8,128)S(1)}, bf16[256,2048]{1,0:T(8,128)(2,1)}) custom-call(bf16[4,4,4,16,512]{4,3,2,1,0:T(8,128)(2,1)S(1)} %copy-done.1, bf16[4,4,4,16,512]{4,3,2,1,0:T(8,128)(2,1)S(1)} %copy-done.2, bf16[512,7168]{1,0:T(8,128)(2,1)S(1)} %bitcast.71, bf16[512,7168]{1,0:T(8,128)(2,1)} %collective-permute-done.23.refs_3_, ...), custom_call_target="tpu_custom_call" | custom-call | tf_op jit(solution)/shard_map/down/pallas_call | solution.py:206
  218.6 6.0 %down.9 = (f32[256,2560]{1,0:T(8,128)S(1)}, bf16[256,2560]{1,0:T(8,128)(2,1)S(1)}) custom-call(bf16[4,4,4,16,512]{4,3,2,1,0:T(8,128)(2,1)S(1)} %copy-done.1, bf16[4,4,4,16,512]{4,3,2,1,0:T(8,128)(2,1)S(1)} %copy-done.2, bf16[512,7168]{1,0:T(8,128)(2,1)S(1)} %bitcast.72, bf16[512,7168]{1,0:T(8,128)(2,1)} %collective-permute-done.23.refs_3_, ...), custom_call_target="tpu_custom_call" | custom-call | tf_op jit(solution)/shard_map/down/pallas_call | solution.py:206
  225.1 1.1 collective-permute-done.42
  226.3 5.7 %down.10 = (f32[256,2560]{1,0:T(8,128)S(1)}, bf16[256,2560]{1,0:T(8,128)(2,1)S(1)}) custom-call(bf16[4,4,4,16,512]{4,3,2,1,0:T(8,128)(2,1)S(1)} %copy-done.1, bf16[4,4,4,16,512]{4,3,2,1,0:T(8,128)(2,1)S(1)} %copy-done.2, bf16[512,7168]{1,0:T(8,128)(2,1)S(1)} %bitcast.73, bf16[512,7168]{1,0:T(8,128)(2,1)} %collective-permute-done.23.refs_3_, ...), custom_call_target="tpu_custom_call" | custom-call | tf_op jit(solution)/shard_map/down/pallas_call | solution.py:206
  232.1 1.6 collective-permute-done.30
  233.7 1.5 convert_add_fusion.2
  235.3 2.4 collective-permute-start.33
  237.7 4.6 %collective-permute-done.25 = bf16[256,2560]{1,0:T(8,128)(2,1)S(1)} collective-permute-done((bf16[256,2560]{1,0:T(8,128)(2,1)S(1)}, bf16[256,2560]{1,0:T(8,128)(2,1)S(1)}, u32[]{:S(2)}, u32[]{:S(2)}) %collective-permute-start.25) | collective-permute-done | bytes 1310752 | tf_op jit(solution)/shard_map/ppermute | solution.py:28
  242.7 1.4 copy-done.7
  244.1 11.2 %collective-permute-done.29 = bf16[256,2560]{1,0:T(8,128)(2,1)S(1)} collective-permute-done((bf16[256,2560]{1,0:T(8,128)(2,1)S(1)}, bf16[256,2560]{1,0:T(8,128)(2,1)S(1)}, u32[]{:S(2)}, u32[]{:S(2)}) %collective-permute-start.29) | collective-permute-done | bytes 1310752 | tf_op jit(solution)/shard_map/ppermute | solution.py:28
  255.8 1.4 copy-done.6
  257.2 2.3 collective-permute-start.32
  259.8 9.2 %collective-permute-done.28 = bf16[2,4,16,2560]{3,2,1,0:T(8,128)(2,1)S(1)} collective-permute-done((bf16[2,4,16,2560]{3,2,1,0:T(8,128)(2,1)S(1)}, bf16[2,4,16,2560]{3,2,1,0:T(8,128)(2,1)S(1)}, u32[]{:S(2)}, u32[]{:S(2)}) %collective-permute-start.28) | collective-permute-done | bytes 655392 | tf_op jit(solution)/shard_map/ppermute | solution.py:28
  269.2 1.1 slice-done
  270.9 1.6 collective-permute-start.35
  272.6 2.7 collective-permute-start.39
  275.3 2.3 collective-permute-done.31
  277.7 1.5 collective-permute-done.35
  279.3 2.7 collective-permute-start.34
  282.0 2.6 collective-permute-start.38
  284.7 1.4 collective-permute-start.41
  286.2 2.4 collective-permute-done.38
  289.1 4.1 %collective-permute-done.40 = bf16[16,2560]{1,0:T(8,128)(2,1)S(1)} collective-permute-done((bf16[16,2560]{1,0:T(8,128)(2,1)S(1)}, bf16[16,2560]{1,0:T(8,128)(2,1)S(1)}, u32[]{:S(2)}, u32[]{:S(2)}) %collective-permute-start.40) | collective-permute-done | bytes 81952 | tf_op jit(solution)/shard_map/ppermute | solution.py:28
  (124 shorter events, 14.0 us)
Async XLA Ops:
  0.6 12.1 %collective-permute-start.15 = (bf16[7168,512]{1,0:T(8,128)(2,1)}, bf16[7168,512]{1,0:T(8,128)(2,1)}, u32[]{:S(2)}, u32[]{:S(2)}) collective-permute-start(bf16[7168,512]{1,0:T(8,128)(2,1)} %bitcast.74), channel_id=1, source_target_pairs={{0,4},{4,0},{1,5},{5,1},{2,6},{6,2},{3,7},{7,3},{8,12},{12,8},{9,1... | collective-permute-start | bytes 22020104 | tf_op jit(solution)/shard_map/ppermute | solution.py:32
  12.7 20.4 %collective-permute-start.16 = (bf16[7168,512]{1,0:T(8,128)(2,1)}, bf16[7168,512]{1,0:T(8,128)(2,1)}, u32[]{:S(2)}, u32[]{:S(2)}) collective-permute-start(bf16[7168,512]{1,0:T(8,128)(2,1)} %bitcast.79), channel_id=1, source_target_pairs={{0,4},{4,0},{1,5},{5,1},{2,6},{6,2},{3,7},{7,3},{8,12},{12,8},{9,1... | collective-permute-start | bytes 22020104 | tf_op jit(solution)/shard_map/ppermute | solution.py:32
  16.3 6.2 %collective-permute-start.2 = (bf16[16,2176]{1,0:T(8,128)(2,1)S(1)}, bf16[16,2176]{1,0:T(8,128)(2,1)S(1)}, u32[]{:S(2)}, u32[]{:S(2)}) collective-permute-start(bf16[16,2176]{1,0:T(8,128)(2,1)S(1)} %get-tuple-element.125), channel_id=1, source_target_pairs={{0,32},{32,0},{64,96},{96,64},{4,100},{36,68},{68,36},{100,4},{1,3... | collective-permute-start | bytes 208904 | tf_op jit(solution)/shard_map/ppermute | solution.py:28
  19.3 4.5 %collective-permute-start = (bf16[16,2560]{1,0:T(8,128)(2,1)S(1)}, bf16[16,2560]{1,0:T(8,128)(2,1)S(1)}, u32[]{:S(2)}, u32[]{:S(2)}) collective-permute-start(bf16[16,2560]{1,0:T(8,128)(2,1)S(1)} %get-tuple-element.128), channel_id=1, source_target_pairs={{0,1},{1,0},{2,3},{3,2},{4,7},{5,6},{6,5},{7,4},{8,9},{9,8},{10,11... | collective-permute-start | bytes 245768 | tf_op jit(solution)/shard_map/ppermute | solution.py:28
  20.9 4.4 %collective-permute-start.1 = (bf16[16,2560]{1,0:T(8,128)(2,1)S(1)}, bf16[16,2560]{1,0:T(8,128)(2,1)S(1)}, u32[]{:S(2)}, u32[]{:S(2)}) collective-permute-start(bf16[16,2560]{1,0:T(8,128)(2,1)S(1)} %get-tuple-element.129), channel_id=1, source_target_pairs={{0,8},{8,0},{16,24},{24,16},{4,28},{12,20},{20,12},{28,4},{1,9},{9... | collective-permute-start | bytes 245768 | tf_op jit(solution)/shard_map/ppermute | solution.py:28
  25.3 7.7 %collective-permute-start.5 = (bf16[2,16,2176]{2,1,0:T(8,128)(2,1)S(1)}, bf16[2,16,2176]{2,1,0:T(8,128)(2,1)S(1)}, u32[]{:S(2)}, u32[]{:S(2)}) collective-permute-start(bf16[2,16,2176]{2,1,0:T(8,128)(2,1)S(1)} %pad_maximum_fusion.12), channel_id=1, source_target_pairs={{0,96},{32,64},{64,32},{96,0},{4,36},{36,4},{68,100},{100,68},{1,9... | collective-permute-start | bytes 417800 | tf_op jit(solution)/shard_map/ppermute | solution.py:28
  27.9 6.5 %collective-permute-start.3 = (bf16[2,16,2560]{2,1,0:T(8,128)(2,1)S(1)}, bf16[2,16,2560]{2,1,0:T(8,128)(2,1)S(1)}, u32[]{:S(2)}, u32[]{:S(2)}) collective-permute-start(bf16[2,16,2560]{2,1,0:T(8,128)(2,1)S(1)} %pad_maximum_fusion.10), channel_id=1, source_target_pairs={{0,3},{1,2},{2,1},{3,0},{4,5},{5,4},{6,7},{7,6},{8,11},{9,10},{10,... | collective-permute-start | bytes 491528 | tf_op jit(solution)/shard_map/ppermute | solution.py:28
  30.0 6.5 %collective-permute-start.4 = (bf16[2,16,2560]{2,1,0:T(8,128)(2,1)S(1)}, bf16[2,16,2560]{2,1,0:T(8,128)(2,1)S(1)}, u32[]{:S(2)}, u32[]{:S(2)}) collective-permute-start(bf16[2,16,2560]{2,1,0:T(8,128)(2,1)S(1)} %pad_maximum_fusion.11), channel_id=1, source_target_pairs={{0,24},{8,16},{16,8},{24,0},{4,12},{12,4},{20,28},{28,20},{1,25},{... | collective-permute-start | bytes 491528 | tf_op jit(solution)/shard_map/ppermute | solution.py:28
  33.1 133.3 %collective-permute-start.23 = (bf16[512,7168]{1,0:T(8,128)(2,1)}, bf16[512,7168]{1,0:T(8,128)(2,1)}, u32[]{:S(2)}, u32[]{:S(2)}) collective-permute-start(bf16[512,7168]{1,0:T(8,128)(2,1)} %bitcast.67), channel_id=1, source_target_pairs={{0,4},{4,0},{1,5},{5,1},{2,6},{6,2},{3,7},{7,3},{8,12},{12,8},{9,1... | collective-permute-start | bytes 22020104 | tf_op jit(solution)/shard_map/ppermute | solution.py:32
  36.6 6.6 %collective-permute-start.8 = (bf16[4,16,2176]{2,1,0:T(8,128)(2,1)S(1)}, bf16[4,16,2176]{2,1,0:T(8,128)(2,1)S(1)}, u32[]{:S(2)}, u32[]{:S(2)}) collective-permute-start(bf16[4,16,2176]{2,1,0:T(8,128)(2,1)S(1)} %pad_maximum_fusion.8), channel_id=1, source_target_pairs={{0,1},{1,0},{2,3},{3,2},{4,7},{5,6},{6,5},{7,4},{8,9},{9,8},{10,11... | collective-permute-start | bytes 835592 | tf_op jit(solution)/shard_map/ppermute | solution.py:28
  37.3 7.1 %collective-permute-start.6 = (bf16[4,16,2560]{2,1,0:T(8,128)(2,1)S(1)}, bf16[4,16,2560]{2,1,0:T(8,128)(2,1)S(1)}, u32[]{:S(2)}, u32[]{:S(2)}) collective-permute-start(bf16[4,16,2560]{2,1,0:T(8,128)(2,1)S(1)} %pad_maximum_fusion.6), channel_id=1, source_target_pairs={{0,8},{8,0},{16,24},{24,16},{4,28},{12,20},{20,12},{28,4},{1,9},{9... | collective-permute-start | bytes 983048 | tf_op jit(solution)/shard_map/ppermute | solution.py:28
  37.6 7.1 %collective-permute-start.7 = (bf16[4,16,2560]{2,1,0:T(8,128)(2,1)S(1)}, bf16[4,16,2560]{2,1,0:T(8,128)(2,1)S(1)}, u32[]{:S(2)}, u32[]{:S(2)}) collective-permute-start(bf16[4,16,2560]{2,1,0:T(8,128)(2,1)S(1)} %pad_maximum_fusion.7), channel_id=1, source_target_pairs={{0,32},{32,0},{64,96},{96,64},{4,100},{36,68},{68,36},{100,4},{1,3... | collective-permute-start | bytes 983048 | tf_op jit(solution)/shard_map/ppermute | solution.py:28
  44.8 10.8 %collective-permute-start.11 = (bf16[2,4,16,2176]{3,2,1,0:T(8,128)(2,1)S(1)}, bf16[2,4,16,2176]{3,2,1,0:T(8,128)(2,1)S(1)}, u32[]{:S(2)}, u32[]{:S(2)}) collective-permute-start(bf16[2,4,16,2176]{3,2,1,0:T(8,128)(2,1)S(1)} %pad_maximum_fusion.5), channel_id=1, source_target_pairs={{0,3},{1,2},{2,1},{3,0},{4,5},{5,4},{6,7},{7,6},{8,11},{9,10},{10,... | collective-permute-start | bytes 1671176 | tf_op jit(solution)/shard_map/ppermute | solution.py:28
  45.6 11.8 %collective-permute-start.9 = (bf16[2,4,16,2560]{3,2,1,0:T(8,128)(2,1)S(1)}, bf16[2,4,16,2560]{3,2,1,0:T(8,128)(2,1)S(1)}, u32[]{:S(2)}, u32[]{:S(2)}) collective-permute-start(bf16[2,4,16,2560]{3,2,1,0:T(8,128)(2,1)S(1)} %pad_maximum_fusion.3), channel_id=1, source_target_pairs={{0,24},{8,16},{16,8},{24,0},{4,12},{12,4},{20,28},{28,20},{1,25},{... | collective-permute-start | bytes 1966088 | tf_op jit(solution)/shard_map/ppermute | solution.py:28
  48.2 12.1 %collective-permute-start.10 = (bf16[2,4,16,2560]{3,2,1,0:T(8,128)(2,1)S(1)}, bf16[2,4,16,2560]{3,2,1,0:T(8,128)(2,1)S(1)}, u32[]{:S(2)}, u32[]{:S(2)}) collective-permute-start(bf16[2,4,16,2560]{3,2,1,0:T(8,128)(2,1)S(1)} %pad_maximum_fusion.4), channel_id=1, source_target_pairs={{0,96},{32,64},{64,32},{96,0},{4,36},{36,4},{68,100},{100,68},{1,9... | collective-permute-start | bytes 1966088 | tf_op jit(solution)/shard_map/ppermute | solution.py:28
  55.7 8.5 %copy-start.5 = (bf16[4,4,16,2176]{3,2,1,0:T(8,128)(2,1)}, bf16[4,4,16,2176]{3,2,1,0:T(8,128)(2,1)S(1)}, u32[]{:S(2)}) copy-start(bf16[4,4,16,2176]{3,2,1,0:T(8,128)(2,1)S(1)} %pad_maximum_fusion.2.refs_2_.refs_4_) | copy-start | bytes 3342340
  57.5 6.7 %copy-start.8 = (bf16[4,4,16,2560]{3,2,1,0:T(8,128)(2,1)}, bf16[4,4,16,2560]{3,2,1,0:T(8,128)(2,1)S(1)}, u32[]{:S(2)}) copy-start(bf16[4,4,16,2560]{3,2,1,0:T(8,128)(2,1)S(1)} %pad_maximum_fusion.refs_0_) | copy-start | bytes 3932164
  61.6 22.8 %collective-permute-start.12 = (bf16[4,4,16,2560]{3,2,1,0:T(8,128)(2,1)S(1)}, bf16[4,4,16,2560]{3,2,1,0:T(8,128)(2,1)}, u32[]{:S(2)}, u32[]{:S(2)}) collective-permute-start(bf16[4,4,16,2560]{3,2,1,0:T(8,128)(2,1)S(1)} %pad_maximum_fusion.refs_0_), channel_id=1, source_target_pairs={{0,32},{32,0},{64,96},{96,64},{4,100},{36,68},{68,36},{100,4},{1,3... | collective-permute-start | bytes 3932168 | tf_op jit(solution)/shard_map/ppermute | solution.py:28
  61.6 22.8 %collective-permute-start.13 = (bf16[4,4,16,2560]{3,2,1,0:T(8,128)(2,1)}, bf16[4,4,16,2560]{3,2,1,0:T(8,128)(2,1)}, u32[]{:S(2)}, u32[]{:S(2)}) collective-permute-start(bf16[4,4,16,2560]{3,2,1,0:T(8,128)(2,1)} %pad_maximum_fusion.1.refs_1_), channel_id=1, source_target_pairs={{0,1},{1,0},{2,3},{3,2},{4,7},{5,6},{6,5},{7,4},{8,9},{9,8},{10,11... | collective-permute-start | bytes 3932168 | tf_op jit(solution)/shard_map/ppermute | solution.py:28
  63.0 21.4 %collective-permute-start.14 = (bf16[4,4,16,2176]{3,2,1,0:T(8,128)(2,1)S(1)}, bf16[4,4,16,2176]{3,2,1,0:T(8,128)(2,1)S(1)}, u32[]{:S(2)}, u32[]{:S(2)}) collective-permute-start(bf16[4,4,16,2176]{3,2,1,0:T(8,128)(2,1)S(1)} %pad_maximum_fusion.2.refs_2_.refs_4_), channel_id=1, source_target_pairs={{0,8},{8,0},{16,24},{24,16},{4,28},{12,20},{20,12},{28,4},{1,9},{9... | collective-permute-start | bytes 3342344 | tf_op jit(solution)/shard_map/ppermute | solution.py:28
  84.4 3.3 %copy-start.9 = (bf16[4,4,16,2176]{3,2,1,0:T(8,128)(2,1)}, bf16[4,4,16,2176]{3,2,1,0:T(8,128)(2,1)S(1)}, u32[]{:S(2)}) copy-start(bf16[4,4,16,2176]{3,2,1,0:T(8,128)(2,1)S(1)} %collective-permute-done.14.refs_2_.refs_5_) | copy-start | bytes 3342340
  84.4 23.4 %collective-permute-start.17 = (bf16[4,4,16,2560]{3,2,1,0:T(8,128)(2,1)}, bf16[4,4,16,2560]{3,2,1,0:T(8,128)(2,1)S(1)}, u32[]{:S(2)}, u32[]{:S(2)}) collective-permute-start(bf16[4,4,16,2560]{3,2,1,0:T(8,128)(2,1)} %copy-done.8), channel_id=1, source_target_pairs={{0,96},{32,64},{64,32},{96,0},{4,36},{36,4},{68,100},{100,68},{1,9... | collective-permute-start | bytes 3932168 | tf_op jit(solution)/shard_map/ppermute | solution.py:28
  85.0 22.8 %collective-permute-start.18 = (bf16[4,4,16,2560]{3,2,1,0:T(8,128)(2,1)}, bf16[4,4,16,2560]{3,2,1,0:T(8,128)(2,1)}, u32[]{:S(2)}, u32[]{:S(2)}) collective-permute-start(bf16[4,4,16,2560]{3,2,1,0:T(8,128)(2,1)} %pad_maximum_fusion.1.refs_1_), channel_id=1, source_target_pairs={{0,3},{1,2},{2,1},{3,0},{4,5},{5,4},{6,7},{7,6},{8,11},{9,10},{10,... | collective-permute-start | bytes 3932168 | tf_op jit(solution)/shard_map/ppermute | solution.py:28
  87.1 20.7 %collective-permute-start.19 = (bf16[4,4,16,2176]{3,2,1,0:T(8,128)(2,1)}, bf16[4,4,16,2176]{3,2,1,0:T(8,128)(2,1)S(1)}, u32[]{:S(2)}, u32[]{:S(2)}) collective-permute-start(bf16[4,4,16,2176]{3,2,1,0:T(8,128)(2,1)} %copy-done.5), channel_id=1, source_target_pairs={{0,24},{8,16},{16,8},{24,0},{4,12},{12,4},{20,28},{28,20},{1,25},{... | collective-permute-start | bytes 3342344 | tf_op jit(solution)/shard_map/ppermute | solution.py:28
  107.8 7.7 %copy-start.10 = (bf16[4,4,16,2176]{3,2,1,0:T(8,128)(2,1)}, bf16[4,4,16,2176]{3,2,1,0:T(8,128)(2,1)S(1)}, u32[]{:S(2)}) copy-start(bf16[4,4,16,2176]{3,2,1,0:T(8,128)(2,1)S(1)} %collective-permute-done.19.refs_2_.refs_6_) | copy-start | bytes 3342340
  107.8 2.6 copy-start.12
  107.8 27.7 %collective-permute-start.20 = (bf16[4,4,16,2560]{3,2,1,0:T(8,128)(2,1)}, bf16[4,4,16,2560]{3,2,1,0:T(8,128)(2,1)}, u32[]{:S(2)}, u32[]{:S(2)}) collective-permute-start(bf16[4,4,16,2560]{3,2,1,0:T(8,128)(2,1)} %collective-permute-done.12.refs_0_), channel_id=1, source_target_pairs={{0,96},{32,64},{64,32},{96,0},{4,36},{36,4},{68,100},{100,68},{1,9... | collective-permute-start | bytes 3932168 | tf_op jit(solution)/shard_map/ppermute | solution.py:28
  110.4 25.1 %collective-permute-start.21 = (bf16[4,4,16,2560]{3,2,1,0:T(8,128)(2,1)}, bf16[4,4,16,2560]{3,2,1,0:T(8,128)(2,1)}, u32[]{:S(2)}, u32[]{:S(2)}) collective-permute-start(bf16[4,4,16,2560]{3,2,1,0:T(8,128)(2,1)} %collective-permute-done.13.refs_1_), channel_id=1, source_target_pairs={{0,3},{1,2},{2,1},{3,0},{4,5},{5,4},{6,7},{7,6},{8,11},{9,10},{10,... | collective-permute-start | bytes 3932168 | tf_op jit(solution)/shard_map/ppermute | solution.py:28
  111.6 24.0 %collective-permute-start.22 = (bf16[4,4,16,2176]{3,2,1,0:T(8,128)(2,1)}, bf16[4,4,16,2176]{3,2,1,0:T(8,128)(2,1)S(1)}, u32[]{:S(2)}, u32[]{:S(2)}) collective-permute-start(bf16[4,4,16,2176]{3,2,1,0:T(8,128)(2,1)} %copy-done.9), channel_id=1, source_target_pairs={{0,24},{8,16},{16,8},{24,0},{4,12},{12,4},{20,28},{28,20},{1,25},{... | collective-permute-start | bytes 3342344 | tf_op jit(solution)/shard_map/ppermute | solution.py:28
  135.5 1.0 copy-start.11
  166.4 3.1 %copy-start = (bf16[1,512,7168]{2,1,0:T(8,128)(2,1)S(1)}, bf16[1,512,7168]{2,1,0:T(8,128)(2,1)}, u32[]{:S(2)}) copy-start(bf16[1,512,7168]{2,1,0:T(8,128)(2,1)} %param.11) | copy-start | bytes 22020100
  169.5 1.2 copy-start.1
  170.7 1.2 copy-start.2
  177.4 41.2 %collective-permute-start.24 = (bf16[2,256,2560]{2,1,0:T(8,128)(2,1)S(1)}, bf16[2,256,2560]{2,1,0:T(8,128)(2,1)S(1)}, u32[]{:S(2)}, u32[]{:S(2)}) collective-permute-start(bf16[2,256,2560]{2,1,0:T(8,128)(2,1)S(1)} %down.6), channel_id=1, source_target_pairs={{0,96},{32,64},{64,32},{96,0},{4,36},{36,4},{68,100},{100,68},{1,9... | collective-permute-start | bytes 7864328 | tf_op jit(solution)/shard_map/ppermute | solution.py:28
  183.0 30.3 %collective-permute-start.27 = (bf16[2,256,2048]{2,1,0:T(8,128)(2,1)S(1)}, bf16[2,256,2048]{2,1,0:T(8,128)(2,1)S(1)}, u32[]{:S(2)}, u32[]{:S(2)}) collective-permute-start(bf16[2,256,2048]{2,1,0:T(8,128)(2,1)S(1)} %down.8), channel_id=1, source_target_pairs={{0,24},{8,16},{16,8},{24,0},{4,12},{12,4},{20,28},{28,20},{1,25},{... | collective-permute-start | bytes 6291464 | tf_op jit(solution)/shard_map/ppermute | solution.py:28
  188.9 37.4 %collective-permute-start.26 = (bf16[2,256,2560]{2,1,0:T(8,128)(2,1)S(1)}, bf16[2,256,2560]{2,1,0:T(8,128)(2,1)S(1)}, u32[]{:S(2)}, u32[]{:S(2)}) collective-permute-start(bf16[2,256,2560]{2,1,0:T(8,128)(2,1)S(1)} %down.7), channel_id=1, source_target_pairs={{0,3},{1,2},{2,1},{3,0},{4,5},{5,4},{6,7},{7,6},{8,11},{9,10},{10,... | collective-permute-start | bytes 7864328 | tf_op jit(solution)/shard_map/ppermute | solution.py:28
  218.6 6.0 %copy-start.3 = (f32[256,2048]{1,0:T(8,128)}, f32[256,2048]{1,0:T(8,128)S(1)}, u32[]{:S(2)}) copy-start(f32[256,2048]{1,0:T(8,128)S(1)} %get-tuple-element.107) | copy-start | bytes 6291460
  218.6 6.5 %copy-start.13 = (f32[1,256]{1,0:T(1,128)S(1)}, f32[1,256]{1,0:T(1,128)}, u32[]{:S(2)}) copy-start(f32[1,256]{1,0:T(1,128)} %get-tuple-element.121) | copy-start | bytes 3076
  218.6 15.1 %collective-permute-start.30 = (bf16[256,2048]{1,0:T(8,128)(2,1)}, bf16[256,2048]{1,0:T(8,128)(2,1)}, u32[]{:S(2)}, u32[]{:S(2)}) collective-permute-start(bf16[256,2048]{1,0:T(8,128)(2,1)} %get-tuple-element.103), channel_id=1, source_target_pairs={{0,8},{8,0},{16,24},{24,16},{4,28},{12,20},{20,12},{28,4},{1,9},{9... | collective-permute-start | bytes 3145736 | tf_op jit(solution)/shard_map/ppermute | solution.py:28
  224.6 17.7 %collective-permute-start.25 = (bf16[256,2560]{1,0:T(8,128)(2,1)S(1)}, bf16[256,2560]{1,0:T(8,128)(2,1)S(1)}, u32[]{:S(2)}, u32[]{:S(2)}) collective-permute-start(bf16[256,2560]{1,0:T(8,128)(2,1)S(1)} %get-tuple-element.99), channel_id=1, source_target_pairs={{0,32},{32,0},{64,96},{96,64},{4,100},{36,68},{68,36},{100,4},{1,3... | collective-permute-start | bytes 3932168 | tf_op jit(solution)/shard_map/ppermute | solution.py:28
  225.1 1.1 collective-permute-start.42
  226.3 7.4 %copy-start.4 = (f32[256,2048]{1,0:T(8,128)S(1)}, f32[256,2048]{1,0:T(8,128)}, u32[]{:S(2)}) copy-start(f32[256,2048]{1,0:T(8,128)} %copy-done.3) | copy-start | bytes 6291460
  232.0 23.3 %collective-permute-start.29 = (bf16[256,2560]{1,0:T(8,128)(2,1)S(1)}, bf16[256,2560]{1,0:T(8,128)(2,1)S(1)}, u32[]{:S(2)}, u32[]{:S(2)}) collective-permute-start(bf16[256,2560]{1,0:T(8,128)(2,1)S(1)} %get-tuple-element.101), channel_id=1, source_target_pairs={{0,1},{1,0},{2,3},{3,2},{4,7},{5,6},{6,5},{7,4},{8,9},{9,8},{10,11... | collective-permute-start | bytes 3932168 | tf_op jit(solution)/shard_map/ppermute | solution.py:28
  235.3 24.2 %collective-permute-start.33 = (bf16[4,2,16,2048]{3,2,0,1:T(8,128)(2,1)S(1)}, bf16[4,2,16,2048]{3,2,0,1:T(8,128)(2,1)S(1)}, u32[]{:S(2)}, u32[]{:S(2)}) collective-permute-start(bf16[4,2,16,2048]{3,2,0,1:T(8,128)(2,1)S(1)} %copy.20), channel_id=1, source_target_pairs={{0,3},{1,2},{2,1},{3,0},{4,5},{5,4},{6,7},{7,6},{8,11},{9,10},{10,... | collective-permute-start | bytes 1572872 | tf_op jit(solution)/shard_map/ppermute | solution.py:28
  242.6 1.5 copy-start.7
  255.7 1.5 copy-start.6
  257.2 11.8 %collective-permute-start.28 = (bf16[2,4,16,2560]{3,2,1,0:T(8,128)(2,1)S(1)}, bf16[2,4,16,2560]{3,2,1,0:T(8,128)(2,1)S(1)}, u32[]{:S(2)}, u32[]{:S(2)}) collective-permute-start(bf16[2,4,16,2560]{3,2,1,0:T(8,128)(2,1)S(1)} %bitcast.91), channel_id=1, source_target_pairs={{0,24},{8,16},{16,8},{24,0},{4,12},{12,4},{20,28},{28,20},{1,25},{... | collective-permute-start | bytes 1966088 | tf_op jit(solution)/shard_map/ppermute | solution.py:28
  257.2 11.8 %slice-start.1 = ((f32[256,2560]{1,0:T(8,128)}), f32[128,2560]{1,0:T(8,128)S(1)}, s32[]{:S(2)}) async-start(f32[256,2560]{1,0:T(8,128)} %copy-done.7), calls=%async_computation.1 | async-start | bytes 2621440 | tf_op jit(solution)/shard_map/slice | solution.py:293
  257.2 12.0 %collective-permute-start.32 = (bf16[2,4,16,2560]{3,2,1,0:T(8,128)(2,1)S(1)}, bf16[2,4,16,2560]{3,2,1,0:T(8,128)(2,1)S(1)}, u32[]{:S(2)}, u32[]{:S(2)}) collective-permute-start(bf16[2,4,16,2560]{3,2,1,0:T(8,128)(2,1)S(1)} %bitcast.92), channel_id=1, source_target_pairs={{0,96},{32,64},{64,32},{96,0},{4,36},{36,4},{68,100},{100,68},{1,9... | collective-permute-start | bytes 1966088 | tf_op jit(solution)/shard_map/ppermute | solution.py:28
  259.7 12.8 %collective-permute-start.36 = (bf16[4,16,2048]{2,1,0:T(8,128)(2,1)S(1)}, bf16[4,16,2048]{2,1,0:T(8,128)(2,1)S(1)}, u32[]{:S(2)}, u32[]{:S(2)}) collective-permute-start(bf16[4,16,2048]{2,1,0:T(8,128)(2,1)S(1)} %fusion.5), channel_id=1, source_target_pairs={{0,1},{1,0},{2,3},{3,2},{4,7},{5,6},{6,5},{7,4},{8,9},{9,8},{10,11... | collective-permute-start | bytes 786440 | tf_op jit(solution)/shard_map/ppermute | solution.py:28
  269.0 1.3 slice-start
  270.5 7.2 %collective-permute-start.31 = (bf16[4,16,2560]{2,1,0:T(8,128)(2,1)S(1)}, bf16[4,16,2560]{2,1,0:T(8,128)(2,1)S(1)}, u32[]{:S(2)}, u32[]{:S(2)}) collective-permute-start(bf16[4,16,2560]{2,1,0:T(8,128)(2,1)S(1)} %fusion.3), channel_id=1, source_target_pairs={{0,8},{8,0},{16,24},{24,16},{4,28},{12,20},{20,12},{28,4},{1,9},{9... | collective-permute-start | bytes 983048 | tf_op jit(solution)/shard_map/ppermute | solution.py:28
  270.9 8.3 %collective-permute-start.35 = (bf16[4,16,2560]{2,1,0:T(8,128)(2,1)S(1)}, bf16[4,16,2560]{2,1,0:T(8,128)(2,1)S(1)}, u32[]{:S(2)}, u32[]{:S(2)}) collective-permute-start(bf16[4,16,2560]{2,1,0:T(8,128)(2,1)S(1)} %fusion.4), channel_id=1, source_target_pairs={{0,32},{32,0},{64,96},{96,64},{4,100},{36,68},{68,36},{100,4},{1,3... | collective-permute-start | bytes 983048 | tf_op jit(solution)/shard_map/ppermute | solution.py:28
  272.6 12.0 %collective-permute-start.39 = (bf16[2,16,2048]{2,1,0:T(8,128)(2,1)S(1)}, bf16[2,16,2048]{2,1,0:T(8,128)(2,1)S(1)}, u32[]{:S(2)}, u32[]{:S(2)}) collective-permute-start(bf16[2,16,2048]{2,1,0:T(8,128)(2,1)S(1)} %slice.225), channel_id=1, source_target_pairs={{0,96},{32,64},{64,32},{96,0},{4,36},{36,4},{68,100},{100,68},{1,9... | collective-permute-start | bytes 393224 | tf_op jit(solution)/shard_map/ppermute | solution.py:28
  279.3 6.8 %collective-permute-start.34 = (bf16[2,16,2560]{2,1,0:T(8,128)(2,1)S(1)}, bf16[2,16,2560]{2,1,0:T(8,128)(2,1)S(1)}, u32[]{:S(2)}, u32[]{:S(2)}) collective-permute-start(bf16[2,16,2560]{2,1,0:T(8,128)(2,1)S(1)} %slice.224), channel_id=1, source_target_pairs={{0,3},{1,2},{2,1},{3,0},{4,5},{5,4},{6,7},{7,6},{8,11},{9,10},{10,... | collective-permute-start | bytes 491528 | tf_op jit(solution)/shard_map/ppermute | solution.py:28
  282.0 6.5 %collective-permute-start.38 = (bf16[2,16,2560]{2,1,0:T(8,128)(2,1)S(1)}, bf16[2,16,2560]{2,1,0:T(8,128)(2,1)S(1)}, u32[]{:S(2)}, u32[]{:S(2)}) collective-permute-start(bf16[2,16,2560]{2,1,0:T(8,128)(2,1)S(1)} %slice.223), channel_id=1, source_target_pairs={{0,24},{8,16},{16,8},{24,0},{4,12},{12,4},{20,28},{28,20},{1,25},{... | collective-permute-start | bytes 491528 | tf_op jit(solution)/shard_map/ppermute | solution.py:28
  284.7 4.3 %collective-permute-start.41 = (bf16[16,2048]{1,0:T(8,128)(2,1)S(1)}, bf16[16,2048]{1,0:T(8,128)(2,1)S(1)}, u32[]{:S(2)}, u32[]{:S(2)}) collective-permute-start(bf16[16,2048]{1,0:T(8,128)(2,1)S(1)} %fusion.14), channel_id=1, source_target_pairs={{0,32},{32,0},{64,96},{96,64},{4,100},{36,68},{68,36},{100,4},{1,3... | collective-permute-start | bytes 196616 | tf_op jit(solution)/shard_map/ppermute | solution.py:28
  288.6 4.5 %collective-permute-start.40 = (bf16[16,2560]{1,0:T(8,128)(2,1)S(1)}, bf16[16,2560]{1,0:T(8,128)(2,1)S(1)}, u32[]{:S(2)}, u32[]{:S(2)}) collective-permute-start(bf16[16,2560]{1,0:T(8,128)(2,1)S(1)} %fusion.13), channel_id=1, source_target_pairs={{0,8},{8,0},{16,24},{24,16},{4,28},{12,20},{20,12},{28,4},{1,9},{9... | collective-permute-start | bytes 245768 | tf_op jit(solution)/shard_map/ppermute | solution.py:28
  288.7 4.5 %collective-permute-start.37 = (bf16[16,2560]{1,0:T(8,128)(2,1)S(1)}, bf16[16,2560]{1,0:T(8,128)(2,1)S(1)}, u32[]{:S(2)}, u32[]{:S(2)}) collective-permute-start(bf16[16,2560]{1,0:T(8,128)(2,1)S(1)} %fusion.12), channel_id=1, source_target_pairs={{0,1},{1,0},{2,3},{3,2},{4,7},{5,6},{6,5},{7,4},{8,9},{9,8},{10,11... | collective-permute-start | bytes 245768 | tf_op jit(solution)/shard_map/ppermute | solution.py:28

commit v2 on v1

--- a/solution.py
+++ b/solution.py
@@ -45,6 +45,7 @@
     weights = ROUTE_SCALE * affinity / jnp.sum(affinity, axis=1, keepdims=True)
     hit = routes[:, :, None] == jnp.arange(experts, dtype=jnp.int32)[None, None, :]
     mask = jnp.sum(hit.astype(jnp.float32), axis=1)
+    mask = mask + swap(mask)
     dense = jnp.sum(jnp.where(hit, weights[:, :, None], 0.0), axis=1)
     high = lax.reduce_precision(dense, 8, 7)
     rest = dense - high
@@ -53,45 +54,81 @@
     return jnp.concatenate([mask, high, mid, low], axis=1).astype(jnp.bfloat16)
 
 
-def in_kernel(limits, t0, t1, t2, w0, w1, w2, w3, out, acc):
-    j = pl.program_id(0)
-
-    @pl.when((j == 0) | (j == limits[0]) | (j == limits[1]))
-    def _():
-        acc[...] = jnp.zeros_like(acc)
-
-    flat = [t[...].reshape(acc.shape[1], t.shape[-1]) for t in (t0, t1, t2)]
-    rows = jnp.where(j < limits[0], flat[0], jnp.where(j < limits[1], flat[1], flat[2]))
-    for k, w in enumerate((w0, w1, w2, w3)):
-        acc[k] += jnp.dot(rows, w[...], preferred_element_type=jnp.float32)
-
-    @pl.when((j == limits[0] - 1) | (j == limits[1] - 1) | (j == limits[2] - 1))
-    def _():
-        out[0] = acc[...].astype(jnp.bfloat16).reshape(out.shape[1:])
-
-
-def products(blocks, weights, starts, model, chunk):
+def products_kernel(starts, sizes, *refs):
+    blocks, weights, out = refs[:3], refs[3:7], refs[7]
+    rows_buf, weight_buf, out_buf, rows_sem, weight_sem, out_sem = refs[8:]
+    size, rest = sizes[0], sizes[2]
+
+    def rows_copy(t):
+        return pltpu.make_async_copy(
+            blocks[t].at[:, :, :, : sizes[t]], rows_buf.at[t, :, :, :, : sizes[t]], rows_sem.at[t]
+        )
+
+    def full(t, k):
+        source = weights[k].at[pl.ds(pl.multiple_of(t * size, 128), size)]
+        return pltpu.make_async_copy(source, weight_buf.at[k, :size], weight_sem.at[k])
+
+    def tail(k):
+        source = weights[k].at[starts[2] : starts[2] + rest]
+        return pltpu.make_async_copy(source, weight_buf.at[k, :rest], weight_sem.at[k])
+
+    def out_copy(t, k):
+        return pltpu.make_async_copy(out_buf.at[k % 2], out.at[t, k], out_sem.at[k % 2])
+
+    def store(t, k, cols, wait):
+        rows = rows_buf[t, :, :, :, :cols].reshape(-1, cols)
+        total = jnp.dot(rows, weight_buf[k, :cols], preferred_element_type=jnp.float32)
+        wait()
+        out_buf[k % 2] = total.astype(jnp.bfloat16).reshape(out_buf.shape[1:])
+        out_copy(t, k).start()
+
+    rows_copy(0).start()
+    for k in range(3):
+        full(0, k).start()
+    rows_copy(1).start()
+    rows_copy(2).start()
+    rows_copy(0).wait()
+
+    def third(t, carry):
+        for k in range(4):
+            full(t, k).wait()
+            if k == 0:
+                full(t, 3).start()
+            else:
+                pl.when(t == 0)(full(1, k - 1).start)
+                pl.when(t == 1)(tail(k - 1).start)
+            last = out_copy(t, k).wait
+            store(t, k, size, last if k >= 2 else lambda last=last: pl.when(t > 0)(last))
+        pl.when(t == 0)(rows_copy(1).wait)
+        return carry
+
+    lax.fori_loop(0, 2, third, 0)
+    rows_copy(2).wait()
+    for k in range(4):
+        tail(k).wait()
+        if k == 0:
+            tail(3).start()
+        store(2, k, rest, out_copy(2, k).wait)
+    out_copy(2, 2).wait()
+    out_copy(2, 3).wait()
+
+
+def products(blocks, weights, starts, sizes):
     tok, width = blocks[0].shape[2], weights[0].shape[1]
-    limits = (starts[1] // chunk, starts[2] // chunk, model // chunk)
-    firsts = (0,) + limits[:2]
-    tokens = [
-        pl.BlockSpec(
-            (SIDE, SIDE, tok, chunk),
-            lambda j, lo=lo, hi=hi: (0, 0, 0, jnp.clip(j, lo, hi - 1) - lo),
-        )
-        for lo, hi in zip(firsts, limits)
-    ]
-
-    def third(j):
-        return ((j >= limits[0]).astype(jnp.int32) + (j >= limits[1]).astype(jnp.int32), 0, 0, 0, 0, 0)
-
+    longest = max(sizes)
     return pl.pallas_call(
-        lambda *refs: in_kernel(limits, *refs),
+        lambda *refs: products_kernel(starts, sizes, *refs),
         out_shape=jax.ShapeDtypeStruct((3, 4, SIDE, SIDE, tok, width), jnp.bfloat16),
-        grid=(model // chunk,),
-        in_specs=tokens + [pl.BlockSpec((chunk, width), lambda j: (j, 0))] * 4,
-        out_specs=pl.BlockSpec((1, 4, SIDE, SIDE, tok, width), third),
-        scratch_shapes=[pltpu.VMEM((4, SIDE * SIDE * tok, width), jnp.float32)],
+        in_specs=[pl.BlockSpec(memory_space=pl.ANY)] * 7,
+        out_specs=pl.BlockSpec(memory_space=pl.ANY),
+        scratch_shapes=[
+            pltpu.VMEM((3, SIDE, SIDE, tok, longest), jnp.bfloat16),
+            pltpu.VMEM((4, longest, width), jnp.bfloat16),
+            pltpu.VMEM((2, SIDE, SIDE, tok, width), jnp.bfloat16),
+            pltpu.SemaphoreType.DMA((3,)),
+            pltpu.SemaphoreType.DMA((4,)),
+            pltpu.SemaphoreType.DMA((2,)),
+        ],
         name="products",
     )(*blocks, *weights)
 
@@ -158,7 +195,7 @@
     rows = jax.ShapeDtypeStruct((SIDE, SIDE, SIDE, tok, width), jnp.bfloat16)
     return pl.pallas_call(
         lambda *refs: combine_kernel(start, *refs),
-        out_shape=(rows, rows, jax.ShapeDtypeStruct((1, 256), jnp.float32)),
+        out_shape=(rows, rows, jax.ShapeDtypeStruct((1, 128), jnp.float32)),
         in_specs=[pl.BlockSpec(memory_space=pl.ANY)] * 8 + [pl.BlockSpec(memory_space=pltpu.VMEM)],
         out_specs=(pl.BlockSpec(memory_space=pltpu.VMEM),) * 3,
         scratch_shapes=[
@@ -172,18 +209,22 @@
 
 
 def down_kernel(d, lo, added, own_ref, peer_ref, own_w, peer_w, *refs):
-    for p in range(2):
-        index = (slice(None),) * d + (lo + p,)
-        flat = own_ref[index].reshape(-1, own_ref.shape[-1])
-        total = jnp.dot(flat, own_w[...], preferred_element_type=jnp.float32)
-        flat = peer_ref[index].reshape(-1, peer_ref.shape[-1])
-        total = total + jnp.dot(flat, peer_w[...], preferred_element_type=jnp.float32)
-        if added:
-            got, outs = refs[0], refs[1:]
-            total = total + got[p].astype(jnp.float32)
-            outs[p][...] = total.astype(outs[p].dtype)
-        else:
-            refs[0][p] = total.astype(jnp.bfloat16)
+    index = (slice(None),) * d + (slice(lo, lo + 2),)
+    own = own_ref[index]
+    shape = own.shape[:-1] + own_w.shape[1:]
+    total = jnp.dot(
+        own.reshape(-1, own.shape[-1]), own_w[...], preferred_element_type=jnp.float32
+    ) + jnp.dot(
+        peer_ref[index].reshape(-1, own.shape[-1]), peer_w[...], preferred_element_type=jnp.float32
+    )
+    if added:
+        got, outs = refs[0], refs[1:]
+        total = (total + got[...].astype(jnp.float32)).reshape(shape)
+        for p, out in enumerate(outs):
+            part = total[(slice(None),) * d + (p,)]
+            out[...] = part.reshape(out.shape).astype(out.dtype)
+    else:
+        refs[0][...] = total.astype(jnp.bfloat16)
 
 
 def down(own_rows, peer_rows, own_w, peer_w, d, lo, start, size, chunk, got=None):
@@ -191,11 +232,12 @@
     count = SIDE * SIDE * tok
     whole = pl.BlockSpec(own_rows.shape, lambda j: (0,) * 5)
     weight = pl.BlockSpec((width, chunk), lambda j: (0, start // chunk + j))
-    pair = pl.BlockSpec((2, count, chunk), lambda j: (0, 0, j))
+    pair = pl.BlockSpec((2 * count, chunk), lambda j: (0, j))
     one = pl.BlockSpec((count, chunk), lambda j: (0, j))
     operands, specs = [own_rows, peer_rows, own_w, peer_w], [whole, whole, weight, weight]
+    limit = None if got is None else 24 * 1024 * 1024
     if got is None:
-        out_shape, out_specs = jax.ShapeDtypeStruct((2, count, size), jnp.bfloat16), pair
+        out_shape, out_specs = jax.ShapeDtypeStruct((2 * count, size), jnp.bfloat16), pair
     else:
         operands, specs = operands + [got], specs + [pair]
         out_shape = (
@@ -209,7 +251,7 @@
         grid=(size // chunk,),
         in_specs=specs,
         out_specs=out_specs,
-        compiler_params=pltpu.CompilerParams(vmem_limit_bytes=32 * 1024 * 1024),
+        compiler_params=pltpu.CompilerParams(vmem_limit_bytes=limit),
         name="down",
     )(*operands)
 
@@ -228,36 +270,37 @@
     expert = lax.axis_index(EP)
     gate_w, up_w, down_w = gate_weight[0], up_weight[0], down_weight[0]
 
-    gate_p = swap(gate_w)
-    up_p = swap(after([up_w], gate_p)[0])
-    down_p = swap(after([down_w], up_p)[0])
-
     chunk = min(512, model // 3 // 128 * 128)
     starts, sizes = cut(model, chunk)
     whole = jnp.concatenate([tokens, route_columns(routes, route_logits, experts)], axis=1)
     stops = starts[1:] + [model + EXTRA]
     current = [whole[:, lo:hi] for lo, hi in zip(starts, stops)]
-    for stage in range(2):
+    swapped = []
+    for stage, weight in enumerate((gate_w, up_w)):
+        weight, *current = after([weight] + current)
+        other = swap(weight)
         got = [pairwise(c, GATHER[t][stage], 0) for t, c in enumerate(current)]
         current = after([jnp.stack([c, g]) for c, g in zip(current, got)])
         got = [pairwise(c, GATHER[t][stage], 1) for t, c in enumerate(current)]
-        current = after([jnp.concatenate([c, g]) for c, g in zip(current, got)])
+        *current, other = after([jnp.concatenate([c, g]) for c, g in zip(current, got)] + [other])
+        swapped.append(other)
+    gate_p, up_p = swapped
 
     lanes = jnp.arange(EXTRA, dtype=jnp.int32)
     own, peer = lanes % experts == expert, lanes % experts == expert + 1 - 2 * lax.axis_index("c")
-    columns = [own & (lanes >= experts), peer & (lanes >= experts)]
-    columns += [own & (lanes < experts), peer & (lanes < experts)]
+    columns = [own & (lanes >= experts), peer & (lanes >= experts), own & (lanes < experts)]
     pick = jnp.concatenate(
         [jnp.broadcast_to(c[:, None], (EXTRA, 128)) for c in columns], axis=1
     ).astype(jnp.bfloat16)
 
     def part(blocks):
-        return products(blocks, (gate_w, up_w, gate_p, up_p), starts, model, chunk)
+        return products(blocks, (gate_w, up_w, gate_p, up_p), starts, sizes)
 
     def moved(blocks, turn):
         return [pairwise(b, GATHER[t][2], turn) for t, b in enumerate(blocks)]
 
     me = current
+    down_p = swap(after([down_w], *me)[0])
     first, p0 = moved(me, 0), part(me)
     first, me, p0 = split(after(first + me + [p0]))
     second, p1 = moved(me, 1), part(first)
@@ -277,7 +320,7 @@
 
     sides = [n.index(order[0]) for n, order in zip(names, REDUCE)]
     spans = list(zip(sides, starts, sizes))
-    sent = [down(*weights, d, 2, start, size, chunk) for d, start, size in spans]
+    sent = [down(*weights, d, 2, start, size, size // 2) for d, start, size in spans]
     got = traded(sent, 0, 1)
     both = [down(*weights, d, 0, start, size, chunk, g) for (d, start, size), g in zip(spans, got)]
     got = traded([last for _, last in both], 0, 0)
@@ -302,9 +345,8 @@
         for n, order in zip(names, REDUCE):
             n.remove(order[level])
     moe_output = jnp.concatenate([v.astype(jnp.bfloat16) for v in totals], axis=-1)
-    counted = count[:, :128] + swap(count[:, 128:])
     mean_count = float(tok * lax.axis_size("x") * top_k)
-    expert_load = counted[0, :1] / mean_count
+    expert_load = count[0, :1] / mean_count
     return moe_output, expert_load
 
 

time: 298 us -> 251 us (0.84)
  Pallas kernels: 123 us -> 101 us
  waiting for transfers between devices: 95.6 us -> 80.5 us
  local copies, waits for them, and re-layouts: 14.1 us -> 7.61 us
    pallas_call x4, Pallas kernels: 80.3 us -> 54.2 us  [products(): pl.pallas_call(lambda *refs: products_kernel(starts, sizes, *refs), out_s...]
    ppermute x4, waiting for transfers between devices: 13.1 us -> 0.21 us  [swap(): return lax.ppermute(v, 'c', [(0, 1), (1, 0)])]
    unnamed x30 -> x24, local copies, waits for them, and re-layouts: 10.1 us -> 4.56 us
    pallas_call x6, Pallas kernels: 32.4 us -> 37.1 us  [down(): pl.pallas_call(lambda *refs: down_kernel(d, lo, got is not None, *refs),...]
  transfers between devices with their start and end apart: 43 -> 43, of which waited for: 23 -> 30; matrix products, arithmetic and copies ran while one was open for 4% -> 2% of each run, Pallas kernels for 40% -> 38%
where the time goes in v2:
time: 251 us; the launch traced here: 249 us
  Pallas kernels  101 us (40%)
  waiting for transfers between devices  80.5 us (32%)
  starting transfers between devices  50.9 us (20%)
  local copies, waits for them, and re-layouts  7.61 us (3%)
  other arithmetic  6.46 us (3%)
    ppermute x39, waiting for transfers between devices, pairwise(): return lax.ppermute(v, ('c', 'x') if axis == 'x' else (axis, 'c'), pairs)  80.3 us
    pallas_call x4, Pallas kernels, products(): pl.pallas_call(lambda *refs: products_kernel(starts, sizes, *refs), out_s...  54.2 us
    ppermute x39, starting transfers between devices, pairwise(): return lax.ppermute(v, ('c', 'x') if axis == 'x' else (axis, 'c'), pairs)  50.4 us
    pallas_call x6, Pallas kernels, down(): pl.pallas_call(lambda *refs: down_kernel(d, lo, got is not None, *refs),...  37.1 us
    pallas_call x1, Pallas kernels, combine(): pl.pallas_call(lambda *refs: combine_kernel(start, *refs), out_shape=(row...  9.78 us
  transfers between devices with their start and end apart: 43, of which 30 were waited for; matrix products, arithmetic and copies ran while one was open for 2% of the time, Pallas kernels for 38%

profile of v2, /device:TPU:0, one launch (start us, length us, event | category | flops | bytes accessed | tf_op | source)
XLA Modules:
  0.0 248.9 jit_solution(8924974756855543652)
XLA Ops:
  2.1 0.8 copy.12
  3.1 0.9 fusion.17
  4.3 1.0 concatenate.30
  5.7 2.0 collective-permute-start.3
  7.7 1.5 collective-permute-start.1
  9.2 1.6 collective-permute-start.2
  10.8 1.3 collective-permute-done.1
  12.1 1.5 collective-permute-done.2
  13.6 2.6 %collective-permute-start.6 = (bf16[2,16,2176]{2,1,0:T(8,128)(2,1)S(1)}, bf16[2,16,2176]{2,1,0:T(8,128)(2,1)S(1)}, u32[]{:S(2)}, u32[]{:S(2)}) collective-permute-start(bf16[2,16,2176]{2,1,0:T(8,128)(2,1)S(1)} %pad_maximum_fusion.12), channel_id=1, source_target_pairs={{0,96},{32,64},{64,32},{96,0},{4,36},{36,4},{68,100},{100,68},{1,9... | collective-permute-start | bytes 417800 | tf_op jit(solution)/shard_map/ppermute | solution.py:28
  16.2 2.1 collective-permute-start.4
  18.3 3.0 %collective-permute-start.5 = (bf16[2,16,2560]{2,1,0:T(8,128)(2,1)S(1)}, bf16[2,16,2560]{2,1,0:T(8,128)(2,1)S(1)}, u32[]{:S(2)}, u32[]{:S(2)}) collective-permute-start(bf16[2,16,2560]{2,1,0:T(8,128)(2,1)S(1)} %pad_maximum_fusion.11), channel_id=1, source_target_pairs={{0,24},{8,16},{16,8},{24,0},{4,12},{12,4},{20,28},{28,20},{1,25},{... | collective-permute-start | bytes 491528 | tf_op jit(solution)/shard_map/ppermute | solution.py:28
  21.4 1.4 collective-permute-done.4
  22.8 2.1 collective-permute-done.5
  26.0 1.0 collective-permute-start.9
  27.1 4.6 %collective-permute-done.10 = bf16[4,16,2176]{2,1,0:T(8,128)(2,1)S(1)} collective-permute-done((bf16[4,16,2176]{2,1,0:T(8,128)(2,1)S(1)}, bf16[4,16,2176]{2,1,0:T(8,128)(2,1)S(1)}, u32[]{:S(2)}, u32[]{:S(2)}) %collective-permute-start.10) | collective-permute-done | bytes 278560 | tf_op jit(solution)/shard_map/ppermute | solution.py:28
  31.7 1.1 collective-permute-done.8
  33.2 0.8 collective-permute-start.13
  34.0 2.6 %collective-permute-start.11 = (bf16[2,4,16,2560]{3,2,1,0:T(8,128)(2,1)S(1)}, bf16[2,4,16,2560]{3,2,1,0:T(8,128)(2,1)S(1)}, u32[]{:S(2)}, u32[]{:S(2)}) collective-permute-start(bf16[2,4,16,2560]{3,2,1,0:T(8,128)(2,1)S(1)} %pad_maximum_fusion.3), channel_id=1, source_target_pairs={{0,24},{8,16},{16,8},{24,0},{4,12},{12,4},{20,28},{28,20},{1,25},{... | collective-permute-start | bytes 1966088 | tf_op jit(solution)/shard_map/ppermute | solution.py:28
  36.7 0.7 collective-permute-start.12
  37.4 6.6 %collective-permute-done.13 = bf16[2,4,16,2176]{3,2,1,0:T(8,128)(2,1)S(1)} collective-permute-done((bf16[2,4,16,2176]{3,2,1,0:T(8,128)(2,1)S(1)}, bf16[2,4,16,2176]{3,2,1,0:T(8,128)(2,1)S(1)}, u32[]{:S(2)}, u32[]{:S(2)}) %collective-permute-start.13) | collective-permute-done | bytes 557088 | tf_op jit(solution)/shard_map/ppermute | solution.py:28
  44.1 1.7 collective-permute-done.11
  46.0 2.5 %collective-permute-done.12 = bf16[2,4,16,2560]{3,2,1,0:T(8,128)(2,1)S(1)} collective-permute-done((bf16[2,4,16,2560]{3,2,1,0:T(8,128)(2,1)S(1)}, bf16[2,4,16,2560]{3,2,1,0:T(8,128)(2,1)S(1)}, u32[]{:S(2)}, u32[]{:S(2)}) %collective-permute-start.12) | collective-permute-done | bytes 655392 | tf_op jit(solution)/shard_map/ppermute | solution.py:28
  48.4 1.2 pad_maximum_fusion.1.refs_1_
  49.7 1.4 collective-permute-start.16
  51.1 1.3 collective-permute-start.17
  52.5 13.6 %products.4.refs_0_ = bf16[3,4,4,4,16,512]{5,4,3,2,1,0:T(8,128)(2,1)} custom-call(bf16[4,4,16,2560]{3,2,1,0:T(8,128)(2,1)} %copy-done.5, bf16[4,4,16,2560]{3,2,1,0:T(8,128)(2,1)} %pad_maximum_fusion.1.refs_1_, bf16[4,4,16,2176]{3,2,1,0:T(8,128)(2,1)} %copy-done.2, bf16[7168,512]{1,0:T(8,128)(2,1)} %bitcast.65, bf16[7168,512]{1,0:T(8,128)(2,1)} %bitcast.70, ...), custom_call_target="tpu_custom_call" | custom-call | tf_op jit(solution)/shard_map/products/pallas_call | solution.py:119
  66.6 0.8 collective-permute-done.15.refs_0_
  67.7 0.7 collective-permute-start.18
  68.4 2.6 %collective-permute-start.19 = (bf16[4,4,16,2560]{3,2,1,0:T(8,128)(2,1)}, bf16[4,4,16,2560]{3,2,1,0:T(8,128)(2,1)}, u32[]{:S(2)}, u32[]{:S(2)}) collective-permute-start(bf16[4,4,16,2560]{3,2,1,0:T(8,128)(2,1)} %pad_maximum_fusion.1.refs_1_), channel_id=1, source_target_pairs={{0,3},{1,2},{2,1},{3,0},{4,5},{5,4},{6,7},{7,6},{8,11},{9,10},{10,... | collective-permute-start | bytes 3932168 | tf_op jit(solution)/shard_map/ppermute | solution.py:28
  71.0 1.2 collective-permute-start.20
  72.2 13.5 %products.5.refs_1_ = bf16[3,4,4,4,16,512]{5,4,3,2,1,0:T(8,128)(2,1)} custom-call(bf16[4,4,16,2560]{3,2,1,0:T(8,128)(2,1)} %collective-permute-done.15.refs_0_, bf16[4,4,16,2560]{3,2,1,0:T(8,128)(2,1)} %collective-permute-done.16.refs_1_, bf16[4,4,16,2176]{3,2,1,0:T(8,128)(2,1)} %copy-done.6, bf16[7168,512]{1,0:T(8,128)(2,1)} %bitcast.66, ...), custom_call_target="tpu_custom_call" | custom-call | tf_op jit(solution)/shard_map/products/pallas_call | solution.py:119
  85.7 2.2 collective-permute-done.20.refs_2_.refs_6_
  88.0 2.6 %collective-permute-start.21 = (bf16[4,4,16,2560]{3,2,1,0:T(8,128)(2,1)}, bf16[4,4,16,2560]{3,2,1,0:T(8,128)(2,1)}, u32[]{:S(2)}, u32[]{:S(2)}) collective-permute-start(bf16[4,4,16,2560]{3,2,1,0:T(8,128)(2,1)} %collective-permute-done.15.refs_0_), channel_id=1, source_target_pairs={{0,96},{32,64},{64,32},{96,0},{4,36},{36,4},{68,100},{100,68},{1,9... | collective-permute-start | bytes 3932168 | tf_op jit(solution)/shard_map/ppermute | solution.py:28
  90.6 2.1 collective-permute-start.22
  92.7 1.2 collective-permute-start.23
  94.8 13.5 %products.6.refs_2_ = bf16[3,4,4,4,16,512]{5,4,3,2,1,0:T(8,128)(2,1)} custom-call(bf16[4,4,16,2560]{3,2,1,0:T(8,128)(2,1)} %copy-done.9, bf16[4,4,16,2560]{3,2,1,0:T(8,128)(2,1)} %collective-permute-done.19.refs_1_, bf16[4,4,16,2176]{3,2,1,0:T(8,128)(2,1)} %copy-done.7, bf16[7168,512]{1,0:T(8,128)(2,1)} %bitcast.67, bf16[7168,512]{1,0:T(8,128)(2,1)} %bitcast.72, ...), custom_call_target="tpu_custom_call" | custom-call | tf_op jit(solution)/shard_map/products/pallas_call | solution.py:119
  108.4 1.2 collective-permute-done.23.refs_2_.refs_7_
  109.7 0.9 copy-done.8
  110.6 13.5 %products.7.refs_3_ = bf16[3,4,4,4,16,512]{5,4,3,2,1,0:T(8,128)(2,1)} custom-call(bf16[4,4,16,2560]{3,2,1,0:T(8,128)(2,1)} %collective-permute-done.21.refs_0_, bf16[4,4,16,2560]{3,2,1,0:T(8,128)(2,1)} %collective-permute-done.22.refs_1_, bf16[4,4,16,2176]{3,2,1,0:T(8,128)(2,1)} %copy-done.8, bf16[7168,512]{1,0:T(8,128)(2,1)} %bitcast.68, ...), custom_call_target="tpu_custom_call" | custom-call | tf_op jit(solution)/shard_map/products/pallas_call | solution.py:119
  124.2 9.8 %combine.1 = (bf16[4,4,4,16,512]{4,3,2,1,0:T(8,128)(2,1)}, bf16[4,4,4,16,512]{4,3,2,1,0:T(8,128)(2,1)}, f32[1,128]{1,0:T(1,128)}) custom-call(bf16[3,4,4,4,16,512]{5,4,3,2,1,0:T(8,128)(2,1)} %products.4.refs_0_, bf16[3,4,4,4,16,512]{5,4,3,2,1,0:T(8,128)(2,1)} %products.5.refs_1_, bf16[3,4,4,4,16,512]{5,4,3,2,1,0:T(8,128)(2,1)} %products.6.refs_2_, ...), custom_call_target="tpu_custom_call" | custom-call | tf_op jit(solution)/shard_map/combine/pallas_call | solution.py:196
  134.0 6.5 %down.6 = bf16[512,2560]{1,0:T(8,128)(2,1)} custom-call(bf16[4,4,4,16,512]{4,3,2,1,0:T(8,128)(2,1)} %get-tuple-element.112.refs_0_, bf16[4,4,4,16,512]{4,3,2,1,0:T(8,128)(2,1)} %get-tuple-element.113.refs_1_, bf16[512,7168]{1,0:T(8,128)(2,1)} %bitcast.14.refs_2_, bf16[512,7168]{1,0:T(8,128)(2,1)} %collective-permute-done.24.refs_3_), custom_call_target="tpu_custom_call" | custom-call | tf_op jit(solution)/shard_map/down/pallas_call | solution.py:248
  141.2 5.8 %down.8 = bf16[512,2048]{1,0:T(8,128)(2,1)} custom-call(bf16[4,4,4,16,512]{4,3,2,1,0:T(8,128)(2,1)} %get-tuple-element.112.refs_0_, bf16[4,4,4,16,512]{4,3,2,1,0:T(8,128)(2,1)} %get-tuple-element.113.refs_1_, bf16[512,7168]{1,0:T(8,128)(2,1)} %bitcast.14.refs_2_, bf16[512,7168]{1,0:T(8,128)(2,1)} %collective-permute-done.24.refs_3_), custom_call_target="tpu_custom_call" | custom-call | tf_op jit(solution)/shard_map/down/pallas_call | solution.py:248
  147.0 1.2 collective-permute-start.28
  148.2 7.2 %down.7 = bf16[512,2560]{1,0:T(8,128)(2,1)} custom-call(bf16[4,4,4,16,512]{4,3,2,1,0:T(8,128)(2,1)} %get-tuple-element.112.refs_0_, bf16[4,4,4,16,512]{4,3,2,1,0:T(8,128)(2,1)} %get-tuple-element.113.refs_1_, bf16[512,7168]{1,0:T(8,128)(2,1)} %bitcast.14.refs_2_, bf16[512,7168]{1,0:T(8,128)(2,1)} %collective-permute-done.24.refs_3_), custom_call_target="tpu_custom_call" | custom-call | tf_op jit(solution)/shard_map/down/pallas_call | solution.py:248
  155.4 1.4 collective-permute-start.27
  156.8 17.8 %collective-permute-done.28.refs_4_ = bf16[512,2048]{1,0:T(8,128)(2,1)} collective-permute-done((bf16[512,2048]{1,0:T(8,128)(2,1)}, bf16[512,2048]{1,0:T(8,128)(2,1)}, u32[]{:S(2)}, u32[]{:S(2)}) %collective-permute-start.28) | collective-permute-done | bytes 2097184 | tf_op jit(solution)/shard_map/ppermute | solution.py:28
  174.6 5.2 %down.11 = (f32[256,2048]{1,0:T(8,128)S(1)}, bf16[256,2048]{1,0:T(8,128)(2,1)S(1)}) custom-call(bf16[4,4,4,16,512]{4,3,2,1,0:T(8,128)(2,1)S(1)} %copy-done, bf16[4,4,4,16,512]{4,3,2,1,0:T(8,128)(2,1)S(1)} %copy-done.1, bf16[512,7168]{1,0:T(8,128)(2,1)} %bitcast.14.refs_2_, bf16[512,7168]{1,0:T(8,128)(2,1)} %collective-permute-done.24.refs_3_, ...), custom_call_target="tpu_custom_call" | custom-call | tf_op jit(solution)/shard_map/down/pallas_call | solution.py:248
  180.2 6.5 %down.9 = (f32[256,2560]{1,0:T(8,128)S(1)}, bf16[256,2560]{1,0:T(8,128)(2,1)S(1)}) custom-call(bf16[4,4,4,16,512]{4,3,2,1,0:T(8,128)(2,1)S(1)} %copy-done, bf16[4,4,4,16,512]{4,3,2,1,0:T(8,128)(2,1)S(1)} %copy-done.1, bf16[512,7168]{1,0:T(8,128)(2,1)} %bitcast.14.refs_2_, bf16[512,7168]{1,0:T(8,128)(2,1)} %collective-permute-done.24.refs_3_, ...), custom_call_target="tpu_custom_call" | custom-call | tf_op jit(solution)/shard_map/down/pallas_call | solution.py:248
  186.9 1.6 collective-permute-done.27.refs_4_
  188.5 6.0 %down.10 = (f32[256,2560]{1,0:T(8,128)S(1)}, bf16[256,2560]{1,0:T(8,128)(2,1)S(1)}) custom-call(bf16[4,4,4,16,512]{4,3,2,1,0:T(8,128)(2,1)S(1)} %copy-done, bf16[4,4,4,16,512]{4,3,2,1,0:T(8,128)(2,1)S(1)} %copy-done.1, bf16[512,7168]{1,0:T(8,128)(2,1)} %bitcast.14.refs_2_, bf16[512,7168]{1,0:T(8,128)(2,1)} %collective-permute-done.24.refs_3_, ...), custom_call_target="tpu_custom_call" | custom-call | tf_op jit(solution)/shard_map/down/pallas_call | solution.py:248
  195.4 1.5 collective-permute-start.34
  196.9 7.4 %collective-permute-done.26 = bf16[256,2560]{1,0:T(8,128)(2,1)S(1)} collective-permute-done((bf16[256,2560]{1,0:T(8,128)(2,1)S(1)}, bf16[256,2560]{1,0:T(8,128)(2,1)S(1)}, u32[]{:S(2)}, u32[]{:S(2)}) %collective-permute-start.26) | collective-permute-done | bytes 1310752 | tf_op jit(solution)/shard_map/ppermute | solution.py:28
  204.7 1.4 copy-done.4
  206.1 6.0 %collective-permute-done.30 = bf16[256,2560]{1,0:T(8,128)(2,1)S(1)} collective-permute-done((bf16[256,2560]{1,0:T(8,128)(2,1)S(1)}, bf16[256,2560]{1,0:T(8,128)(2,1)S(1)}, u32[]{:S(2)}, u32[]{:S(2)}) %collective-permute-start.30) | collective-permute-done | bytes 1310752 | tf_op jit(solution)/shard_map/ppermute | solution.py:28
  212.6 1.4 copy-done.3
  213.9 1.9 collective-permute-start.29
  215.8 2.1 collective-permute-start.33
  218.1 8.5 %collective-permute-done.29 = bf16[2,4,16,2560]{3,2,1,0:T(8,128)(2,1)S(1)} collective-permute-done((bf16[2,4,16,2560]{3,2,1,0:T(8,128)(2,1)S(1)}, bf16[2,4,16,2560]{3,2,1,0:T(8,128)(2,1)S(1)}, u32[]{:S(2)}, u32[]{:S(2)}) %collective-permute-start.29) | collective-permute-done | bytes 655392 | tf_op jit(solution)/shard_map/ppermute | solution.py:28
  228.4 5.2 %collective-permute-start.40 = (bf16[2,16,2048]{2,1,0:T(8,128)(2,1)S(1)}, bf16[2,16,2048]{2,1,0:T(8,128)(2,1)S(1)}, u32[]{:S(2)}, u32[]{:S(2)}) collective-permute-start(bf16[2,16,2048]{2,1,0:T(8,128)(2,1)S(1)} %slice.213), channel_id=1, source_target_pairs={{0,96},{32,64},{64,32},{96,0},{4,36},{36,4},{68,100},{100,68},{1,9... | collective-permute-start | bytes 393224 | tf_op jit(solution)/shard_map/ppermute | solution.py:28
  235.4 2.1 collective-permute-start.39
  238.1 2.7 %collective-permute-done.35 = bf16[2,16,2560]{2,1,0:T(8,128)(2,1)S(1)} collective-permute-done((bf16[2,16,2560]{2,1,0:T(8,128)(2,1)S(1)}, bf16[2,16,2560]{2,1,0:T(8,128)(2,1)S(1)}, u32[]{:S(2)}, u32[]{:S(2)}) %collective-permute-start.35) | collective-permute-done | bytes 163872 | tf_op jit(solution)/shard_map/ppermute | solution.py:28
  240.9 1.5 collective-permute-done.39
  242.6 2.7 %collective-permute-done.38 = bf16[16,2560]{1,0:T(8,128)(2,1)S(1)} collective-permute-done((bf16[16,2560]{1,0:T(8,128)(2,1)S(1)}, bf16[16,2560]{1,0:T(8,128)(2,1)S(1)}, u32[]{:S(2)}, u32[]{:S(2)}) %collective-permute-start.38) | collective-permute-done | bytes 81952 | tf_op jit(solution)/shard_map/ppermute | solution.py:28
  245.4 1.6 collective-permute-done.41
  (116 shorter events, 14.5 us)
Async XLA Ops:
  3.0 1.3 collective-permute-start
  5.3 19.6 %collective-permute-start.7 = (bf16[7168,512]{1,0:T(8,128)(2,1)}, bf16[7168,512]{1,0:T(8,128)(2,1)}, u32[]{:S(2)}, u32[]{:S(2)}) collective-permute-start(bf16[7168,512]{1,0:T(8,128)(2,1)} %bitcast.64), channel_id=1, source_target_pairs={{0,4},{4,0},{1,5},{5,1},{2,6},{6,2},{3,7},{7,3},{8,12},{12,8},{9,1... | collective-permute-start | bytes 22020104 | tf_op jit(solution)/shard_map/ppermute | solution.py:32
  5.7 5.1 %collective-permute-start.3 = (bf16[16,2176]{1,0:T(8,128)(2,1)S(1)}, bf16[16,2176]{1,0:T(8,128)(2,1)S(1)}, u32[]{:S(2)}, u32[]{:S(2)}) collective-permute-start(bf16[16,2176]{1,0:T(8,128)(2,1)S(1)} %slice.134), channel_id=1, source_target_pairs={{0,32},{32,0},{64,96},{96,64},{4,100},{36,68},{68,36},{100,4},{1,3... | collective-permute-start | bytes 208904 | tf_op jit(solution)/shard_map/ppermute | solution.py:28
  7.7 4.4 %collective-permute-start.1 = (bf16[16,2560]{1,0:T(8,128)(2,1)S(1)}, bf16[16,2560]{1,0:T(8,128)(2,1)S(1)}, u32[]{:S(2)}, u32[]{:S(2)}) collective-permute-start(bf16[16,2560]{1,0:T(8,128)(2,1)S(1)} %get-tuple-element.71), channel_id=1, source_target_pairs={{0,1},{1,0},{2,3},{3,2},{4,7},{5,6},{6,5},{7,4},{8,9},{9,8},{10,11... | collective-permute-start | bytes 245768 | tf_op jit(solution)/shard_map/ppermute | solution.py:28
  9.2 4.4 %collective-permute-start.2 = (bf16[16,2560]{1,0:T(8,128)(2,1)S(1)}, bf16[16,2560]{1,0:T(8,128)(2,1)S(1)}, u32[]{:S(2)}, u32[]{:S(2)}) collective-permute-start(bf16[16,2560]{1,0:T(8,128)(2,1)S(1)} %get-tuple-element.72), channel_id=1, source_target_pairs={{0,8},{8,0},{16,24},{24,16},{4,28},{12,20},{20,12},{28,4},{1,9},{9... | collective-permute-start | bytes 245768 | tf_op jit(solution)/shard_map/ppermute | solution.py:28
  13.6 7.7 %collective-permute-start.6 = (bf16[2,16,2176]{2,1,0:T(8,128)(2,1)S(1)}, bf16[2,16,2176]{2,1,0:T(8,128)(2,1)S(1)}, u32[]{:S(2)}, u32[]{:S(2)}) collective-permute-start(bf16[2,16,2176]{2,1,0:T(8,128)(2,1)S(1)} %pad_maximum_fusion.12), channel_id=1, source_target_pairs={{0,96},{32,64},{64,32},{96,0},{4,36},{36,4},{68,100},{100,68},{1,9... | collective-permute-start | bytes 417800 | tf_op jit(solution)/shard_map/ppermute | solution.py:28
  16.2 6.5 %collective-permute-start.4 = (bf16[2,16,2560]{2,1,0:T(8,128)(2,1)S(1)}, bf16[2,16,2560]{2,1,0:T(8,128)(2,1)S(1)}, u32[]{:S(2)}, u32[]{:S(2)}) collective-permute-start(bf16[2,16,2560]{2,1,0:T(8,128)(2,1)S(1)} %pad_maximum_fusion.10), channel_id=1, source_target_pairs={{0,3},{1,2},{2,1},{3,0},{4,5},{5,4},{6,7},{7,6},{8,11},{9,10},{10,... | collective-permute-start | bytes 491528 | tf_op jit(solution)/shard_map/ppermute | solution.py:28
  18.3 6.5 %collective-permute-start.5 = (bf16[2,16,2560]{2,1,0:T(8,128)(2,1)S(1)}, bf16[2,16,2560]{2,1,0:T(8,128)(2,1)S(1)}, u32[]{:S(2)}, u32[]{:S(2)}) collective-permute-start(bf16[2,16,2560]{2,1,0:T(8,128)(2,1)S(1)} %pad_maximum_fusion.11), channel_id=1, source_target_pairs={{0,24},{8,16},{16,8},{24,0},{4,12},{12,4},{20,28},{28,20},{1,25},{... | collective-permute-start | bytes 491528 | tf_op jit(solution)/shard_map/ppermute | solution.py:28
  24.9 24.8 %collective-permute-start.14 = (bf16[7168,512]{1,0:T(8,128)(2,1)}, bf16[7168,512]{1,0:T(8,128)(2,1)}, u32[]{:S(2)}, u32[]{:S(2)}) collective-permute-start(bf16[7168,512]{1,0:T(8,128)(2,1)} %bitcast.69), channel_id=1, source_target_pairs={{0,4},{4,0},{1,5},{5,1},{2,6},{6,2},{3,7},{7,3},{8,12},{12,8},{9,1... | collective-permute-start | bytes 22020104 | tf_op jit(solution)/shard_map/ppermute | solution.py:32
  25.0 6.6 %collective-permute-start.10 = (bf16[4,16,2176]{2,1,0:T(8,128)(2,1)S(1)}, bf16[4,16,2176]{2,1,0:T(8,128)(2,1)S(1)}, u32[]{:S(2)}, u32[]{:S(2)}) collective-permute-start(bf16[4,16,2176]{2,1,0:T(8,128)(2,1)S(1)} %pad_maximum_fusion.8), channel_id=1, source_target_pairs={{0,1},{1,0},{2,3},{3,2},{4,7},{5,6},{6,5},{7,4},{8,9},{9,8},{10,11... | collective-permute-start | bytes 835592 | tf_op jit(solution)/shard_map/ppermute | solution.py:28
  25.7 7.1 %collective-permute-start.8 = (bf16[4,16,2560]{2,1,0:T(8,128)(2,1)S(1)}, bf16[4,16,2560]{2,1,0:T(8,128)(2,1)S(1)}, u32[]{:S(2)}, u32[]{:S(2)}) collective-permute-start(bf16[4,16,2560]{2,1,0:T(8,128)(2,1)S(1)} %pad_maximum_fusion.6), channel_id=1, source_target_pairs={{0,8},{8,0},{16,24},{24,16},{4,28},{12,20},{20,12},{28,4},{1,9},{9... | collective-permute-start | bytes 983048 | tf_op jit(solution)/shard_map/ppermute | solution.py:28
  26.0 7.1 %collective-permute-start.9 = (bf16[4,16,2560]{2,1,0:T(8,128)(2,1)S(1)}, bf16[4,16,2560]{2,1,0:T(8,128)(2,1)S(1)}, u32[]{:S(2)}, u32[]{:S(2)}) collective-permute-start(bf16[4,16,2560]{2,1,0:T(8,128)(2,1)S(1)} %pad_maximum_fusion.7), channel_id=1, source_target_pairs={{0,32},{32,0},{64,96},{96,64},{4,100},{36,68},{68,36},{100,4},{1,3... | collective-permute-start | bytes 983048 | tf_op jit(solution)/shard_map/ppermute | solution.py:28
  33.2 10.8 %collective-permute-start.13 = (bf16[2,4,16,2176]{3,2,1,0:T(8,128)(2,1)S(1)}, bf16[2,4,16,2176]{3,2,1,0:T(8,128)(2,1)S(1)}, u32[]{:S(2)}, u32[]{:S(2)}) collective-permute-start(bf16[2,4,16,2176]{3,2,1,0:T(8,128)(2,1)S(1)} %pad_maximum_fusion.5), channel_id=1, source_target_pairs={{0,3},{1,2},{2,1},{3,0},{4,5},{5,4},{6,7},{7,6},{8,11},{9,10},{10,... | collective-permute-start | bytes 1671176 | tf_op jit(solution)/shard_map/ppermute | solution.py:28
  34.0 11.8 %collective-permute-start.11 = (bf16[2,4,16,2560]{3,2,1,0:T(8,128)(2,1)S(1)}, bf16[2,4,16,2560]{3,2,1,0:T(8,128)(2,1)S(1)}, u32[]{:S(2)}, u32[]{:S(2)}) collective-permute-start(bf16[2,4,16,2560]{3,2,1,0:T(8,128)(2,1)S(1)} %pad_maximum_fusion.3), channel_id=1, source_target_pairs={{0,24},{8,16},{16,8},{24,0},{4,12},{12,4},{20,28},{28,20},{1,25},{... | collective-permute-start | bytes 1966088 | tf_op jit(solution)/shard_map/ppermute | solution.py:28
  36.7 11.8 %collective-permute-start.12 = (bf16[2,4,16,2560]{3,2,1,0:T(8,128)(2,1)S(1)}, bf16[2,4,16,2560]{3,2,1,0:T(8,128)(2,1)S(1)}, u32[]{:S(2)}, u32[]{:S(2)}) collective-permute-start(bf16[2,4,16,2560]{3,2,1,0:T(8,128)(2,1)S(1)} %pad_maximum_fusion.4), channel_id=1, source_target_pairs={{0,96},{32,64},{64,32},{96,0},{4,36},{36,4},{68,100},{100,68},{1,9... | collective-permute-start | bytes 1966088 | tf_op jit(solution)/shard_map/ppermute | solution.py:28
  44.1 8.3 %copy-start.2 = (bf16[4,4,16,2176]{3,2,1,0:T(8,128)(2,1)}, bf16[4,4,16,2176]{3,2,1,0:T(8,128)(2,1)S(1)}, u32[]{:S(2)}) copy-start(bf16[4,4,16,2176]{3,2,1,0:T(8,128)(2,1)S(1)} %pad_maximum_fusion.2.refs_2_.refs_4_) | copy-start | bytes 3342340
  45.9 6.5 %copy-start.5 = (bf16[4,4,16,2560]{3,2,1,0:T(8,128)(2,1)}, bf16[4,4,16,2560]{3,2,1,0:T(8,128)(2,1)S(1)}, u32[]{:S(2)}) copy-start(bf16[4,4,16,2560]{3,2,1,0:T(8,128)(2,1)S(1)} %pad_maximum_fusion.refs_0_) | copy-start | bytes 3932164
  49.7 84.2 %collective-permute-start.24 = (bf16[512,7168]{1,0:T(8,128)(2,1)}, bf16[512,7168]{1,0:T(8,128)(2,1)}, u32[]{:S(2)}, u32[]{:S(2)}) collective-permute-start(bf16[512,7168]{1,0:T(8,128)(2,1)} %bitcast.14.refs_2_), channel_id=1, source_target_pairs={{0,4},{4,0},{1,5},{5,1},{2,6},{6,2},{3,7},{7,3},{8,12},{12,8},{9,1... | collective-permute-start | bytes 22020104 | tf_op jit(solution)/shard_map/ppermute | solution.py:32
  49.7 17.7 %collective-permute-start.15 = (bf16[4,4,16,2560]{3,2,1,0:T(8,128)(2,1)S(1)}, bf16[4,4,16,2560]{3,2,1,0:T(8,128)(2,1)}, u32[]{:S(2)}, u32[]{:S(2)}) collective-permute-start(bf16[4,4,16,2560]{3,2,1,0:T(8,128)(2,1)S(1)} %pad_maximum_fusion.refs_0_), channel_id=1, source_target_pairs={{0,32},{32,0},{64,96},{96,64},{4,100},{36,68},{68,36},{100,4},{1,3... | collective-permute-start | bytes 3932168 | tf_op jit(solution)/shard_map/ppermute | solution.py:28
  49.7 18.0 %collective-permute-start.16 = (bf16[4,4,16,2560]{3,2,1,0:T(8,128)(2,1)}, bf16[4,4,16,2560]{3,2,1,0:T(8,128)(2,1)}, u32[]{:S(2)}, u32[]{:S(2)}) collective-permute-start(bf16[4,4,16,2560]{3,2,1,0:T(8,128)(2,1)} %pad_maximum_fusion.1.refs_1_), channel_id=1, source_target_pairs={{0,1},{1,0},{2,3},{3,2},{4,7},{5,6},{6,5},{7,4},{8,9},{9,8},{10,11... | collective-permute-start | bytes 3932168 | tf_op jit(solution)/shard_map/ppermute | solution.py:28
  51.1 15.5 %collective-permute-start.17 = (bf16[4,4,16,2176]{3,2,1,0:T(8,128)(2,1)S(1)}, bf16[4,4,16,2176]{3,2,1,0:T(8,128)(2,1)S(1)}, u32[]{:S(2)}, u32[]{:S(2)}) collective-permute-start(bf16[4,4,16,2176]{3,2,1,0:T(8,128)(2,1)S(1)} %pad_maximum_fusion.2.refs_2_.refs_4_), channel_id=1, source_target_pairs={{0,8},{8,0},{16,24},{24,16},{4,28},{12,20},{20,12},{28,4},{1,9},{9... | collective-permute-start | bytes 3342344 | tf_op jit(solution)/shard_map/ppermute | solution.py:28
  66.6 5.6 %copy-start.6 = (bf16[4,4,16,2176]{3,2,1,0:T(8,128)(2,1)}, bf16[4,4,16,2176]{3,2,1,0:T(8,128)(2,1)S(1)}, u32[]{:S(2)}) copy-start(bf16[4,4,16,2176]{3,2,1,0:T(8,128)(2,1)S(1)} %collective-permute-done.17.refs_2_.refs_5_) | copy-start | bytes 3342340
  67.7 20.2 %collective-permute-start.18 = (bf16[4,4,16,2560]{3,2,1,0:T(8,128)(2,1)}, bf16[4,4,16,2560]{3,2,1,0:T(8,128)(2,1)S(1)}, u32[]{:S(2)}, u32[]{:S(2)}) collective-permute-start(bf16[4,4,16,2560]{3,2,1,0:T(8,128)(2,1)} %copy-done.5), channel_id=1, source_target_pairs={{0,96},{32,64},{64,32},{96,0},{4,36},{36,4},{68,100},{100,68},{1,9... | collective-permute-start | bytes 3932168 | tf_op jit(solution)/shard_map/ppermute | solution.py:28
  68.4 19.5 %collective-permute-start.19 = (bf16[4,4,16,2560]{3,2,1,0:T(8,128)(2,1)}, bf16[4,4,16,2560]{3,2,1,0:T(8,128)(2,1)}, u32[]{:S(2)}, u32[]{:S(2)}) collective-permute-start(bf16[4,4,16,2560]{3,2,1,0:T(8,128)(2,1)} %pad_maximum_fusion.1.refs_1_), channel_id=1, source_target_pairs={{0,3},{1,2},{2,1},{3,0},{4,5},{5,4},{6,7},{7,6},{8,11},{9,10},{10,... | collective-permute-start | bytes 3932168 | tf_op jit(solution)/shard_map/ppermute | solution.py:28
  71.0 16.9 %collective-permute-start.20 = (bf16[4,4,16,2176]{3,2,1,0:T(8,128)(2,1)}, bf16[4,4,16,2176]{3,2,1,0:T(8,128)(2,1)S(1)}, u32[]{:S(2)}, u32[]{:S(2)}) collective-permute-start(bf16[4,4,16,2176]{3,2,1,0:T(8,128)(2,1)} %copy-done.2), channel_id=1, source_target_pairs={{0,24},{8,16},{16,8},{24,0},{4,12},{12,4},{20,28},{28,20},{1,25},{... | collective-permute-start | bytes 3342344 | tf_op jit(solution)/shard_map/ppermute | solution.py:28
  87.9 6.9 %copy-start.7 = (bf16[4,4,16,2176]{3,2,1,0:T(8,128)(2,1)}, bf16[4,4,16,2176]{3,2,1,0:T(8,128)(2,1)S(1)}, u32[]{:S(2)}) copy-start(bf16[4,4,16,2176]{3,2,1,0:T(8,128)(2,1)S(1)} %collective-permute-done.20.refs_2_.refs_6_) | copy-start | bytes 3342340
  87.9 2.6 %copy-start.9 = (bf16[4,4,16,2560]{3,2,1,0:T(8,128)(2,1)}, bf16[4,4,16,2560]{3,2,1,0:T(8,128)(2,1)S(1)}, u32[]{:S(2)}) copy-start(bf16[4,4,16,2560]{3,2,1,0:T(8,128)(2,1)S(1)} %collective-permute-done.18.refs_0_) | copy-start | bytes 3932164
  88.0 21.7 %collective-permute-start.21 = (bf16[4,4,16,2560]{3,2,1,0:T(8,128)(2,1)}, bf16[4,4,16,2560]{3,2,1,0:T(8,128)(2,1)}, u32[]{:S(2)}, u32[]{:S(2)}) collective-permute-start(bf16[4,4,16,2560]{3,2,1,0:T(8,128)(2,1)} %collective-permute-done.15.refs_0_), channel_id=1, source_target_pairs={{0,96},{32,64},{64,32},{96,0},{4,36},{36,4},{68,100},{100,68},{1,9... | collective-permute-start | bytes 3932168 | tf_op jit(solution)/shard_map/ppermute | solution.py:28
  90.6 19.1 %collective-permute-start.22 = (bf16[4,4,16,2560]{3,2,1,0:T(8,128)(2,1)}, bf16[4,4,16,2560]{3,2,1,0:T(8,128)(2,1)}, u32[]{:S(2)}, u32[]{:S(2)}) collective-permute-start(bf16[4,4,16,2560]{3,2,1,0:T(8,128)(2,1)} %collective-permute-done.16.refs_1_), channel_id=1, source_target_pairs={{0,3},{1,2},{2,1},{3,0},{4,5},{5,4},{6,7},{7,6},{8,11},{9,10},{10,... | collective-permute-start | bytes 3932168 | tf_op jit(solution)/shard_map/ppermute | solution.py:28
  92.7 16.9 %collective-permute-start.23 = (bf16[4,4,16,2176]{3,2,1,0:T(8,128)(2,1)}, bf16[4,4,16,2176]{3,2,1,0:T(8,128)(2,1)S(1)}, u32[]{:S(2)}, u32[]{:S(2)}) collective-permute-start(bf16[4,4,16,2176]{3,2,1,0:T(8,128)(2,1)} %copy-done.6), channel_id=1, source_target_pairs={{0,24},{8,16},{16,8},{24,0},{4,12},{12,4},{20,28},{28,20},{1,25},{... | collective-permute-start | bytes 3342344 | tf_op jit(solution)/shard_map/ppermute | solution.py:28
  109.6 1.0 copy-start.8
  140.5 39.7 %collective-permute-start.25 = (bf16[512,2560]{1,0:T(8,128)(2,1)}, bf16[512,2560]{1,0:T(8,128)(2,1)}, u32[]{:S(2)}, u32[]{:S(2)}) collective-permute-start(bf16[512,2560]{1,0:T(8,128)(2,1)} %down.6), channel_id=1, source_target_pairs={{0,96},{32,64},{64,32},{96,0},{4,36},{36,4},{68,100},{100,68},{1,9... | collective-permute-start | bytes 7864328 | tf_op jit(solution)/shard_map/ppermute | solution.py:28
  147.0 27.6 %copy-start = (bf16[4,4,4,16,512]{4,3,2,1,0:T(8,128)(2,1)S(1)}, bf16[4,4,4,16,512]{4,3,2,1,0:T(8,128)(2,1)}, u32[]{:S(2)}) copy-start(bf16[4,4,4,16,512]{4,3,2,1,0:T(8,128)(2,1)} %get-tuple-element.112.refs_0_) | copy-start | bytes 3145732
  147.0 27.6 %copy-start.1 = (bf16[4,4,4,16,512]{4,3,2,1,0:T(8,128)(2,1)S(1)}, bf16[4,4,4,16,512]{4,3,2,1,0:T(8,128)(2,1)}, u32[]{:S(2)}) copy-start(bf16[4,4,4,16,512]{4,3,2,1,0:T(8,128)(2,1)} %get-tuple-element.113.refs_1_) | copy-start | bytes 3145732
  147.0 27.6 %collective-permute-start.28 = (bf16[512,2048]{1,0:T(8,128)(2,1)}, bf16[512,2048]{1,0:T(8,128)(2,1)}, u32[]{:S(2)}, u32[]{:S(2)}) collective-permute-start(bf16[512,2048]{1,0:T(8,128)(2,1)} %down.8), channel_id=1, source_target_pairs={{0,24},{8,16},{16,8},{24,0},{4,12},{12,4},{20,28},{28,20},{1,25},{... | collective-permute-start | bytes 6291464 | tf_op jit(solution)/shard_map/ppermute | solution.py:28
  155.4 33.1 %collective-permute-start.27 = (bf16[512,2560]{1,0:T(8,128)(2,1)}, bf16[512,2560]{1,0:T(8,128)(2,1)S(1)}, u32[]{:S(2)}, u32[]{:S(2)}) collective-permute-start(bf16[512,2560]{1,0:T(8,128)(2,1)} %down.7), channel_id=1, source_target_pairs={{0,3},{1,2},{2,1},{3,0},{4,5},{5,4},{6,7},{7,6},{8,11},{9,10},{10,... | collective-permute-start | bytes 7864328 | tf_op jit(solution)/shard_map/ppermute | solution.py:28
  179.8 7.0 %copy-start.10 = (f32[1,128]{1,0:T(1,128)S(1)}, f32[1,128]{1,0:T(1,128)}, u32[]{:S(2)}) copy-start(f32[1,128]{1,0:T(1,128)} %get-tuple-element.139) | copy-start | bytes 1540
  179.8 15.1 %collective-permute-start.31 = (bf16[256,2048]{1,0:T(8,128)(2,1)S(1)}, bf16[256,2048]{1,0:T(8,128)(2,1)S(1)}, u32[]{:S(2)}, u32[]{:S(2)}) collective-permute-start(bf16[256,2048]{1,0:T(8,128)(2,1)S(1)} %get-tuple-element.121), channel_id=1, source_target_pairs={{0,8},{8,0},{16,24},{24,16},{4,28},{12,20},{20,12},{28,4},{1,9},{9... | collective-permute-start | bytes 3145736 | tf_op jit(solution)/shard_map/ppermute | solution.py:28
  186.6 17.7 %collective-permute-start.26 = (bf16[256,2560]{1,0:T(8,128)(2,1)S(1)}, bf16[256,2560]{1,0:T(8,128)(2,1)S(1)}, u32[]{:S(2)}, u32[]{:S(2)}) collective-permute-start(bf16[256,2560]{1,0:T(8,128)(2,1)S(1)} %get-tuple-element.117), channel_id=1, source_target_pairs={{0,32},{32,0},{64,96},{96,64},{4,100},{36,68},{68,36},{100,4},{1,3... | collective-permute-start | bytes 3932168 | tf_op jit(solution)/shard_map/ppermute | solution.py:28
  194.5 17.7 %collective-permute-start.30 = (bf16[256,2560]{1,0:T(8,128)(2,1)S(1)}, bf16[256,2560]{1,0:T(8,128)(2,1)S(1)}, u32[]{:S(2)}, u32[]{:S(2)}) collective-permute-start(bf16[256,2560]{1,0:T(8,128)(2,1)S(1)} %get-tuple-element.119), channel_id=1, source_target_pairs={{0,1},{1,0},{2,3},{3,2},{4,7},{5,6},{6,5},{7,4},{8,9},{9,8},{10,11... | collective-permute-start | bytes 3932168 | tf_op jit(solution)/shard_map/ppermute | solution.py:28
  195.4 22.5 %collective-permute-start.34 = (bf16[4,2,16,2048]{3,2,0,1:T(8,128)(2,1)S(1)}, bf16[4,2,16,2048]{3,2,0,1:T(8,128)(2,1)S(1)}, u32[]{:S(2)}, u32[]{:S(2)}) collective-permute-start(bf16[4,2,16,2048]{3,2,0,1:T(8,128)(2,1)S(1)} %copy.20), channel_id=1, source_target_pairs={{0,3},{1,2},{2,1},{3,0},{4,5},{5,4},{6,7},{7,6},{8,11},{9,10},{10,... | collective-permute-start | bytes 1572872 | tf_op jit(solution)/shard_map/ppermute | solution.py:28
  204.6 1.5 copy-start.4
  212.5 1.5 copy-start.3
  213.9 12.7 %collective-permute-start.29 = (bf16[2,4,16,2560]{3,2,1,0:T(8,128)(2,1)S(1)}, bf16[2,4,16,2560]{3,2,1,0:T(8,128)(2,1)S(1)}, u32[]{:S(2)}, u32[]{:S(2)}) collective-permute-start(bf16[2,4,16,2560]{3,2,1,0:T(8,128)(2,1)S(1)} %bitcast.82), channel_id=1, source_target_pairs={{0,24},{8,16},{16,8},{24,0},{4,12},{12,4},{20,28},{28,20},{1,25},{... | collective-permute-start | bytes 1966088 | tf_op jit(solution)/shard_map/ppermute | solution.py:28
  215.8 10.8 %slice-start.1 = ((f32[256,2560]{1,0:T(8,128)}), f32[128,2560]{1,0:T(8,128)S(1)}, s32[]{:S(2)}) async-start(f32[256,2560]{1,0:T(8,128)} %copy-done.4), calls=%async_computation.1 | async-start | bytes 2621440 | tf_op jit(solution)/shard_map/slice | solution.py:336
  215.8 11.8 %collective-permute-start.33 = (bf16[2,4,16,2560]{3,2,1,0:T(8,128)(2,1)S(1)}, bf16[2,4,16,2560]{3,2,1,0:T(8,128)(2,1)S(1)}, u32[]{:S(2)}, u32[]{:S(2)}) collective-permute-start(bf16[2,4,16,2560]{3,2,1,0:T(8,128)(2,1)S(1)} %bitcast.81), channel_id=1, source_target_pairs={{0,96},{32,64},{64,32},{96,0},{4,36},{36,4},{68,100},{100,68},{1,9... | collective-permute-start | bytes 1966088 | tf_op jit(solution)/shard_map/ppermute | solution.py:28
  218.0 10.3 %collective-permute-start.37 = (bf16[4,16,2048]{2,1,0:T(8,128)(2,1)S(1)}, bf16[4,16,2048]{2,1,0:T(8,128)(2,1)S(1)}, u32[]{:S(2)}, u32[]{:S(2)}) collective-permute-start(bf16[4,16,2048]{2,1,0:T(8,128)(2,1)S(1)} %fusion.5), channel_id=1, source_target_pairs={{0,1},{1,0},{2,3},{3,2},{4,7},{5,6},{6,5},{7,4},{8,9},{9,8},{10,11... | collective-permute-start | bytes 786440 | tf_op jit(solution)/shard_map/ppermute | solution.py:28
  226.6 1.3 slice-start
  226.8 7.2 %collective-permute-start.32 = (bf16[4,16,2560]{2,1,0:T(8,128)(2,1)S(1)}, bf16[4,16,2560]{2,1,0:T(8,128)(2,1)S(1)}, u32[]{:S(2)}, u32[]{:S(2)}) collective-permute-start(bf16[4,16,2560]{2,1,0:T(8,128)(2,1)S(1)} %fusion.3), channel_id=1, source_target_pairs={{0,8},{8,0},{16,24},{24,16},{4,28},{12,20},{20,12},{28,4},{1,9},{9... | collective-permute-start | bytes 983048 | tf_op jit(solution)/shard_map/ppermute | solution.py:28
  228.2 7.2 %collective-permute-start.36 = (bf16[4,16,2560]{2,1,0:T(8,128)(2,1)S(1)}, bf16[4,16,2560]{2,1,0:T(8,128)(2,1)S(1)}, u32[]{:S(2)}, u32[]{:S(2)}) collective-permute-start(bf16[4,16,2560]{2,1,0:T(8,128)(2,1)S(1)} %fusion.4), channel_id=1, source_target_pairs={{0,32},{32,0},{64,96},{96,64},{4,100},{36,68},{68,36},{100,4},{1,3... | collective-permute-start | bytes 983048 | tf_op jit(solution)/shard_map/ppermute | solution.py:28
  228.4 9.0 %collective-permute-start.40 = (bf16[2,16,2048]{2,1,0:T(8,128)(2,1)S(1)}, bf16[2,16,2048]{2,1,0:T(8,128)(2,1)S(1)}, u32[]{:S(2)}, u32[]{:S(2)}) collective-permute-start(bf16[2,16,2048]{2,1,0:T(8,128)(2,1)S(1)} %slice.213), channel_id=1, source_target_pairs={{0,96},{32,64},{64,32},{96,0},{4,36},{36,4},{68,100},{100,68},{1,9... | collective-permute-start | bytes 393224 | tf_op jit(solution)/shard_map/ppermute | solution.py:28
  234.2 6.6 %collective-permute-start.35 = (bf16[2,16,2560]{2,1,0:T(8,128)(2,1)S(1)}, bf16[2,16,2560]{2,1,0:T(8,128)(2,1)S(1)}, u32[]{:S(2)}, u32[]{:S(2)}) collective-permute-start(bf16[2,16,2560]{2,1,0:T(8,128)(2,1)S(1)} %slice.212), channel_id=1, source_target_pairs={{0,3},{1,2},{2,1},{3,0},{4,5},{5,4},{6,7},{7,6},{8,11},{9,10},{10,... | collective-permute-start | bytes 491528 | tf_op jit(solution)/shard_map/ppermute | solution.py:28
  235.4 7.0 %collective-permute-start.39 = (bf16[2,16,2560]{2,1,0:T(8,128)(2,1)S(1)}, bf16[2,16,2560]{2,1,0:T(8,128)(2,1)S(1)}, u32[]{:S(2)}, u32[]{:S(2)}) collective-permute-start(bf16[2,16,2560]{2,1,0:T(8,128)(2,1)S(1)} %slice.211), channel_id=1, source_target_pairs={{0,24},{8,16},{16,8},{24,0},{4,12},{12,4},{20,28},{28,20},{1,25},{... | collective-permute-start | bytes 491528 | tf_op jit(solution)/shard_map/ppermute | solution.py:28
  237.5 5.1 %collective-permute-start.42 = (bf16[16,2048]{1,0:T(8,128)(2,1)S(1)}, bf16[16,2048]{1,0:T(8,128)(2,1)S(1)}, u32[]{:S(2)}, u32[]{:S(2)}) collective-permute-start(bf16[16,2048]{1,0:T(8,128)(2,1)S(1)} %fusion.14), channel_id=1, source_target_pairs={{0,32},{32,0},{64,96},{96,64},{4,100},{36,68},{68,36},{100,4},{1,3... | collective-permute-start | bytes 196616 | tf_op jit(solution)/shard_map/ppermute | solution.py:28
  240.8 4.5 %collective-permute-start.38 = (bf16[16,2560]{1,0:T(8,128)(2,1)S(1)}, bf16[16,2560]{1,0:T(8,128)(2,1)S(1)}, u32[]{:S(2)}, u32[]{:S(2)}) collective-permute-start(bf16[16,2560]{1,0:T(8,128)(2,1)S(1)} %fusion.12), channel_id=1, source_target_pairs={{0,1},{1,0},{2,3},{3,2},{4,7},{5,6},{6,5},{7,4},{8,9},{9,8},{10,11... | collective-permute-start | bytes 245768 | tf_op jit(solution)/shard_map/ppermute | solution.py:28
  242.5 4.5 %collective-permute-start.41 = (bf16[16,2560]{1,0:T(8,128)(2,1)S(1)}, bf16[16,2560]{1,0:T(8,128)(2,1)S(1)}, u32[]{:S(2)}, u32[]{:S(2)}) collective-permute-start(bf16[16,2560]{1,0:T(8,128)(2,1)S(1)} %fusion.13), channel_id=1, source_target_pairs={{0,8},{8,0},{16,24},{24,16},{4,28},{12,20},{20,12},{28,4},{1,9},{9... | collective-permute-start | bytes 245768 | tf_op jit(solution)/shard_map/ppermute | solution.py:28

commit v3 on v2

--- a/solution.py
+++ b/solution.py
@@ -34,10 +34,6 @@
 
 def after(values, *others):
     return list(lax.optimization_barrier(tuple(values) + others)[: len(values)])
-
-
-def split(values):
-    return values[:3], values[3:6], values[6]
 
 
 def route_columns(routes, route_logits, experts):
@@ -61,7 +57,9 @@
 
     def rows_copy(t):
         return pltpu.make_async_copy(
-            blocks[t].at[:, :, :, : sizes[t]], rows_buf.at[t, :, :, :, : sizes[t]], rows_sem.at[t]
+            blocks[t].at[:, :, :, :, : sizes[t]],
+            rows_buf.at[t, :, :, :, :, : sizes[t]],
+            rows_sem.at[t],
         )
 
     def full(t, k):
@@ -76,7 +74,7 @@
         return pltpu.make_async_copy(out_buf.at[k % 2], out.at[t, k], out_sem.at[k % 2])
 
     def store(t, k, cols, wait):
-        rows = rows_buf[t, :, :, :, :cols].reshape(-1, cols)
+        rows = rows_buf[t, :, :, :, :, :cols].reshape(-1, cols)
         total = jnp.dot(rows, weight_buf[k, :cols], preferred_element_type=jnp.float32)
         wait()
         out_buf[k % 2] = total.astype(jnp.bfloat16).reshape(out_buf.shape[1:])
@@ -114,17 +112,17 @@
 
 
 def products(blocks, weights, starts, sizes):
-    tok, width = blocks[0].shape[2], weights[0].shape[1]
+    tok, width = blocks[0].shape[3], weights[0].shape[1]
     longest = max(sizes)
     return pl.pallas_call(
         lambda *refs: products_kernel(starts, sizes, *refs),
-        out_shape=jax.ShapeDtypeStruct((3, 4, SIDE, SIDE, tok, width), jnp.bfloat16),
+        out_shape=jax.ShapeDtypeStruct((3, 4, 2, SIDE, SIDE, tok, width), jnp.bfloat16),
         in_specs=[pl.BlockSpec(memory_space=pl.ANY)] * 7,
         out_specs=pl.BlockSpec(memory_space=pl.ANY),
         scratch_shapes=[
-            pltpu.VMEM((3, SIDE, SIDE, tok, longest), jnp.bfloat16),
+            pltpu.VMEM((3, 2, SIDE, SIDE, tok, longest), jnp.bfloat16),
             pltpu.VMEM((4, longest, width), jnp.bfloat16),
-            pltpu.VMEM((2, SIDE, SIDE, tok, width), jnp.bfloat16),
+            pltpu.VMEM((2, 2, SIDE, SIDE, tok, width), jnp.bfloat16),
             pltpu.SemaphoreType.DMA((3,)),
             pltpu.SemaphoreType.DMA((4,)),
             pltpu.SemaphoreType.DMA((2,)),
@@ -133,25 +131,100 @@
     )(*blocks, *weights)
 
 
-def combine_kernel(start, *refs):
-    parts, extras = refs[:4], refs[4:8]
-    pick_ref = refs[8]
-    own_ref, peer_ref, count_ref = refs[9:12]
-    buf, extra_buf, route_buf, sems = refs[12:]
+def down_steps(plan, lo, own_rows, peer_rows, own_w, peer_w, outs, bufs):
+    dims, sizes, chunk = plan
+    weight_buf, out_buf, weight_sem, out_sem = bufs
+    blocks = [size // chunk for size in sizes]
+    total = sum(blocks)
+
+    def fetch(c):
+        slot = c % 3
+        columns = pl.ds(pl.multiple_of(c * chunk, chunk), chunk)
+        return [
+            pltpu.make_async_copy(w.at[:, columns], weight_buf.at[slot, e], weight_sem.at[slot, e])
+            for e, w in enumerate((own_w, peer_w))
+        ]
+
+    def begin():
+        for c in range(2):
+            for copy in fetch(c):
+                copy.start()
+
+    def finish():
+        first = 0
+        for d, count, out in zip(dims, blocks, outs):
+            index = (slice(None),) * d + (slice(lo, lo + 2),)
+
+            def save(c, j, out=out):
+                columns = pl.ds(pl.multiple_of(j * chunk, chunk), chunk)
+                return pltpu.make_async_copy(
+                    out_buf.at[c % 2], out.at[:, columns], out_sem.at[c % 2]
+                )
+
+            def step(j, carry, first=first, index=index, save=save):
+                c = first + j
+                for copy in fetch(c):
+                    copy.wait()
+
+                @pl.when(c + 2 < total)
+                def _():
+                    for copy in fetch(c + 2):
+                        copy.start()
+
+                value = None
+                for e, rows in enumerate((own_rows, peer_rows)):
+                    flat = rows[index]
+                    flat = flat.reshape(-1, flat.shape[-1])
+                    term = jnp.dot(flat, weight_buf[c % 3, e], preferred_element_type=jnp.float32)
+                    value = term if value is None else value + term
+                pl.when(c >= 2)(save(c, j).wait)
+                out_buf[c % 2] = value.astype(jnp.bfloat16)
+                save(c, j).start()
+                return carry
+
+            lax.fori_loop(0, count, step, 0)
+            first += count
+        save(total - 2, blocks[-1] - 2).wait()
+        save(total - 1, blocks[-1] - 1).wait()
+
+    return begin, finish
+
+
+def down_scratch(count, width, chunk):
+    return [
+        pltpu.VMEM((3, 2, width, chunk), jnp.bfloat16),
+        pltpu.VMEM((2, count, chunk), jnp.bfloat16),
+        pltpu.SemaphoreType.DMA((3, 2)),
+        pltpu.SemaphoreType.DMA((2,)),
+    ]
+
+
+def combine_kernel(start, plan, *refs):
+    parts, extras, pick_ref = refs[:2], refs[2:4], refs[4]
+    own_w, peer_w = refs[5:7]
+    own_out, peer_out, count_ref, *sends = refs[7:13]
+    buf, extra_buf, route_buf, own_ref, peer_ref, sems, rows_sem = refs[13:20]
+    begin, finish = down_steps(plan, 2, own_ref, peer_ref, own_w, peer_w, sends, refs[20:])
 
     def copies(i, slot):
         sem = sems.at[slot]
-        out = [pltpu.make_async_copy(parts[i].at[0], buf.at[slot, :, 0], sem.at[0])]
+        out = [pltpu.make_async_copy(parts[i // 2].at[0, :, i % 2], buf.at[slot, :, 0], sem.at[0])]
         for r in range(SIDE):
             out.append(
-                pltpu.make_async_copy(parts[r].at[1, :, i], buf.at[slot, :, 1, :, r], sem.at[1 + r])
-            )
-            out.append(
-                pltpu.make_async_copy(parts[r].at[2, :, :, i], buf.at[slot, :, 2, r], sem.at[5 + r])
+                pltpu.make_async_copy(
+                    parts[r // 2].at[1, :, r % 2, i], buf.at[slot, :, 1, :, r], sem.at[1 + r]
+                )
             )
             out.append(
                 pltpu.make_async_copy(
-                    extras[r].at[:, i, :, start : start + EXTRA], extra_buf.at[slot, r], sem.at[9 + r]
+                    parts[r // 2].at[2, :, r % 2, :, i], buf.at[slot, :, 2, r], sem.at[5 + r]
+                )
+            )
+            out.append(
+                pltpu.make_async_copy(
+                    extras[r // 2].at[r % 2, :, i, :, start : start + EXTRA],
+                    extra_buf.at[slot, r],
+                    sem.at[9 + r],
                 )
             )
         return out
@@ -165,6 +238,8 @@
         if i + 1 < SIDE:
             for copy in copies(i + 1, 1 - slot):
                 copy.start()
+        else:
+            begin()
         for copy in copies(i, slot):
             copy.wait()
         extra = extra_buf[slot].reshape(SIDE * SIDE * tok, EXTRA)
@@ -188,72 +263,62 @@
             return carry
 
         lax.fori_loop(0, SIDE * SIDE, block, 0)
-
-
-def combine(parts, extras, pick, start):
+    kept = [
+        pltpu.make_async_copy(own_ref, own_out, rows_sem.at[0]),
+        pltpu.make_async_copy(peer_ref, peer_out, rows_sem.at[1]),
+    ]
+    for copy in kept:
+        copy.start()
+    finish()
+    for copy in kept:
+        copy.wait()
+
+
+def combine(parts, extras, pick, start, own_w, peer_w, plan):
     tok, width = parts[0].shape[-2:]
     rows = jax.ShapeDtypeStruct((SIDE, SIDE, SIDE, tok, width), jnp.bfloat16)
+    count = 2 * SIDE * SIDE * tok
+    anywhere = pl.BlockSpec(memory_space=pl.ANY)
+    inside = pl.BlockSpec(memory_space=pltpu.VMEM)
     return pl.pallas_call(
-        lambda *refs: combine_kernel(start, *refs),
-        out_shape=(rows, rows, jax.ShapeDtypeStruct((1, 128), jnp.float32)),
-        in_specs=[pl.BlockSpec(memory_space=pl.ANY)] * 8 + [pl.BlockSpec(memory_space=pltpu.VMEM)],
-        out_specs=(pl.BlockSpec(memory_space=pltpu.VMEM),) * 3,
+        lambda *refs: combine_kernel(start, plan, *refs),
+        out_shape=(rows, rows, jax.ShapeDtypeStruct((1, 128), jnp.float32))
+        + tuple(jax.ShapeDtypeStruct((count, size), jnp.bfloat16) for size in plan[1]),
+        in_specs=[anywhere] * 4 + [inside] + [anywhere] * 2,
+        out_specs=(anywhere, anywhere, inside) + (anywhere,) * 3,
         scratch_shapes=[
             pltpu.VMEM((2, 4, 3, SIDE, SIDE, tok, width), jnp.bfloat16),
             pltpu.VMEM((2, SIDE, SIDE, tok, EXTRA), jnp.bfloat16),
             pltpu.VMEM((SIDE, SIDE, tok, 256), jnp.float32),
+            pltpu.VMEM(rows.shape, jnp.bfloat16),
+            pltpu.VMEM(rows.shape, jnp.bfloat16),
             pltpu.SemaphoreType.DMA((2, 13)),
-        ],
+            pltpu.SemaphoreType.DMA((2,)),
+        ]
+        + down_scratch(count, width, plan[2]),
         name="combine",
-    )(*parts, *extras, pick)
-
-
-def down_kernel(d, lo, added, own_ref, peer_ref, own_w, peer_w, *refs):
-    index = (slice(None),) * d + (slice(lo, lo + 2),)
-    own = own_ref[index]
-    shape = own.shape[:-1] + own_w.shape[1:]
-    total = jnp.dot(
-        own.reshape(-1, own.shape[-1]), own_w[...], preferred_element_type=jnp.float32
-    ) + jnp.dot(
-        peer_ref[index].reshape(-1, own.shape[-1]), peer_w[...], preferred_element_type=jnp.float32
-    )
-    if added:
-        got, outs = refs[0], refs[1:]
-        total = (total + got[...].astype(jnp.float32)).reshape(shape)
-        for p, out in enumerate(outs):
-            part = total[(slice(None),) * d + (p,)]
-            out[...] = part.reshape(out.shape).astype(out.dtype)
-    else:
-        refs[0][...] = total.astype(jnp.bfloat16)
-
-
-def down(own_rows, peer_rows, own_w, peer_w, d, lo, start, size, chunk, got=None):
+    )(*parts, *extras, pick, own_w, peer_w)
+
+
+def keep_kernel(plan, own_ref, peer_ref, own_w, peer_w, *refs):
+    begin, finish = down_steps(plan, 0, own_ref, peer_ref, own_w, peer_w, refs[:3], refs[3:])
+    begin()
+    finish()
+
+
+def keep(own_rows, peer_rows, own_w, peer_w, plan):
     tok, width = own_rows.shape[-2:]
-    count = SIDE * SIDE * tok
-    whole = pl.BlockSpec(own_rows.shape, lambda j: (0,) * 5)
-    weight = pl.BlockSpec((width, chunk), lambda j: (0, start // chunk + j))
-    pair = pl.BlockSpec((2 * count, chunk), lambda j: (0, j))
-    one = pl.BlockSpec((count, chunk), lambda j: (0, j))
-    operands, specs = [own_rows, peer_rows, own_w, peer_w], [whole, whole, weight, weight]
-    limit = None if got is None else 24 * 1024 * 1024
-    if got is None:
-        out_shape, out_specs = jax.ShapeDtypeStruct((2 * count, size), jnp.bfloat16), pair
-    else:
-        operands, specs = operands + [got], specs + [pair]
-        out_shape = (
-            jax.ShapeDtypeStruct((count, size), jnp.float32),
-            jax.ShapeDtypeStruct((count, size), jnp.bfloat16),
-        )
-        out_specs = (one, one)
+    count = 2 * SIDE * SIDE * tok
+    anywhere = pl.BlockSpec(memory_space=pl.ANY)
+    inside = pl.BlockSpec(memory_space=pltpu.VMEM)
     return pl.pallas_call(
-        lambda *refs: down_kernel(d, lo, got is not None, *refs),
-        out_shape=out_shape,
-        grid=(size // chunk,),
-        in_specs=specs,
-        out_specs=out_specs,
-        compiler_params=pltpu.CompilerParams(vmem_limit_bytes=limit),
-        name="down",
-    )(*operands)
+        lambda *refs: keep_kernel(plan, *refs),
+        out_shape=tuple(jax.ShapeDtypeStruct((count, size), jnp.bfloat16) for size in plan[1]),
+        in_specs=[inside] * 2 + [anywhere] * 2,
+        out_specs=(anywhere,) * 3,
+        scratch_shapes=down_scratch(count, width, plan[2]),
+        name="keep",
+    )(own_rows, peer_rows, own_w, peer_w)
 
 
 def cut(total, chunk):
@@ -301,50 +366,58 @@
 
     me = current
     down_p = swap(after([down_w], *me)[0])
-    first, p0 = moved(me, 0), part(me)
-    first, me, p0 = split(after(first + me + [p0]))
-    second, p1 = moved(me, 1), part(first)
-    second, first, p1 = split(after(second + first + [p1]))
-    both, p2 = moved(first, 1), part(second)
-    both, second, p2 = split(after(both + second + [p2]))
-    parts = [p0, p1, p2, part(both)]
-    extras = [me[2], first[2], second[2], both[2]]
-    own_rows, peer_rows, count = combine(parts, extras, pick, model - starts[2])
-
-    weights = (own_rows, peer_rows, down_w, down_p)
-    names = [["z", "y", "x"] for _ in REDUCE]
+    near = moved(me, 0)
+    near = after([jnp.stack([m, f]) for m, f in zip(me, near)])
+    far, p0 = moved(near, 1), part(near)
+    *far, p0 = after(far + [p0])
+    p1 = part(far)
+
+    names = ["z", "y", "x"]
+    dims = tuple(names.index(order[0]) for order in REDUCE)
+    plan = (dims, tuple(sizes), chunk)
+    own_rows, peer_rows, count, *sent = combine(
+        (p0, p1), (near[2], far[2]), pick, model - starts[2], down_w, down_p, plan
+    )
 
     def traded(values, level, turn):
         got = [pairwise(v, order[level], turn) for v, order in zip(values, REDUCE)]
         return [after([g], *values)[0] for g in got]
 
-    sides = [n.index(order[0]) for n, order in zip(names, REDUCE)]
-    spans = list(zip(sides, starts, sizes))
-    sent = [down(*weights, d, 2, start, size, size // 2) for d, start, size in spans]
+    def summed(terms):
+        total = terms[0].astype(jnp.float32)
+        for term in terms[1:]:
+            total = total + term.astype(jnp.float32)
+        return total.astype(jnp.bfloat16)
+
     got = traded(sent, 0, 1)
-    both = [down(*weights, d, 0, start, size, chunk, g) for (d, start, size), g in zip(spans, got)]
-    got = traded([last for _, last in both], 0, 0)
-    totals = []
-    for (total, _), g, n, order, size in zip(both, got, names, REDUCE, sizes):
-        n.remove(order[0])
-        totals.append((total + g.astype(jnp.float32)).reshape(SIDE, SIDE, tok, size))
-    for level in (1, 2):
-        sides = [n.index(order[level]) for n, order in zip(names, REDUCE)]
-        sent = [lax.slice_in_dim(v, 2, 4, axis=d).astype(jnp.bfloat16) for v, d in zip(totals, sides)]
-        got = traded(sent, level, 1)
-        totals = [
-            lax.slice_in_dim(v, 0, 2, axis=d) + g.astype(jnp.float32)
-            for v, g, d in zip(totals, got, sides)
+    kept = keep(own_rows, peer_rows, down_w, down_p, plan)
+    terms, left = [], []
+    for k, g, d, size, order in zip(kept, got, dims, sizes, REDUCE):
+        shape = [SIDE] * d + [2] + [SIDE] * (2 - d) + [tok, size]
+        terms.append([k.reshape(shape), g.reshape(shape)])
+        left.append(list(names))
+    for level in range(3):
+        sides = [n.index(order[level]) for n, order in zip(left, REDUCE)]
+        if level:
+            sent = [
+                summed([lax.slice_in_dim(v, 2, 4, axis=d) for v in vs]) for vs, d in zip(terms, sides)
+            ]
+            got = traded(sent, level, 1)
+            terms = [
+                [lax.slice_in_dim(v, 0, 2, axis=d) for v in vs] + [g]
+                for vs, g, d in zip(terms, got, sides)
+            ]
+        sent = [
+            summed([lax.index_in_dim(v, 1, d, False) for v in vs]) for vs, d in zip(terms, sides)
         ]
-        sent = [lax.index_in_dim(v, 1, d, False).astype(jnp.bfloat16) for v, d in zip(totals, sides)]
         got = traded(sent, level, 0)
-        totals = [
-            lax.index_in_dim(v, 0, d, False) + g.astype(jnp.float32)
-            for v, g, d in zip(totals, got, sides)
+        terms = [
+            [lax.index_in_dim(v, 0, d, False) for v in vs] + [g]
+            for vs, g, d in zip(terms, got, sides)
         ]
-        for n, order in zip(names, REDUCE):
+        for n, order in zip(left, REDUCE):
             n.remove(order[level])
-    moe_output = jnp.concatenate([v.astype(jnp.bfloat16) for v in totals], axis=-1)
+    moe_output = jnp.concatenate([summed(vs) for vs in terms], axis=-1)
     mean_count = float(tok * lax.axis_size("x") * top_k)
     expert_load = count[0, :1] / mean_count
     return moe_output, expert_load

time: 251 us -> 251 us (level)
  Pallas kernels: 101 us -> 78.2 us
  waiting for transfers between devices: 80.5 us -> 96 us
  other arithmetic: 6.46 us -> 18 us
    ppermute x39 -> x36, waiting for transfers between devices: 80.3 us -> 95.8 us  [pairwise(): return lax.ppermute(v, ('c', 'x') if axis == 'x' else (axis, 'c'), pairs)]
    pallas_call x4 -> x2, Pallas kernels: 54.2 us -> 42.2 us  [products(): pl.pallas_call(lambda *refs: products_kernel(starts, sizes, *refs), out_s...]
    pallas_call x7 -> x2, Pallas kernels: 46.9 us -> 35.9 us  [the longest x1 21.5 us: combine(): pl.pallas_call(lambda *refs: combine_kernel(start, plan, *refs), out_shap...]
    convert_element_type x3 -> x17, other arithmetic: 0.05 us -> 10.3 us  [summed(): return total.astype(jnp.bfloat16)]
    another operation x2 -> x5, other arithmetic: 0.01 us -> 3.7 us  [the longest x3 3.69 us: on_device(): near = after([jnp.stack([m, f]) for m, f in zip(me, near)])]
    unnamed x24 -> x11, local copies, waits for them, and re-layouts: 4.56 us -> 1.33 us
    squeeze x0 -> x2, local copies, waits for them, and re-layouts: none -> 2.74 us  [on_device(): lax.index_in_dim(v, 0, d, False)]
    ppermute x39 -> x36, starting transfers between devices: 50.4 us -> 48.8 us  [pairwise(): return lax.ppermute(v, ('c', 'x') if axis == 'x' else (axis, 'c'), pairs)]
  transfers between devices with their start and end apart: 43 -> 40, of which waited for: 30 -> 27; matrix products, arithmetic and copies ran while one was open for 2% -> 7% of each run, Pallas kernels for 38% -> 23%
where the time goes in v3:
time: 251 us; the launch traced here: 250 us
  waiting for transfers between devices  96 us (38%)
  Pallas kernels  78.2 us (31%)
  starting transfers between devices  49.4 us (20%)
  other arithmetic  18 us (7%)
  local copies, waits for them, and re-layouts  6.37 us (3%)
    ppermute x36, waiting for transfers between devices, pairwise(): return lax.ppermute(v, ('c', 'x') if axis == 'x' else (axis, 'c'), pairs)  95.8 us
    ppermute x36, starting transfers between devices, pairwise(): return lax.ppermute(v, ('c', 'x') if axis == 'x' else (axis, 'c'), pairs)  48.8 us
    pallas_call x2, Pallas kernels, products(): pl.pallas_call(lambda *refs: products_kernel(starts, sizes, *refs), out_s...  42.2 us
    pallas_call x1, Pallas kernels, combine(): pl.pallas_call(lambda *refs: combine_kernel(start, plan, *refs), out_shap...  21.5 us
    pallas_call x1, Pallas kernels, keep(): pl.pallas_call(lambda *refs: keep_kernel(plan, *refs), out_shape=tuple((j...  14.5 us
    convert_element_type x17, other arithmetic, summed(): return total.astype(jnp.bfloat16)  10.3 us
  transfers between devices with their start and end apart: 40, of which 27 were waited for; matrix products, arithmetic and copies ran while one was open for 7% of the time, Pallas kernels for 23%

profile of v3, /device:TPU:0, one launch (start us, length us, event | category | flops | bytes accessed | tf_op | source)
XLA Modules:
  0.0 250.2 jit_solution(7499847297879381122)
XLA Ops:
  2.1 0.8 copy.18
  3.1 0.9 fusion.22
  4.3 1.0 concatenate.30
  5.7 2.0 collective-permute-start.3
  7.7 1.5 collective-permute-start.1
  9.2 1.6 collective-permute-start.2
  10.8 1.3 collective-permute-done.1
  12.1 1.5 collective-permute-done.2
  13.6 2.6 %collective-permute-start.6 = (bf16[2,16,2176]{2,1,0:T(8,128)(2,1)S(1)}, bf16[2,16,2176]{2,1,0:T(8,128)(2,1)S(1)}, u32[]{:S(2)}, u32[]{:S(2)}) collective-permute-start(bf16[2,16,2176]{2,1,0:T(8,128)(2,1)S(1)} %pad_maximum_fusion.15), channel_id=1, source_target_pairs={{0,96},{32,64},{64,32},{96,0},{4,36},{36,4},{68,100},{100,68},{1,9... | collective-permute-start | bytes 417800 | tf_op jit(solution)/shard_map/ppermute | solution.py:28
  16.2 2.1 collective-permute-start.4
  18.3 3.0 %collective-permute-start.5 = (bf16[2,16,2560]{2,1,0:T(8,128)(2,1)S(1)}, bf16[2,16,2560]{2,1,0:T(8,128)(2,1)S(1)}, u32[]{:S(2)}, u32[]{:S(2)}) collective-permute-start(bf16[2,16,2560]{2,1,0:T(8,128)(2,1)S(1)} %pad_maximum_fusion.14), channel_id=1, source_target_pairs={{0,24},{8,16},{16,8},{24,0},{4,12},{12,4},{20,28},{28,20},{1,25},{... | collective-permute-start | bytes 491528 | tf_op jit(solution)/shard_map/ppermute | solution.py:28
  21.4 1.4 collective-permute-done.4
  22.8 2.1 collective-permute-done.5
  26.0 1.0 collective-permute-start.9
  27.1 4.6 %collective-permute-done.10 = bf16[4,16,2176]{2,1,0:T(8,128)(2,1)S(1)} collective-permute-done((bf16[4,16,2176]{2,1,0:T(8,128)(2,1)S(1)}, bf16[4,16,2176]{2,1,0:T(8,128)(2,1)S(1)}, u32[]{:S(2)}, u32[]{:S(2)}) %collective-permute-start.10) | collective-permute-done | bytes 278560 | tf_op jit(solution)/shard_map/ppermute | solution.py:28
  31.7 1.1 collective-permute-done.8
  33.2 0.8 collective-permute-start.13
  34.0 2.6 %collective-permute-start.11 = (bf16[2,4,16,2560]{3,2,1,0:T(8,128)(2,1)S(1)}, bf16[2,4,16,2560]{3,2,1,0:T(8,128)(2,1)S(1)}, u32[]{:S(2)}, u32[]{:S(2)}) collective-permute-start(bf16[2,4,16,2560]{3,2,1,0:T(8,128)(2,1)S(1)} %pad_maximum_fusion.6), channel_id=1, source_target_pairs={{0,24},{8,16},{16,8},{24,0},{4,12},{12,4},{20,28},{28,20},{1,25},{... | collective-permute-start | bytes 1966088 | tf_op jit(solution)/shard_map/ppermute | solution.py:28
  37.4 6.6 %collective-permute-done.13 = bf16[2,4,16,2176]{3,2,1,0:T(8,128)(2,1)S(1)} collective-permute-done((bf16[2,4,16,2176]{3,2,1,0:T(8,128)(2,1)S(1)}, bf16[2,4,16,2176]{3,2,1,0:T(8,128)(2,1)S(1)}, u32[]{:S(2)}, u32[]{:S(2)}) %collective-permute-start.13) | collective-permute-done | bytes 557088 | tf_op jit(solution)/shard_map/ppermute | solution.py:28
  44.1 1.7 collective-permute-done.11
  45.9 2.5 %collective-permute-done.12 = bf16[2,4,16,2560]{3,2,1,0:T(8,128)(2,1)S(1)} collective-permute-done((bf16[2,4,16,2560]{3,2,1,0:T(8,128)(2,1)S(1)}, bf16[2,4,16,2560]{3,2,1,0:T(8,128)(2,1)S(1)}, u32[]{:S(2)}, u32[]{:S(2)}) %collective-permute-start.12) | collective-permute-done | bytes 655392 | tf_op jit(solution)/shard_map/ppermute | solution.py:28
  48.7 1.4 collective-permute-start.17
  50.1 1.3 collective-permute-start.16
  51.4 12.8 %collective-permute-done.17 = bf16[4,4,16,2176]{3,2,1,0:T(8,128)(2,1)S(1)} collective-permute-done((bf16[4,4,16,2176]{3,2,1,0:T(8,128)(2,1)S(1)}, bf16[4,4,16,2176]{3,2,1,0:T(8,128)(2,1)S(1)}, u32[]{:S(2)}, u32[]{:S(2)}) %collective-permute-start.17) | collective-permute-done | bytes 1114144 | tf_op jit(solution)/shard_map/ppermute | solution.py:28
  64.5 3.2 %collective-permute-done.15 = bf16[4,4,16,2560]{3,2,1,0:T(8,128)(2,1)S(1)} collective-permute-done((bf16[4,4,16,2560]{3,2,1,0:T(8,128)(2,1)S(1)}, bf16[4,4,16,2560]{3,2,1,0:T(8,128)(2,1)S(1)}, u32[]{:S(2)}, u32[]{:S(2)}) %collective-permute-start.15) | collective-permute-done | bytes 1310752 | tf_op jit(solution)/shard_map/ppermute | solution.py:28
  67.7 1.7 pad_maximum_fusion.refs_0_
  69.4 1.7 pad_maximum_fusion.1.refs_1_
  71.2 0.7 collective-permute-start.18
  71.9 2.6 %collective-permute-start.19 = (bf16[2,4,4,16,2560]{4,3,2,1,0:T(8,128)(2,1)}, bf16[2,4,4,16,2560]{4,3,2,1,0:T(8,128)(2,1)}, u32[]{:S(2)}, u32[]{:S(2)}) collective-permute-start(bf16[2,4,4,16,2560]{4,3,2,1,0:T(8,128)(2,1)} %pad_maximum_fusion.1.refs_1_), channel_id=1, source_target_pairs={{0,3},{1,2},{2,1},{3,0},{4,5},{5,4},{6,7},{7,6},{8,11},{9,10},{10,... | collective-permute-start | bytes 7864328 | tf_op jit(solution)/shard_map/ppermute | solution.py:28
  76.0 21.1 %products.2.refs_0_ = bf16[3,4,2,4,4,16,512]{6,5,4,3,2,1,0:T(8,128)(2,1)} custom-call(bf16[2,4,4,16,2560]{4,3,2,1,0:T(8,128)(2,1)} %pad_maximum_fusion.refs_0_, bf16[2,4,4,16,2560]{4,3,2,1,0:T(8,128)(2,1)} %pad_maximum_fusion.1.refs_1_, bf16[2,4,4,16,2176]{4,3,2,1,0:T(8,128)(2,1)} %copy-done, bf16[7168,512]{1,0:T(8,128)(2,1)} %bitcast.158, ...), custom_call_target="tpu_custom_call" | custom-call | tf_op jit(solution)/shard_map/products/pallas_call | solution.py:117
  97.1 6.1 %collective-permute-done.20.refs_2_.refs_3_ = bf16[2,4,4,16,2176]{4,3,2,1,0:T(8,128)(2,1)} collective-permute-done((bf16[2,4,4,16,2176]{4,3,2,1,0:T(8,128)(2,1)S(1)}, bf16[2,4,4,16,2176]{4,3,2,1,0:T(8,128)(2,1)}, u32[]{:S(2)}, u32[]{:S(2)}) %collective-permute-start.20) | collective-permute-done | bytes 2228256 | tf_op jit(solution)/shard_map/ppermute | solution.py:28
  103.2 1.1 collective-permute-done.18.refs_0_
  104.3 0.7 collective-permute-done.19.refs_1_
  105.1 21.1 %products.3.refs_1_ = bf16[3,4,2,4,4,16,512]{6,5,4,3,2,1,0:T(8,128)(2,1)} custom-call(bf16[2,4,4,16,2560]{4,3,2,1,0:T(8,128)(2,1)} %collective-permute-done.18.refs_0_, bf16[2,4,4,16,2560]{4,3,2,1,0:T(8,128)(2,1)} %collective-permute-done.19.refs_1_, bf16[2,4,4,16,2176]{4,3,2,1,0:T(8,128)(2,1)} %collective-permute-done.20.refs_2_.refs_3_, ...), custom_call_target="tpu_custom_call" | custom-call | tf_op jit(solution)/shard_map/products/pallas_call | solution.py:117
  126.2 21.5 %combine.1 = (bf16[4,4,4,16,512]{4,3,2,1,0:T(8,128)(2,1)}, bf16[4,4,4,16,512]{4,3,2,1,0:T(8,128)(2,1)}, f32[1,128]{1,0:T(1,128)}, bf16[512,2560]{1,0:T(8,128)(2,...) custom-call(bf16[3,4,2,4,4,16,512]{6,5,4,3,2,1,0:T(8,128)(2,1)} %products.2.refs_0_, ...), custom_call_target="tpu_custom_call" | custom-call | tf_op jit(solution)/shard_map/combine/pallas_call | solution.py:283
  148.4 2.5 %collective-permute-start.22 = (bf16[512,2560]{1,0:T(8,128)(2,1)}, bf16[512,2560]{1,0:T(8,128)(2,1)S(1)}, u32[]{:S(2)}, u32[]{:S(2)}) collective-permute-start(bf16[512,2560]{1,0:T(8,128)(2,1)} %get-tuple-element.92), channel_id=1, source_target_pairs={{0,96},{32,64},{64,32},{96,0},{4,36},{36,4},{68,100},{100,68},{1,9... | collective-permute-start | bytes 7864328 | tf_op jit(solution)/shard_map/ppermute | solution.py:28
  150.9 2.6 %collective-permute-start.24 = (bf16[512,2560]{1,0:T(8,128)(2,1)}, bf16[512,2560]{1,0:T(8,128)(2,1)}, u32[]{:S(2)}, u32[]{:S(2)}) collective-permute-start(bf16[512,2560]{1,0:T(8,128)(2,1)} %get-tuple-element.93), channel_id=1, source_target_pairs={{0,3},{1,2},{2,1},{3,0},{4,5},{5,4},{6,7},{7,6},{8,11},{9,10},{10,... | collective-permute-start | bytes 7864328 | tf_op jit(solution)/shard_map/ppermute | solution.py:28
  153.5 14.5 %keep.1 = (bf16[512,2560]{1,0:T(8,128)(2,1)}, bf16[512,2560]{1,0:T(8,128)(2,1)}, bf16[512,2048]{1,0:T(8,128)(2,1)}) custom-call(bf16[4,4,4,16,512]{4,3,2,1,0:T(8,128)(2,1)} %get-tuple-element.89.refs_0_, bf16[4,4,4,16,512]{4,3,2,1,0:T(8,128)(2,1)} %get-tuple-element.90.refs_1_, bf16[512,7168]{1,0:T(8,128)(2,1)} %bitcast.20.refs_5_.refs_2_, ...), custom_call_target="tpu_custom_call" | custom-call | tf_op jit(solution)/shard_map/keep/pallas_call | solution.py:314
  168.0 1.4 slice_bitcast_fusion.1
  169.5 5.8 %collective-permute-done.25 = bf16[512,2048]{1,0:T(8,128)(2,1)} collective-permute-done((bf16[512,2048]{1,0:T(8,128)(2,1)}, bf16[512,2048]{1,0:T(8,128)(2,1)}, u32[]{:S(2)}, u32[]{:S(2)}) %collective-permute-start.25) | collective-permute-done | bytes 2097184 | tf_op jit(solution)/shard_map/ppermute | solution.py:28
  175.3 1.8 fusion.2
  177.2 1.3 slice_bitcast_fusion
  178.5 4.0 %collective-permute-done.22 = bf16[512,2560]{1,0:T(8,128)(2,1)S(1)} collective-permute-done((bf16[512,2560]{1,0:T(8,128)(2,1)}, bf16[512,2560]{1,0:T(8,128)(2,1)S(1)}, u32[]{:S(2)}, u32[]{:S(2)}) %collective-permute-start.22) | collective-permute-done | bytes 2621472 | tf_op jit(solution)/shard_map/ppermute | solution.py:28
  183.2 0.9 collective-permute-done.24
  184.6 1.8 fusion
  186.6 5.4 %collective-permute-done.28 = bf16[4,4,16,2048]{3,2,1,0:T(8,128)(2,1)S(1)} collective-permute-done((bf16[4,4,16,2048]{3,2,1,0:T(8,128)(2,1)S(1)}, bf16[4,4,16,2048]{3,2,1,0:T(8,128)(2,1)S(1)}, u32[]{:S(2)}, u32[]{:S(2)}) %collective-permute-start.28) | collective-permute-done | bytes 1048608 | tf_op jit(solution)/shard_map/ppermute | solution.py:28
  192.2 2.7 %collective-permute-start.31 = (bf16[4,2,16,2048]{3,2,1,0:T(8,128)(2,1)S(1)}, bf16[4,2,16,2048]{3,2,1,0:T(8,128)(2,1)S(1)}, u32[]{:S(2)}, u32[]{:S(2)}) collective-permute-start(bf16[4,2,16,2048]{3,2,1,0:T(8,128)(2,1)S(1)} %add_convert_fusion.4), channel_id=1, source_target_pairs={{0,3},{1,2},{2,1},{3,0},{4,5},{5,4},{6,7},{7,6},{8,11},{9,10},{10,... | collective-permute-start | bytes 1572872 | tf_op jit(solution)/shard_map/ppermute | solution.py:28
  194.9 5.7 %collective-permute-done.23 = bf16[4,4,16,2560]{3,2,1,0:T(8,128)(2,1)S(1)} collective-permute-done((bf16[4,4,16,2560]{3,2,1,0:T(8,128)(2,1)S(1)}, bf16[4,4,16,2560]{3,2,1,0:T(8,128)(2,1)S(1)}, u32[]{:S(2)}, u32[]{:S(2)}) %collective-permute-start.23) | collective-permute-done | bytes 1310752 | tf_op jit(solution)/shard_map/ppermute | solution.py:28
  200.7 3.0 %collective-permute-start.26 = (bf16[2,4,16,2560]{3,2,1,0:T(8,128)(2,1)S(1)}, bf16[2,4,16,2560]{3,2,1,0:T(8,128)(2,1)S(1)}, u32[]{:S(2)}, u32[]{:S(2)}) collective-permute-start(bf16[2,4,16,2560]{3,2,1,0:T(8,128)(2,1)S(1)} %add_convert_fusion.3), channel_id=1, source_target_pairs={{0,24},{8,16},{16,8},{24,0},{4,12},{12,4},{20,28},{28,20},{1,25},{... | collective-permute-start | bytes 1966088 | tf_op jit(solution)/shard_map/ppermute | solution.py:28
  203.7 5.6 %collective-permute-done.27 = bf16[4,4,16,2560]{3,2,1,0:T(8,128)(2,1)S(1)} collective-permute-done((bf16[4,4,16,2560]{3,2,1,0:T(8,128)(2,1)S(1)}, bf16[4,4,16,2560]{3,2,1,0:T(8,128)(2,1)S(1)}, u32[]{:S(2)}, u32[]{:S(2)}) %collective-permute-start.27) | collective-permute-done | bytes 1310752 | tf_op jit(solution)/shard_map/ppermute | solution.py:28
  209.3 1.4 fusion.1
  210.6 2.2 collective-permute-start.30
  213.8 12.2 %collective-permute-done.30 = bf16[2,4,16,2560]{3,2,1,0:T(8,128)(2,1)S(1)} collective-permute-done((bf16[2,4,16,2560]{3,2,1,0:T(8,128)(2,1)S(1)}, bf16[2,4,16,2560]{3,2,1,0:T(8,128)(2,1)S(1)}, u32[]{:S(2)}, u32[]{:S(2)}) %collective-permute-start.30) | collective-permute-done | bytes 655392 | tf_op jit(solution)/shard_map/ppermute | solution.py:28
  226.0 1.1 fusion.3
  227.4 2.2 collective-permute-start.37
  229.6 2.7 %collective-permute-start.32 = (bf16[2,16,2560]{2,1,0:T(8,128)(2,1)S(1)}, bf16[2,16,2560]{2,1,0:T(8,128)(2,1)S(1)}, u32[]{:S(2)}, u32[]{:S(2)}) collective-permute-start(bf16[2,16,2560]{2,1,0:T(8,128)(2,1)S(1)} %fusion.8), channel_id=1, source_target_pairs={{0,3},{1,2},{2,1},{3,0},{4,5},{5,4},{6,7},{7,6},{8,11},{9,10},{10,... | collective-permute-start | bytes 491528 | tf_op jit(solution)/shard_map/ppermute | solution.py:28
  232.3 2.0 collective-permute-done.33
  234.3 1.0 fusion.6
  235.3 2.7 %collective-permute-start.36 = (bf16[2,16,2560]{2,1,0:T(8,128)(2,1)S(1)}, bf16[2,16,2560]{2,1,0:T(8,128)(2,1)S(1)}, u32[]{:S(2)}, u32[]{:S(2)}) collective-permute-start(bf16[2,16,2560]{2,1,0:T(8,128)(2,1)S(1)} %fusion.6), channel_id=1, source_target_pairs={{0,24},{8,16},{16,8},{24,0},{4,12},{12,4},{20,28},{28,20},{1,25},{... | collective-permute-start | bytes 491528 | tf_op jit(solution)/shard_map/ppermute | solution.py:28
  238.5 0.7 collective-permute-start.35
  239.2 2.8 %collective-permute-done.36 = bf16[2,16,2560]{2,1,0:T(8,128)(2,1)S(1)} collective-permute-done((bf16[2,16,2560]{2,1,0:T(8,128)(2,1)S(1)}, bf16[2,16,2560]{2,1,0:T(8,128)(2,1)S(1)}, u32[]{:S(2)}, u32[]{:S(2)}) %collective-permute-start.36) | collective-permute-done | bytes 163872 | tf_op jit(solution)/shard_map/ppermute | solution.py:28
  242.0 1.0 fusion.13
  243.2 4.2 %collective-permute-done.38 = bf16[16,2560]{1,0:T(8,128)(2,1)S(1)} collective-permute-done((bf16[16,2560]{1,0:T(8,128)(2,1)S(1)}, bf16[16,2560]{1,0:T(8,128)(2,1)S(1)}, u32[]{:S(2)}, u32[]{:S(2)}) %collective-permute-start.38) | collective-permute-done | bytes 81952 | tf_op jit(solution)/shard_map/ppermute | solution.py:28
  247.4 1.0 fusion.12
  (85 shorter events, 12.1 us)
Async XLA Ops:
  3.0 1.3 collective-permute-start
  5.3 19.6 %collective-permute-start.7 = (bf16[7168,512]{1,0:T(8,128)(2,1)}, bf16[7168,512]{1,0:T(8,128)(2,1)}, u32[]{:S(2)}, u32[]{:S(2)}) collective-permute-start(bf16[7168,512]{1,0:T(8,128)(2,1)} %bitcast.157), channel_id=1, source_target_pairs={{0,4},{4,0},{1,5},{5,1},{2,6},{6,2},{3,7},{7,3},{8,12},{12,8},{9,1... | collective-permute-start | bytes 22020104 | tf_op jit(solution)/shard_map/ppermute | solution.py:32
  5.7 5.1 %collective-permute-start.3 = (bf16[16,2176]{1,0:T(8,128)(2,1)S(1)}, bf16[16,2176]{1,0:T(8,128)(2,1)S(1)}, u32[]{:S(2)}, u32[]{:S(2)}) collective-permute-start(bf16[16,2176]{1,0:T(8,128)(2,1)S(1)} %slice.524), channel_id=1, source_target_pairs={{0,32},{32,0},{64,96},{96,64},{4,100},{36,68},{68,36},{100,4},{1,3... | collective-permute-start | bytes 208904 | tf_op jit(solution)/shard_map/ppermute | solution.py:28
  7.7 4.4 %collective-permute-start.1 = (bf16[16,2560]{1,0:T(8,128)(2,1)S(1)}, bf16[16,2560]{1,0:T(8,128)(2,1)S(1)}, u32[]{:S(2)}, u32[]{:S(2)}) collective-permute-start(bf16[16,2560]{1,0:T(8,128)(2,1)S(1)} %get-tuple-element.59), channel_id=1, source_target_pairs={{0,1},{1,0},{2,3},{3,2},{4,7},{5,6},{6,5},{7,4},{8,9},{9,8},{10,11... | collective-permute-start | bytes 245768 | tf_op jit(solution)/shard_map/ppermute | solution.py:28
  9.2 4.4 %collective-permute-start.2 = (bf16[16,2560]{1,0:T(8,128)(2,1)S(1)}, bf16[16,2560]{1,0:T(8,128)(2,1)S(1)}, u32[]{:S(2)}, u32[]{:S(2)}) collective-permute-start(bf16[16,2560]{1,0:T(8,128)(2,1)S(1)} %get-tuple-element.60), channel_id=1, source_target_pairs={{0,8},{8,0},{16,24},{24,16},{4,28},{12,20},{20,12},{28,4},{1,9},{9... | collective-permute-start | bytes 245768 | tf_op jit(solution)/shard_map/ppermute | solution.py:28
  13.6 7.7 %collective-permute-start.6 = (bf16[2,16,2176]{2,1,0:T(8,128)(2,1)S(1)}, bf16[2,16,2176]{2,1,0:T(8,128)(2,1)S(1)}, u32[]{:S(2)}, u32[]{:S(2)}) collective-permute-start(bf16[2,16,2176]{2,1,0:T(8,128)(2,1)S(1)} %pad_maximum_fusion.15), channel_id=1, source_target_pairs={{0,96},{32,64},{64,32},{96,0},{4,36},{36,4},{68,100},{100,68},{1,9... | collective-permute-start | bytes 417800 | tf_op jit(solution)/shard_map/ppermute | solution.py:28
  16.2 6.5 %collective-permute-start.4 = (bf16[2,16,2560]{2,1,0:T(8,128)(2,1)S(1)}, bf16[2,16,2560]{2,1,0:T(8,128)(2,1)S(1)}, u32[]{:S(2)}, u32[]{:S(2)}) collective-permute-start(bf16[2,16,2560]{2,1,0:T(8,128)(2,1)S(1)} %pad_maximum_fusion.13), channel_id=1, source_target_pairs={{0,3},{1,2},{2,1},{3,0},{4,5},{5,4},{6,7},{7,6},{8,11},{9,10},{10,... | collective-permute-start | bytes 491528 | tf_op jit(solution)/shard_map/ppermute | solution.py:28
  18.3 6.5 %collective-permute-start.5 = (bf16[2,16,2560]{2,1,0:T(8,128)(2,1)S(1)}, bf16[2,16,2560]{2,1,0:T(8,128)(2,1)S(1)}, u32[]{:S(2)}, u32[]{:S(2)}) collective-permute-start(bf16[2,16,2560]{2,1,0:T(8,128)(2,1)S(1)} %pad_maximum_fusion.14), channel_id=1, source_target_pairs={{0,24},{8,16},{16,8},{24,0},{4,12},{12,4},{20,28},{28,20},{1,25},{... | collective-permute-start | bytes 491528 | tf_op jit(solution)/shard_map/ppermute | solution.py:28
  24.9 23.7 %collective-permute-start.14 = (bf16[7168,512]{1,0:T(8,128)(2,1)}, bf16[7168,512]{1,0:T(8,128)(2,1)}, u32[]{:S(2)}, u32[]{:S(2)}) collective-permute-start(bf16[7168,512]{1,0:T(8,128)(2,1)} %bitcast.160), channel_id=1, source_target_pairs={{0,4},{4,0},{1,5},{5,1},{2,6},{6,2},{3,7},{7,3},{8,12},{12,8},{9,1... | collective-permute-start | bytes 22020104 | tf_op jit(solution)/shard_map/ppermute | solution.py:32
  25.0 6.6 %collective-permute-start.10 = (bf16[4,16,2176]{2,1,0:T(8,128)(2,1)S(1)}, bf16[4,16,2176]{2,1,0:T(8,128)(2,1)S(1)}, u32[]{:S(2)}, u32[]{:S(2)}) collective-permute-start(bf16[4,16,2176]{2,1,0:T(8,128)(2,1)S(1)} %pad_maximum_fusion.11), channel_id=1, source_target_pairs={{0,1},{1,0},{2,3},{3,2},{4,7},{5,6},{6,5},{7,4},{8,9},{9,8},{10,11... | collective-permute-start | bytes 835592 | tf_op jit(solution)/shard_map/ppermute | solution.py:28
  25.7 7.1 %collective-permute-start.8 = (bf16[4,16,2560]{2,1,0:T(8,128)(2,1)S(1)}, bf16[4,16,2560]{2,1,0:T(8,128)(2,1)S(1)}, u32[]{:S(2)}, u32[]{:S(2)}) collective-permute-start(bf16[4,16,2560]{2,1,0:T(8,128)(2,1)S(1)} %pad_maximum_fusion.9), channel_id=1, source_target_pairs={{0,8},{8,0},{16,24},{24,16},{4,28},{12,20},{20,12},{28,4},{1,9},{9... | collective-permute-start | bytes 983048 | tf_op jit(solution)/shard_map/ppermute | solution.py:28
  26.0 7.1 %collective-permute-start.9 = (bf16[4,16,2560]{2,1,0:T(8,128)(2,1)S(1)}, bf16[4,16,2560]{2,1,0:T(8,128)(2,1)S(1)}, u32[]{:S(2)}, u32[]{:S(2)}) collective-permute-start(bf16[4,16,2560]{2,1,0:T(8,128)(2,1)S(1)} %pad_maximum_fusion.10), channel_id=1, source_target_pairs={{0,32},{32,0},{64,96},{96,64},{4,100},{36,68},{68,36},{100,4},{1,3... | collective-permute-start | bytes 983048 | tf_op jit(solution)/shard_map/ppermute | solution.py:28
  33.2 10.8 %collective-permute-start.13 = (bf16[2,4,16,2176]{3,2,1,0:T(8,128)(2,1)S(1)}, bf16[2,4,16,2176]{3,2,1,0:T(8,128)(2,1)S(1)}, u32[]{:S(2)}, u32[]{:S(2)}) collective-permute-start(bf16[2,4,16,2176]{3,2,1,0:T(8,128)(2,1)S(1)} %pad_maximum_fusion.8), channel_id=1, source_target_pairs={{0,3},{1,2},{2,1},{3,0},{4,5},{5,4},{6,7},{7,6},{8,11},{9,10},{10,... | collective-permute-start | bytes 1671176 | tf_op jit(solution)/shard_map/ppermute | solution.py:28
  34.0 11.8 %collective-permute-start.11 = (bf16[2,4,16,2560]{3,2,1,0:T(8,128)(2,1)S(1)}, bf16[2,4,16,2560]{3,2,1,0:T(8,128)(2,1)S(1)}, u32[]{:S(2)}, u32[]{:S(2)}) collective-permute-start(bf16[2,4,16,2560]{3,2,1,0:T(8,128)(2,1)S(1)} %pad_maximum_fusion.6), channel_id=1, source_target_pairs={{0,24},{8,16},{16,8},{24,0},{4,12},{12,4},{20,28},{28,20},{1,25},{... | collective-permute-start | bytes 1966088 | tf_op jit(solution)/shard_map/ppermute | solution.py:28
  36.7 11.8 %collective-permute-start.12 = (bf16[2,4,16,2560]{3,2,1,0:T(8,128)(2,1)S(1)}, bf16[2,4,16,2560]{3,2,1,0:T(8,128)(2,1)S(1)}, u32[]{:S(2)}, u32[]{:S(2)}) collective-permute-start(bf16[2,4,16,2560]{3,2,1,0:T(8,128)(2,1)S(1)} %pad_maximum_fusion.7), channel_id=1, source_target_pairs={{0,96},{32,64},{64,32},{96,0},{4,36},{36,4},{68,100},{100,68},{1,9... | collective-permute-start | bytes 1966088 | tf_op jit(solution)/shard_map/ppermute | solution.py:28
  48.6 77.6 %collective-permute-start.21 = (bf16[512,7168]{1,0:T(8,128)(2,1)}, bf16[512,7168]{1,0:T(8,128)(2,1)}, u32[]{:S(2)}, u32[]{:S(2)}) collective-permute-start(bf16[512,7168]{1,0:T(8,128)(2,1)} %bitcast.20.refs_5_.refs_2_), channel_id=1, source_target_pairs={{0,4},{4,0},{1,5},{5,1},{2,6},{6,2},{3,7},{7,3},{8,12},{12,8},{9,1... | collective-permute-start | bytes 22020104 | tf_op jit(solution)/shard_map/ppermute | solution.py:32
  48.7 15.6 %collective-permute-start.17 = (bf16[4,4,16,2176]{3,2,1,0:T(8,128)(2,1)S(1)}, bf16[4,4,16,2176]{3,2,1,0:T(8,128)(2,1)S(1)}, u32[]{:S(2)}, u32[]{:S(2)}) collective-permute-start(bf16[4,4,16,2176]{3,2,1,0:T(8,128)(2,1)S(1)} %pad_maximum_fusion.5), channel_id=1, source_target_pairs={{0,8},{8,0},{16,24},{24,16},{4,28},{12,20},{20,12},{28,4},{1,9},{9... | collective-permute-start | bytes 3342344 | tf_op jit(solution)/shard_map/ppermute | solution.py:28
  50.1 17.6 %collective-permute-start.15 = (bf16[4,4,16,2560]{3,2,1,0:T(8,128)(2,1)S(1)}, bf16[4,4,16,2560]{3,2,1,0:T(8,128)(2,1)S(1)}, u32[]{:S(2)}, u32[]{:S(2)}) collective-permute-start(bf16[4,4,16,2560]{3,2,1,0:T(8,128)(2,1)S(1)} %pad_maximum_fusion.3), channel_id=1, source_target_pairs={{0,32},{32,0},{64,96},{96,64},{4,100},{36,68},{68,36},{100,4},{1,3... | collective-permute-start | bytes 3932168 | tf_op jit(solution)/shard_map/ppermute | solution.py:28
  50.1 19.4 %collective-permute-start.16 = (bf16[4,4,16,2560]{3,2,1,0:T(8,128)(2,1)S(1)}, bf16[4,4,16,2560]{3,2,1,0:T(8,128)(2,1)S(1)}, u32[]{:S(2)}, u32[]{:S(2)}) collective-permute-start(bf16[4,4,16,2560]{3,2,1,0:T(8,128)(2,1)S(1)} %pad_maximum_fusion.4), channel_id=1, source_target_pairs={{0,1},{1,0},{2,3},{3,2},{4,7},{5,6},{6,5},{7,4},{8,9},{9,8},{10,11... | collective-permute-start | bytes 3932168 | tf_op jit(solution)/shard_map/ppermute | solution.py:28
  64.5 10.0 %copy-start = (bf16[2,4,4,16,2176]{4,3,2,1,0:T(8,128)(2,1)}, bf16[2,4,4,16,2176]{4,3,2,1,0:T(8,128)(2,1)S(1)}, u32[]{:S(2)}) copy-start(bf16[2,4,4,16,2176]{4,3,2,1,0:T(8,128)(2,1)S(1)} %pad_maximum_fusion.2.refs_2_) | copy-start | bytes 6684676
  71.2 33.2 %collective-permute-start.18 = (bf16[2,4,4,16,2560]{4,3,2,1,0:T(8,128)(2,1)}, bf16[2,4,4,16,2560]{4,3,2,1,0:T(8,128)(2,1)}, u32[]{:S(2)}, u32[]{:S(2)}) collective-permute-start(bf16[2,4,4,16,2560]{4,3,2,1,0:T(8,128)(2,1)} %pad_maximum_fusion.refs_0_), channel_id=1, source_target_pairs={{0,96},{32,64},{64,32},{96,0},{4,36},{36,4},{68,100},{100,68},{1,9... | collective-permute-start | bytes 7864328 | tf_op jit(solution)/shard_map/ppermute | solution.py:28
  71.9 33.2 %collective-permute-start.19 = (bf16[2,4,4,16,2560]{4,3,2,1,0:T(8,128)(2,1)}, bf16[2,4,4,16,2560]{4,3,2,1,0:T(8,128)(2,1)}, u32[]{:S(2)}, u32[]{:S(2)}) collective-permute-start(bf16[2,4,4,16,2560]{4,3,2,1,0:T(8,128)(2,1)} %pad_maximum_fusion.1.refs_1_), channel_id=1, source_target_pairs={{0,3},{1,2},{2,1},{3,0},{4,5},{5,4},{6,7},{7,6},{8,11},{9,10},{10,... | collective-permute-start | bytes 7864328 | tf_op jit(solution)/shard_map/ppermute | solution.py:28
  74.5 28.8 %collective-permute-start.20 = (bf16[2,4,4,16,2176]{4,3,2,1,0:T(8,128)(2,1)S(1)}, bf16[2,4,4,16,2176]{4,3,2,1,0:T(8,128)(2,1)}, u32[]{:S(2)}, u32[]{:S(2)}) collective-permute-start(bf16[2,4,4,16,2176]{4,3,2,1,0:T(8,128)(2,1)S(1)} %pad_maximum_fusion.2.refs_2_), channel_id=1, source_target_pairs={{0,24},{8,16},{16,8},{24,0},{4,12},{12,4},{20,28},{28,20},{1,25},{... | collective-permute-start | bytes 6684680 | tf_op jit(solution)/shard_map/ppermute | solution.py:28
  147.7 27.6 %collective-permute-start.25 = (bf16[512,2048]{1,0:T(8,128)(2,1)}, bf16[512,2048]{1,0:T(8,128)(2,1)}, u32[]{:S(2)}, u32[]{:S(2)}) collective-permute-start(bf16[512,2048]{1,0:T(8,128)(2,1)} %get-tuple-element.94), channel_id=1, source_target_pairs={{0,24},{8,16},{16,8},{24,0},{4,12},{12,4},{20,28},{28,20},{1,25},{... | collective-permute-start | bytes 6291464 | tf_op jit(solution)/shard_map/ppermute | solution.py:28
  148.4 34.1 %collective-permute-start.22 = (bf16[512,2560]{1,0:T(8,128)(2,1)}, bf16[512,2560]{1,0:T(8,128)(2,1)S(1)}, u32[]{:S(2)}, u32[]{:S(2)}) collective-permute-start(bf16[512,2560]{1,0:T(8,128)(2,1)} %get-tuple-element.92), channel_id=1, source_target_pairs={{0,96},{32,64},{64,32},{96,0},{4,36},{36,4},{68,100},{100,68},{1,9... | collective-permute-start | bytes 7864328 | tf_op jit(solution)/shard_map/ppermute | solution.py:28
  150.9 33.2 %collective-permute-start.24 = (bf16[512,2560]{1,0:T(8,128)(2,1)}, bf16[512,2560]{1,0:T(8,128)(2,1)}, u32[]{:S(2)}, u32[]{:S(2)}) collective-permute-start(bf16[512,2560]{1,0:T(8,128)(2,1)} %get-tuple-element.93), channel_id=1, source_target_pairs={{0,3},{1,2},{2,1},{3,0},{4,5},{5,4},{6,7},{7,6},{8,11},{9,10},{10,... | collective-permute-start | bytes 7864328 | tf_op jit(solution)/shard_map/ppermute | solution.py:28
  168.0 1.5 copy-start.4
  168.0 7.3 %copy-start.3 = (bf16[512,2048]{1,0:T(8,128)(2,1)S(1)}, bf16[512,2048]{1,0:T(8,128)(2,1)}, u32[]{:S(2)}) copy-start(bf16[512,2048]{1,0:T(8,128)(2,1)} %get-tuple-element.98) | copy-start | bytes 6291460
  175.3 7.2 %copy-start.1 = (bf16[512,2560]{1,0:T(8,128)(2,1)S(1)}, bf16[512,2560]{1,0:T(8,128)(2,1)}, u32[]{:S(2)}) copy-start(bf16[512,2560]{1,0:T(8,128)(2,1)} %get-tuple-element.91) | copy-start | bytes 7864324
  177.1 14.9 %collective-permute-start.28 = (bf16[4,4,16,2048]{3,2,1,0:T(8,128)(2,1)S(1)}, bf16[4,4,16,2048]{3,2,1,0:T(8,128)(2,1)S(1)}, u32[]{:S(2)}, u32[]{:S(2)}) collective-permute-start(bf16[4,4,16,2048]{3,2,1,0:T(8,128)(2,1)S(1)} %fusion.2), channel_id=1, source_target_pairs={{0,8},{8,0},{16,24},{24,16},{4,28},{12,20},{20,12},{28,4},{1,9},{9... | collective-permute-start | bytes 3145736 | tf_op jit(solution)/shard_map/ppermute | solution.py:28
  182.9 1.7 copy-start.2
  182.9 17.7 %collective-permute-start.23 = (bf16[4,4,16,2560]{3,2,1,0:T(8,128)(2,1)S(1)}, bf16[4,4,16,2560]{3,2,1,0:T(8,128)(2,1)S(1)}, u32[]{:S(2)}, u32[]{:S(2)}) collective-permute-start(bf16[4,4,16,2560]{3,2,1,0:T(8,128)(2,1)S(1)} %bitcast.181), channel_id=1, source_target_pairs={{0,32},{32,0},{64,96},{96,64},{4,100},{36,68},{68,36},{100,4},{1,3... | collective-permute-start | bytes 3932168 | tf_op jit(solution)/shard_map/ppermute | solution.py:28
  186.5 22.8 %collective-permute-start.27 = (bf16[4,4,16,2560]{3,2,1,0:T(8,128)(2,1)S(1)}, bf16[4,4,16,2560]{3,2,1,0:T(8,128)(2,1)S(1)}, u32[]{:S(2)}, u32[]{:S(2)}) collective-permute-start(bf16[4,4,16,2560]{3,2,1,0:T(8,128)(2,1)S(1)} %fusion), channel_id=1, source_target_pairs={{0,1},{1,0},{2,3},{3,2},{4,7},{5,6},{6,5},{7,4},{8,9},{9,8},{10,11... | collective-permute-start | bytes 3932168 | tf_op jit(solution)/shard_map/ppermute | solution.py:28
  192.2 20.6 %collective-permute-start.31 = (bf16[4,2,16,2048]{3,2,1,0:T(8,128)(2,1)S(1)}, bf16[4,2,16,2048]{3,2,1,0:T(8,128)(2,1)S(1)}, u32[]{:S(2)}, u32[]{:S(2)}) collective-permute-start(bf16[4,2,16,2048]{3,2,1,0:T(8,128)(2,1)S(1)} %add_convert_fusion.4), channel_id=1, source_target_pairs={{0,3},{1,2},{2,1},{3,0},{4,5},{5,4},{6,7},{7,6},{8,11},{9,10},{10,... | collective-permute-start | bytes 1572872 | tf_op jit(solution)/shard_map/ppermute | solution.py:28
  200.7 12.9 %collective-permute-start.26 = (bf16[2,4,16,2560]{3,2,1,0:T(8,128)(2,1)S(1)}, bf16[2,4,16,2560]{3,2,1,0:T(8,128)(2,1)S(1)}, u32[]{:S(2)}, u32[]{:S(2)}) collective-permute-start(bf16[2,4,16,2560]{3,2,1,0:T(8,128)(2,1)S(1)} %add_convert_fusion.3), channel_id=1, source_target_pairs={{0,24},{8,16},{16,8},{24,0},{4,12},{12,4},{20,28},{28,20},{1,25},{... | collective-permute-start | bytes 1966088 | tf_op jit(solution)/shard_map/ppermute | solution.py:28
  210.6 15.4 %collective-permute-start.30 = (bf16[2,4,16,2560]{3,2,1,0:T(8,128)(2,1)S(1)}, bf16[2,4,16,2560]{3,2,1,0:T(8,128)(2,1)S(1)}, u32[]{:S(2)}, u32[]{:S(2)}) collective-permute-start(bf16[2,4,16,2560]{3,2,1,0:T(8,128)(2,1)S(1)} %fusion.1), channel_id=1, source_target_pairs={{0,96},{32,64},{64,32},{96,0},{4,36},{36,4},{68,100},{100,68},{1,9... | collective-permute-start | bytes 1966088 | tf_op jit(solution)/shard_map/ppermute | solution.py:28
  213.0 14.3 %collective-permute-start.34 = (bf16[4,16,2048]{2,1,0:T(8,128)(2,1)S(1)}, bf16[4,16,2048]{2,1,0:T(8,128)(2,1)S(1)}, u32[]{:S(2)}, u32[]{:S(2)}) collective-permute-start(bf16[4,16,2048]{2,1,0:T(8,128)(2,1)S(1)} %fusion.9), channel_id=1, source_target_pairs={{0,1},{1,0},{2,3},{3,2},{4,7},{5,6},{6,5},{7,4},{8,9},{9,8},{10,11... | collective-permute-start | bytes 786440 | tf_op jit(solution)/shard_map/ppermute | solution.py:28
  213.7 15.8 %collective-permute-start.29 = (bf16[4,16,2560]{2,1,0:T(8,128)(2,1)S(1)}, bf16[4,16,2560]{2,1,0:T(8,128)(2,1)S(1)}, u32[]{:S(2)}, u32[]{:S(2)}) collective-permute-start(bf16[4,16,2560]{2,1,0:T(8,128)(2,1)S(1)} %fusion.4), channel_id=1, source_target_pairs={{0,8},{8,0},{16,24},{24,16},{4,28},{12,20},{20,12},{28,4},{1,9},{9... | collective-permute-start | bytes 983048 | tf_op jit(solution)/shard_map/ppermute | solution.py:28
  227.2 7.2 %collective-permute-start.33 = (bf16[4,16,2560]{2,1,0:T(8,128)(2,1)S(1)}, bf16[4,16,2560]{2,1,0:T(8,128)(2,1)S(1)}, u32[]{:S(2)}, u32[]{:S(2)}) collective-permute-start(bf16[4,16,2560]{2,1,0:T(8,128)(2,1)S(1)} %fusion.3), channel_id=1, source_target_pairs={{0,32},{32,0},{64,96},{96,64},{4,100},{36,68},{68,36},{100,4},{1,3... | collective-permute-start | bytes 983048 | tf_op jit(solution)/shard_map/ppermute | solution.py:28
  227.4 10.7 %collective-permute-start.37 = (bf16[2,16,2048]{2,1,0:T(8,128)(2,1)S(1)}, bf16[2,16,2048]{2,1,0:T(8,128)(2,1)S(1)}, u32[]{:S(2)}, u32[]{:S(2)}) collective-permute-start(bf16[2,16,2048]{2,1,0:T(8,128)(2,1)S(1)} %fusion.10), channel_id=1, source_target_pairs={{0,96},{32,64},{64,32},{96,0},{4,36},{36,4},{68,100},{100,68},{1,9... | collective-permute-start | bytes 393224 | tf_op jit(solution)/shard_map/ppermute | solution.py:28
  229.6 8.7 %collective-permute-start.32 = (bf16[2,16,2560]{2,1,0:T(8,128)(2,1)S(1)}, bf16[2,16,2560]{2,1,0:T(8,128)(2,1)S(1)}, u32[]{:S(2)}, u32[]{:S(2)}) collective-permute-start(bf16[2,16,2560]{2,1,0:T(8,128)(2,1)S(1)} %fusion.8), channel_id=1, source_target_pairs={{0,3},{1,2},{2,1},{3,0},{4,5},{5,4},{6,7},{7,6},{8,11},{9,10},{10,... | collective-permute-start | bytes 491528 | tf_op jit(solution)/shard_map/ppermute | solution.py:28
  235.3 6.6 %collective-permute-start.36 = (bf16[2,16,2560]{2,1,0:T(8,128)(2,1)S(1)}, bf16[2,16,2560]{2,1,0:T(8,128)(2,1)S(1)}, u32[]{:S(2)}, u32[]{:S(2)}) collective-permute-start(bf16[2,16,2560]{2,1,0:T(8,128)(2,1)S(1)} %fusion.6), channel_id=1, source_target_pairs={{0,24},{8,16},{16,8},{24,0},{4,12},{12,4},{20,28},{28,20},{1,25},{... | collective-permute-start | bytes 491528 | tf_op jit(solution)/shard_map/ppermute | solution.py:28
  238.1 4.9 %collective-permute-start.39 = (bf16[16,2048]{1,0:T(8,128)(2,1)S(1)}, bf16[16,2048]{1,0:T(8,128)(2,1)S(1)}, u32[]{:S(2)}, u32[]{:S(2)}) collective-permute-start(bf16[16,2048]{1,0:T(8,128)(2,1)S(1)} %fusion.19), channel_id=1, source_target_pairs={{0,32},{32,0},{64,96},{96,64},{4,100},{36,68},{68,36},{100,4},{1,3... | collective-permute-start | bytes 196616 | tf_op jit(solution)/shard_map/ppermute | solution.py:28
  238.5 4.6 %collective-permute-start.35 = (bf16[16,2560]{1,0:T(8,128)(2,1)S(1)}, bf16[16,2560]{1,0:T(8,128)(2,1)S(1)}, u32[]{:S(2)}, u32[]{:S(2)}) collective-permute-start(bf16[16,2560]{1,0:T(8,128)(2,1)S(1)} %fusion.14), channel_id=1, source_target_pairs={{0,1},{1,0},{2,3},{3,2},{4,7},{5,6},{6,5},{7,4},{8,9},{9,8},{10,11... | collective-permute-start | bytes 245768 | tf_op jit(solution)/shard_map/ppermute | solution.py:28
  242.9 4.5 %collective-permute-start.38 = (bf16[16,2560]{1,0:T(8,128)(2,1)S(1)}, bf16[16,2560]{1,0:T(8,128)(2,1)S(1)}, u32[]{:S(2)}, u32[]{:S(2)}) collective-permute-start(bf16[16,2560]{1,0:T(8,128)(2,1)S(1)} %fusion.13), channel_id=1, source_target_pairs={{0,8},{8,0},{16,24},{24,16},{4,28},{12,20},{20,12},{28,4},{1,9},{9... | collective-permute-start | bytes 245768 | tf_op jit(solution)/shard_map/ppermute | solution.py:28
